TPU v7x, 32 devices: a whole 2x2x4 slice. The times are simulated.
32 devices in a mesh: dp: 16 (over z, y, core), tensor: 2 (over x).
Axes of the slice: x: 2, y: 2, z: 4, core: 2. Of those that a mesh axis runs over, the one named last changes fastest.
Arguments:
- layer_input: bfloat16 [32768, 1024], P(('dp', 'tensor')), may hold values from -6 to 6
- target: bfloat16 [32768, 1024], P(('dp', 'tensor')), may hold values from -6 to 6
- segment: int32 [32768], P('dp'), may hold values from 0 to 2047, as said below
- pad_mask: int32 [32768], P(('dp', 'tensor')), may hold values from 0 to 1, as said below
- norm1_gain: float32 [1024], replicated, may hold values from 0.5 to 1.5
- w_query: bfloat16 [1024, 1024], P('dp', 'tensor'), may hold values from -0.1875 to 0.1875
- w_key: bfloat16 [1024, 1024], P('dp', 'tensor'), may hold values from -0.1875 to 0.1875
- w_value: bfloat16 [1024, 2048], P('dp', 'tensor'), may hold values from -0.1875 to 0.1875
- w_gate_out: bfloat16 [1024, 2048], P('dp', 'tensor'), may hold values from -0.1875 to 0.1875
- w_decay: bfloat16 [1024, 8], P('dp', 'tensor'), may hold values from -0.1875 to 0.1875
- w_beta: bfloat16 [1024, 8], P('dp', 'tensor'), may hold values from -0.1875 to 0.1875
- conv_query: float32 [4, 1024], replicated, may hold values from -3 to 3
- conv_key: float32 [4, 1024], replicated, may hold values from -3 to 3
- conv_value: float32 [4, 2048], replicated, may hold values from -3 to 3
- decay_scale: float32 [8], replicated, may hold values from 0.3 to 8
- decay_bias: float32 [8], replicated, may hold values from -5 to -2
- out_norm_gain: float32 [256], replicated, may hold values from 0.5 to 1.5
- w_out: bfloat16 [1024, 2048], P('dp', 'tensor'), may hold values from -0.25 to 0.25
- norm2_gain: float32 [1024], replicated, may hold values from 0.5 to 1.5
- w_ffn_gate: bfloat16 [1024, 2816], P('dp', 'tensor'), may hold values from -0.1875 to 0.1875
- w_ffn_up: bfloat16 [1024, 2816], P('dp', 'tensor'), may hold values from -0.1875 to 0.1875
- w_ffn_down: bfloat16 [1024, 2816], P('dp', 'tensor'), may hold values from -0.109375 to 0.109375
Outputs:
- output: float32 [32768, 1024], P(('dp', 'tensor'))
- loss: float32 [], replicated
- grad_input: float32 [32768, 1024], P(('dp', 'tensor'))
- grad_norm1_gain: float32 [1024], replicated
- grad_w_query: float32 [1024, 1024], P('dp', 'tensor')
- grad_w_key: float32 [1024, 1024], P('dp', 'tensor')
- grad_w_value: float32 [1024, 2048], P('dp', 'tensor')
- grad_w_gate_out: float32 [1024, 2048], P('dp', 'tensor')
- grad_w_decay: float32 [1024, 8], P('dp', 'tensor')
- grad_w_beta: float32 [1024, 8], P('dp', 'tensor')
- grad_conv_query: float32 [4, 1024], replicated
- grad_conv_key: float32 [4, 1024], replicated
- grad_conv_value: float32 [4, 2048], replicated
- grad_decay_scale: float32 [8], replicated
- grad_decay_bias: float32 [8], replicated
- grad_out_norm_gain: float32 [256], replicated
- grad_w_out: float32 [1024, 2048], P('dp', 'tensor')
- grad_norm2_gain: float32 [1024], replicated
- grad_w_ffn_gate: float32 [1024, 2816], P('dp', 'tensor')
- grad_w_ffn_up: float32 [1024, 2816], P('dp', 'tensor')
- grad_w_ffn_down: float32 [1024, 2816], P('dp', 'tensor')
Inputs may be any that keep to these rules, and one draw needn't show every extreme that they name: `segment`: ids never decrease within a sequence of 1024 tokens; each document's tokens share one id, the padding at a sequence's end has an id of its own, and different sequences share no id. Documents have 1 to 800 tokens, the last of a sequence cut to fit. `pad_mask`: each sequence of 1024 tokens ends with 1 to max(64, 2) padding tokens, marked 0; all other tokens are 1.
All inputs are finite; a program needn't handle non-finite values.
Results may differ from a plain program's by a relative error of at most 0.015.
Values may be sent and summed in bfloat16 or wider, within the bound.
No kernel may reach another device: no remote copies, remote signals or barrier semaphores. Data moves between devices by JAX's collectives and lax.ppermute only.
A program may use at most 384 MiB of HBM per device.

v0:
```python
import jax
import jax.numpy as jnp
from jax import lax
from jax.sharding import PartitionSpec as P

CH = 64
LENGTH = 1024


exact_precision = lax.Precision.HIGHEST


def rms_scale(values, gain):
    return values * lax.rsqrt(jnp.mean(values * values, axis=-1, keepdims=True) + 1e-06) * gain


def shift_masks(segment_ids, taps):
    masks = [jnp.ones(segment_ids.shape, jnp.float32)]
    for offset in range(1, taps):
        earlier = jnp.concatenate([jnp.full((offset,), -1, jnp.int32), segment_ids[:-offset]])
        masks.append((segment_ids == earlier).astype(jnp.float32))
    return masks


def short_conv(values, kernel, masks):
    result = values * kernel[0]
    for offset in range(1, len(masks)):
        shifted = jnp.concatenate(
            [jnp.zeros((offset, values.shape[1]), jnp.float32), values[:-offset]]
        )
        result = result + shifted * masks[offset][:, None] * kernel[offset]
    return result


def unit_rows(values):
    return values * lax.rsqrt(jnp.sum(values * values, axis=-1, keepdims=True) + 1e-06)


def lower_inverse(lower_part, length):
    negative = -lower_part
    inverse = jnp.eye(length, dtype=jnp.float32) + negative
    power = negative
    covered = 2
    while covered < length:
        power = jnp.einsum("hij,hjk->hik", power, power, precision=exact_precision)
        inverse = inverse + jnp.einsum("hij,hjk->hik", inverse, power, precision=exact_precision)
        covered = covered * 2
    return inverse


def block_update(state, inputs):
    queries, keys, values, betas, log_decay, seg_block, previous = inputs
    length = queries.shape[0]
    cumulative = jnp.cumsum(log_decay, axis=0)
    order = jnp.arange(length)
    causal = order[:, None] >= order[None, :]
    strict = order[:, None] > order[None, :]
    same_doc = seg_block[:, None] == seg_block[None, :]
    visible = (same_doc & causal)[:, :, None]
    spread = cumulative[:, None, :] - cumulative[None, :, :]
    weights = jnp.where(visible, jnp.exp(jnp.where(visible, spread, 0.0)), 0.0)
    carried = (seg_block == previous).astype(jnp.float32)
    carry_decay = jnp.exp(cumulative) * carried[:, None]
    key_gram = jnp.einsum("ihd,jhd->ijh", keys, keys, precision=exact_precision)
    lower_part = jnp.where(strict[:, :, None], betas[:, None, :] * weights * key_gram, 0.0)
    inverse = lower_inverse(jnp.transpose(lower_part, (2, 0, 1)), length)
    key_state = jnp.einsum("ihd,hde->ihe", keys, state, precision=exact_precision)
    target_rows = betas[:, :, None] * (values - carry_decay[:, :, None] * key_state)
    pseudo = jnp.einsum("hij,jhe->hie", inverse, target_rows, precision=exact_precision)
    scores = jnp.einsum("ihd,jhd->hij", queries, keys, precision=exact_precision) * jnp.transpose(
        weights, (2, 0, 1)
    )
    query_state = jnp.einsum("ihd,hde->ihe", queries, state, precision=exact_precision)
    outputs = carry_decay[:, :, None] * query_state + jnp.einsum(
        "hij,hje->ihe", scores, pseudo, precision=exact_precision
    )
    last_weights = weights[-1]
    new_state = (carried[-1] * jnp.exp(cumulative[-1]))[:, None, None] * state + jnp.einsum(
        "jh,jhd,hje->hde", last_weights, keys, pseudo, precision=exact_precision
    )
    return (new_state, outputs)


def mixer_sequence(
    q_pre,
    k_pre,
    v_pre,
    g_pre,
    a_pre,
    b_pre,
    segment_ids,
    conv_q,
    conv_k,
    conv_v,
    scale_rate,
    bias_rate,
    out_gain,
):
    length = q_pre.shape[0]
    heads = a_pre.shape[1]
    key_size = q_pre.shape[1] // heads
    value_size = v_pre.shape[1] // heads
    masks = shift_masks(segment_ids, conv_q.shape[0])
    queries = unit_rows(
        jax.nn.silu(short_conv(q_pre, conv_q, masks)).reshape(length, heads, key_size)
    ) * key_size ** (-0.5)
    keys = unit_rows(jax.nn.silu(short_conv(k_pre, conv_k, masks)).reshape(length, heads, key_size))
    values = jax.nn.silu(short_conv(v_pre, conv_v, masks)).reshape(length, heads, value_size)
    betas = jax.nn.sigmoid(b_pre)
    log_decay = -scale_rate * jax.nn.softplus(a_pre + bias_rate)
    blocks = length // CH
    seg_blocks = segment_ids.reshape(blocks, CH)
    previous = jnp.concatenate([jnp.full((1,), -1, jnp.int32), seg_blocks[:-1, -1]])
    state = jnp.zeros((heads, key_size, value_size), jnp.float32)
    carried_in = (
        queries.reshape(blocks, CH, heads, key_size),
        keys.reshape(blocks, CH, heads, key_size),
        values.reshape(blocks, CH, heads, value_size),
        betas.reshape(blocks, CH, heads),
        log_decay.reshape(blocks, CH, heads),
        seg_blocks,
        previous,
    )
    final_state, outputs = lax.scan(jax.checkpoint(block_update), state, carried_in)
    outputs = outputs.reshape(length, heads, value_size)
    gated = rms_scale(outputs, out_gain) * jax.nn.silu(g_pre.reshape(length, heads, value_size))
    return gated.reshape(length, heads * value_size)


def contract_rows(left, right):
    return lax.dot_general(
        left, right, (((0,), (0,)), ((), ())), preferred_element_type=jnp.float32
    )


def contract_cols(left, right):
    return lax.dot_general(
        left, right, (((1,), (1,)), ((), ())), preferred_element_type=jnp.float32
    )


def feed_inputs(normed_rows, gate_weight, up_weight):
    gate_pre = jnp.dot(normed_rows, gate_weight, preferred_element_type=jnp.float32)
    up_pre = jnp.dot(normed_rows, up_weight, preferred_element_type=jnp.float32)
    return (gate_pre, up_pre)


def on_device(
    layer_input,
    target,
    segment,
    pad_mask,
    norm1_gain,
    w_query,
    w_key,
    w_value,
    w_gate_out,
    w_decay,
    w_beta,
    conv_query,
    conv_key,
    conv_value,
    decay_scale,
    decay_bias,
    out_norm_gain,
    w_out,
    norm2_gain,
    w_ffn_gate,
    w_ffn_up,
    w_ffn_down,
):
    own_rows, width = layer_input.shape
    group_rows = segment.shape[0]
    sequences = group_rows // LENGTH
    tensor_index = lax.axis_index("tensor")
    heads_local = w_decay.shape[1]
    query_cols = w_query.shape[1]
    value_cols = w_value.shape[1]
    input_float = layer_input.astype(jnp.float32)
    normed_own, norm1_pull = jax.vjp(rms_scale, input_float, norm1_gain)
    normed = lax.all_gather(normed_own.astype(jnp.bfloat16), "tensor", axis=0, tiled=True)
    full_query, full_key, full_value, full_gate, full_decay, full_beta, full_out = (
        lax.all_gather(w_query, "dp", axis=0, tiled=True),
        lax.all_gather(w_key, "dp", axis=0, tiled=True),
        lax.all_gather(w_value, "dp", axis=0, tiled=True),
        lax.all_gather(w_gate_out, "dp", axis=0, tiled=True),
        lax.all_gather(w_decay, "dp", axis=0, tiled=True),
        lax.all_gather(w_beta, "dp", axis=0, tiled=True),
        lax.all_gather(w_out, "dp", axis=0, tiled=True),
    )
    proj_weights = (full_query, full_key, full_value, full_gate, full_decay, full_beta)
    projected = [
        jnp.dot(normed, weight, preferred_element_type=jnp.float32) for weight in proj_weights
    ]
    conv_q_local = lax.dynamic_slice_in_dim(conv_query, tensor_index * query_cols, query_cols, 1)
    conv_k_local = lax.dynamic_slice_in_dim(conv_key, tensor_index * query_cols, query_cols, 1)
    conv_v_local = lax.dynamic_slice_in_dim(conv_value, tensor_index * value_cols, value_cols, 1)
    scale_local = lax.dynamic_slice_in_dim(decay_scale, tensor_index * heads_local, heads_local, 0)
    bias_local = lax.dynamic_slice_in_dim(decay_bias, tensor_index * heads_local, heads_local, 0)
    seg_rows = segment.reshape(sequences, LENGTH)

    def mixer_local(
        q_pre,
        k_pre,
        v_pre,
        g_pre,
        a_pre,
        b_pre,
        conv_q,
        conv_k,
        conv_v,
        scale_rate,
        bias_rate,
        out_gain,
    ):
        shaped = [
            item.reshape(sequences, LENGTH, item.shape[1])
            for item in (q_pre, k_pre, v_pre, g_pre, a_pre, b_pre)
        ]
        mixed_rows = jax.vmap(
            mixer_sequence, in_axes=(0, 0, 0, 0, 0, 0, 0, None, None, None, None, None, None)
        )(*shaped, seg_rows, conv_q, conv_k, conv_v, scale_rate, bias_rate, out_gain)
        return mixed_rows.reshape(group_rows, mixed_rows.shape[2])

    mixed, mixer_pull = jax.vjp(
        mixer_local,
        *projected,
        conv_q_local,
        conv_k_local,
        conv_v_local,
        scale_local,
        bias_local,
        out_norm_gain
    )
    mixed_low = mixed.astype(jnp.bfloat16)
    attention = lax.psum_scatter(
        contract_cols(mixed_low, full_out), "tensor", scatter_dimension=0, tiled=True
    )
    residual = input_float + attention
    normed2_own, norm2_pull = jax.vjp(rms_scale, residual, norm2_gain)
    normed2 = lax.all_gather(normed2_own.astype(jnp.bfloat16), "tensor", axis=0, tiled=True)
    ffn_gate_w, ffn_up_w, ffn_down_w = (
        lax.all_gather(w_ffn_gate, "dp", axis=0, tiled=True),
        lax.all_gather(w_ffn_up, "dp", axis=0, tiled=True),
        lax.all_gather(w_ffn_down, "dp", axis=0, tiled=True),
    )
    gate_pre, up_pre = feed_inputs(normed2, ffn_gate_w, ffn_up_w)
    hidden = (jax.nn.silu(gate_pre) * up_pre).astype(jnp.bfloat16)
    ffn_out = lax.psum_scatter(
        contract_cols(hidden, ffn_down_w).astype(jnp.bfloat16),
        "tensor",
        scatter_dimension=0,
        tiled=True,
    ).astype(jnp.float32)
    output = residual + ffn_out
    live = pad_mask.astype(jnp.float32)
    error = output - target.astype(jnp.float32)
    loss_sum, count = lax.psum(
        (jnp.sum(live[:, None] * error * error), jnp.sum(live)), ("dp", "tensor")
    )
    loss = loss_sum / (count * width)
    all_tokens = own_rows * lax.axis_size("dp") * lax.axis_size("tensor")
    grad_output = error * live[:, None] * (all_tokens / count)
    grad_ffn = lax.all_gather(grad_output.astype(jnp.bfloat16), "tensor", axis=0, tiled=True)
    grad_hidden = jnp.dot(grad_ffn, ffn_down_w, preferred_element_type=jnp.float32)
    sigmoid_gate = jax.nn.sigmoid(gate_pre)
    grad_gate = (
        grad_hidden * up_pre * sigmoid_gate * (1.0 + gate_pre * (1.0 - sigmoid_gate))
    ).astype(jnp.bfloat16)
    grad_up = (grad_hidden * gate_pre * sigmoid_gate).astype(jnp.bfloat16)
    grad_down_local = contract_rows(grad_ffn, hidden)
    grad_gate_local = contract_rows(normed2, grad_gate)
    grad_up_local = contract_rows(normed2, grad_up)
    normed2_part = contract_cols(grad_gate, ffn_gate_w) + contract_cols(grad_up, ffn_up_w)
    grad_normed2 = lax.psum_scatter(
        normed2_part.astype(jnp.bfloat16), "tensor", scatter_dimension=0, tiled=True
    ).astype(jnp.float32)
    grad_residual_norm, grad_gain_two = norm2_pull(grad_normed2)
    grad_residual = grad_output + grad_residual_norm
    grad_attention = lax.all_gather(
        grad_residual.astype(jnp.bfloat16), "tensor", axis=0, tiled=True
    )
    grad_mixed = jnp.dot(grad_attention, full_out, preferred_element_type=jnp.float32)
    grad_out_local = contract_rows(grad_attention, mixed_low)
    mixer_grads = mixer_pull(grad_mixed)
    pre_grads = [item.astype(jnp.bfloat16) for item in mixer_grads[:6]]
    normed_part = contract_cols(pre_grads[0], full_query)
    for grad_item, weight in zip(pre_grads[1:], proj_weights[1:]):
        normed_part = normed_part + contract_cols(grad_item, weight)
    weight_locals = [contract_rows(normed, grad_item) for grad_item in pre_grads]
    grad_normed = lax.psum_scatter(
        normed_part.astype(jnp.bfloat16), "tensor", scatter_dimension=0, tiled=True
    ).astype(jnp.float32)
    grad_input_norm, grad_gain_one = norm1_pull(grad_normed)
    grad_input = grad_residual + grad_input_norm
    owned = (
        lax.psum_scatter(
            grad_gate_local.astype(jnp.bfloat16), "dp", scatter_dimension=0, tiled=True
        ).astype(jnp.float32),
        lax.psum_scatter(
            grad_up_local.astype(jnp.bfloat16), "dp", scatter_dimension=0, tiled=True
        ).astype(jnp.float32),
        lax.psum_scatter(
            grad_down_local.astype(jnp.bfloat16), "dp", scatter_dimension=0, tiled=True
        ).astype(jnp.float32),
        lax.psum_scatter(
            weight_locals[0].astype(jnp.bfloat16), "dp", scatter_dimension=0, tiled=True
        ).astype(jnp.float32),
        lax.psum_scatter(
            weight_locals[1].astype(jnp.bfloat16), "dp", scatter_dimension=0, tiled=True
        ).astype(jnp.float32),
        lax.psum_scatter(
            weight_locals[2].astype(jnp.bfloat16), "dp", scatter_dimension=0, tiled=True
        ).astype(jnp.float32),
        lax.psum_scatter(
            weight_locals[3].astype(jnp.bfloat16), "dp", scatter_dimension=0, tiled=True
        ).astype(jnp.float32),
        lax.psum_scatter(
            weight_locals[4].astype(jnp.bfloat16), "dp", scatter_dimension=0, tiled=True
        ).astype(jnp.float32),
        lax.psum_scatter(
            weight_locals[5].astype(jnp.bfloat16), "dp", scatter_dimension=0, tiled=True
        ).astype(jnp.float32),
        lax.psum_scatter(
            grad_out_local.astype(jnp.bfloat16), "dp", scatter_dimension=0, tiled=True
        ).astype(jnp.float32),
    )
    conv_q_full = lax.dynamic_update_slice_in_dim(
        jnp.zeros_like(conv_query), mixer_grads[6], tensor_index * query_cols, 1
    )
    conv_k_full = lax.dynamic_update_slice_in_dim(
        jnp.zeros_like(conv_key), mixer_grads[7], tensor_index * query_cols, 1
    )
    conv_v_full = lax.dynamic_update_slice_in_dim(
        jnp.zeros_like(conv_value), mixer_grads[8], tensor_index * value_cols, 1
    )
    scale_full = lax.dynamic_update_slice_in_dim(
        jnp.zeros_like(decay_scale), mixer_grads[9], tensor_index * heads_local, 0
    )
    bias_full = lax.dynamic_update_slice_in_dim(
        jnp.zeros_like(decay_bias), mixer_grads[10], tensor_index * heads_local, 0
    )
    summed = lax.psum(
        (
            grad_gain_one,
            grad_gain_two,
            conv_q_full,
            conv_k_full,
            conv_v_full,
            scale_full,
            bias_full,
            mixer_grads[11],
        ),
        ("dp", "tensor"),
    )
    return (
        output,
        loss,
        grad_input,
        summed[0],
        owned[3],
        owned[4],
        owned[5],
        owned[6],
        owned[7],
        owned[8],
        summed[2],
        summed[3],
        summed[4],
        summed[5],
        summed[6],
        summed[7],
        owned[9],
        summed[1],
        owned[0],
        owned[1],
        owned[2],
    )


def solution(mesh):
    return jax.shard_map(
        on_device,
        mesh=mesh,
        in_specs=(
            P(("dp", "tensor"), None),
            P(("dp", "tensor"), None),
            P("dp"),
            P(("dp", "tensor")),
            P(),
            P("dp", "tensor"),
            P("dp", "tensor"),
            P("dp", "tensor"),
            P("dp", "tensor"),
            P("dp", "tensor"),
            P("dp", "tensor"),
            P(),
            P(),
            P(),
            P(),
            P(),
            P(),
            P("dp", "tensor"),
            P(),
            P("dp", "tensor"),
            P("dp", "tensor"),
            P("dp", "tensor"),
        ),
        out_specs=(
            P(("dp", "tensor"), None),
            P(),
            P(("dp", "tensor"), None),
            P(),
            P("dp", "tensor"),
            P("dp", "tensor"),
            P("dp", "tensor"),
            P("dp", "tensor"),
            P("dp", "tensor"),
            P("dp", "tensor"),
            P(),
            P(),
            P(),
            P(),
            P(),
            P(),
            P("dp", "tensor"),
            P(),
            P("dp", "tensor"),
            P("dp", "tensor"),
            P("dp", "tensor"),
        ),
        check_vma=False,
    )
```

profile of v0, /device:TPU:8, one launch (start us, length us, event | category | flops | bytes accessed | tf_op | source)
XLA Modules:
  0.0 3116.8 jit_solution(9823898228020338124)
XLA Ops:
  17.5 18.9 all-gather
  36.6 17.4 all-gather.1
  56.2 51.0 %all-gather.15.cloned.1.call-done = bf16[2048,1024]{1,0:T(8,128)(2,1)} async-done(((bf16[1024,1024]{1,0:T(8,128)(2,1)}), bf16[2048,1024]{1,0:T(8,128)(2,1)}) %all-gather.15.cloned.1.call-update) | async-done | bytes 4194320 | tf_op jit(solution)/shard_map/all_gather | solution.py:181
  114.1 32.3 %all-gather.17.cloned.1.call-done = bf16[1024,512]{1,0:T(8,128)(2,1)} async-done(((bf16[64,512]{1,0:T(8,128)(2,1)}), bf16[1024,512]{1,0:T(8,128)(2,1)}) %all-gather.17.cloned.1.call-update) | async-done | bytes 1048592 | tf_op jit(solution)/shard_map/all_gather | solution.py:184
  265.0 323.5 %while.42 = (s32[]{:T(128)}, f32[2,4,128,256]{3,2,1,0:T(8,128)S(1)}, f32[16,2,64,4,256]{4,2,3,1,0:T(8,128)}, f32[16,2,4,128,256]{4,3,2,1,0:T(8,128)}, s32[16,2,6...) while((s32[]{:T(128)}, ...), condition=%wide.region_5.6_spmd.clone, body=%wide.region_3.5_spmd.clone.sunk | while | flops 1160541952 | bytes 16545918 | solution.py:124
  602.1 13.8 copy.459
  624.7 18.5 multiply_convert_fusion.3
  654.7 98.6 %reduce-scatter.19.cloned.1.call-done = f32[1024,1024]{1,0:T(8,128)} async-done(((f32[2048,1024]{1,0:T(8,128)}), f32[1024,1024]{1,0:T(8,128)}) %reduce-scatter.19.cloned.1.call-update) | async-done | bytes 4194320 | tf_op jit(solution)/shard_map/reduce_scatter | solution.py:236
  761.4 38.9 %all-gather.29.cloned.1.call-done = bf16[1024,1408]{1,0:T(8,128)(2,1)} async-done(((bf16[64,1408]{1,0:T(8,128)(2,1)}), bf16[1024,1408]{1,0:T(8,128)(2,1)}) %all-gather.29.cloned.1.call-update) | async-done | bytes 2883600 | tf_op jit(solution)/shard_map/all_gather | solution.py:243
  800.3 57.3 %all-gather.27.cloned.1.call-done = bf16[2048,1024]{1,0:T(8,128)(2,1)} async-done(((bf16[1024,1024]{1,0:T(8,128)(2,1)}), bf16[2048,1024]{1,0:T(8,128)(2,1)}) %all-gather.27.cloned.1.call-update) | async-done | bytes 4194320 | tf_op jit(solution)/shard_map/all_gather | solution.py:241
  869.6 34.8 %all-gather.31.cloned.1.call-done = bf16[1024,1408]{1,0:T(8,128)(2,1)} async-done(((bf16[64,1408]{1,0:T(8,128)(2,1)}), bf16[1024,1408]{1,0:T(8,128)(2,1)}) %all-gather.31.cloned.1.call-update) | async-done | bytes 2883600 | tf_op jit(solution)/shard_map/all_gather | solution.py:244
  904.4 14.8 multiply_convert_fusion.2
  919.2 30.5 all-gather.33.cloned.1.call-done
  962.3 38.9 %psum.71 = f32[]{:T(128)} all-reduce(f32[]{:T(128)} %convert_reduce_fusion), channel_id=1, replica_groups=mesh['dp'=16,'tensor'=2] {'dp','tensor'}, use_global_device_ids=true, to_apply=%region_13.14 | all-reduce | flops 1 | bytes 8 | tf_op jit(solution)/shard_map/psum | solution.py:258
  1001.9 13.3 reduce-scatter.21.cloned.1.call-done
  1021.7 56.8 %all-gather.35.cloned.1.call-done = bf16[2048,1024]{1,0:T(8,128)(2,1)} async-done(((bf16[1024,1024]{1,0:T(8,128)(2,1)}), bf16[2048,1024]{1,0:T(8,128)(2,1)}) %all-gather.35.cloned.1.call-update) | async-done | bytes 4194320 | tf_op jit(solution)/shard_map/all_gather | solution.py:264
  1078.5 19.6 multiply_convert_fusion
  1115.5 54.4 %reduce-scatter.23.cloned.1.call-done = bf16[1024,1024]{1,0:T(8,128)(2,1)} async-done(((bf16[2048,1024]{1,0:T(8,128)(2,1)}), bf16[1024,1024]{1,0:T(8,128)(2,1)}) %reduce-scatter.23.cloned.1.call-update) | async-done | bytes 2097168 | tf_op jit(solution)/shard_map/reduce_scatter | solution.py:275
  1239.5 18.8 fusion.145
  1268.9 12.6 multiply_reduce_fusion.4
  1300.7 1161.9 %while.43 = (s32[]{:T(128)}, f32[2,4,128,256]{3,2,1,0:T(8,128)}, f32[16,2,64,4,128]{4,2,3,1,0:T(8,128)}, f32[16,2,64,4,128]{4,2,3,1,0:T(8,128)}, f32[16,2,64,4,2...) while((s32[]{:T(128)}, f32[2,4,128,256]{3,2,1,0:T(8,128)}, ...), condition=%wide.region_27.28_spmd.clone, body=%wide.region_17.27_spmd.clone.sunk | while | flops 3179373312 | bytes 74722920 | solution.py:124
  2533.4 28.9 multiply_reduce_fusion.18
  2592.1 13.9 copy.482
  2629.8 25.2 multiply_reduce_fusion.8
  2678.6 12.8 add_convert_fusion.1
  2737.7 16.4 add_convert_fusion
  2767.4 41.9 %reduce-scatter.27.cloned.1.call-done = bf16[64,512]{1,0:T(8,128)(2,1)} async-done(((bf16[1024,512]{1,0:T(8,128)(2,1)}), bf16[64,512]{1,0:T(8,128)(2,1)}) %reduce-scatter.27.cloned.1.call-update) | async-done | bytes 65552 | tf_op jit(solution)/shard_map/reduce_scatter | solution.py:306
  2810.8 62.9 %reduce-scatter.35.cloned.1.call-done = bf16[64,1024]{1,0:T(8,128)(2,1)} async-done(((bf16[1024,1024]{1,0:T(8,128)(2,1)}), bf16[64,1024]{1,0:T(8,128)(2,1)}) %reduce-scatter.35.cloned.1.call-update) | async-done | bytes 131088 | tf_op jit(solution)/shard_map/reduce_scatter | solution.py:324
  2875.3 63.0 %reduce-scatter.31.cloned.1.call-done = bf16[64,1024]{1,0:T(8,128)(2,1)} async-done(((bf16[1024,1024]{1,0:T(8,128)(2,1)}), bf16[64,1024]{1,0:T(8,128)(2,1)}) %reduce-scatter.31.cloned.1.call-update) | async-done | bytes 131088 | tf_op jit(solution)/shard_map/reduce_scatter | solution.py:312
  2940.0 62.7 %reduce-scatter.33.cloned.1.call-done = bf16[64,1024]{1,0:T(8,128)(2,1)} async-done(((bf16[1024,1024]{1,0:T(8,128)(2,1)}), bf16[64,1024]{1,0:T(8,128)(2,1)}) %reduce-scatter.33.cloned.1.call-update) | async-done | bytes 131088 | tf_op jit(solution)/shard_map/reduce_scatter | solution.py:315
  3004.3 54.7 %reduce-scatter.25.cloned.1.call-done = bf16[1024,1024]{1,0:T(8,128)(2,1)} async-done(((bf16[2048,1024]{1,0:T(8,128)(2,1)}), bf16[1024,1024]{1,0:T(8,128)(2,1)}) %reduce-scatter.25.cloned.1.call-update) | async-done | bytes 2097168 | tf_op jit(solution)/shard_map/reduce_scatter | solution.py:291
  3062.3 41.0 %all-reduce.38 = (f32[]{:T(128)}, f32[1024]{0:T(1024)}, f32[4,1024]{1,0:T(4,128)}, f32[4,1024]{1,0:T(4,128)}, f32[4,2048]{1,0:T(4,128)}, /*index=5*/f32[8]{0:T(128)}, f32[8]{0:T(128)}, f32[256]{0:T(256)}, f32[1024]{0:T(1024)}) all-reduce(f32[]{:T(128)} %get-tuple-element.925, ...), channel_id=1, replica_groups=mesh['dp'=16,'tensor'=2] {'dp','tensor'}, use_global_device_ids=true, to_apply=%region_11.12 | all-reduce | flops 18705 | bytes 149640 | tf_op jit(solution)/shard_map/psum | solution.py:258
  (3565 shorter events, 1990.8 us)
Async XLA Ops:
  7.2 49.0 %all-gather.21.cloned.1.call-start = ((), (), s32[]{:S(2)}) async-start(), calls=%async_computation.17 | async-start | bytes 1114112 | tf_op jit(solution)/shard_map/all_gather | solution.py:183
  8.0 99.2 %all-gather.15.cloned.1.call-start = ((), (), s32[]{:S(2)}) async-start(), calls=%async_computation.14 | async-start | bytes 6291456 | tf_op jit(solution)/shard_map/all_gather | solution.py:181
  14.8 131.6 %all-gather.17.cloned.1.call-start = ((), (), s32[]{:S(2)}) async-start(), calls=%async_computation.15 | async-start | bytes 1114112 | tf_op jit(solution)/shard_map/all_gather | solution.py:184
  15.6 200.8 %all-gather.19.cloned.1.call-start = ((), (), s32[]{:S(2)}) async-start(), calls=%async_computation.16 | async-start | bytes 2228224 | tf_op jit(solution)/shard_map/all_gather | solution.py:185
  16.1 608.6 %all-gather.23.cloned.1.call-start = ((), (), s32[]{:S(2)}) async-start(), calls=%async_computation.18 | async-start | bytes 2228224 | tf_op jit(solution)/shard_map/all_gather | solution.py:186
  16.7 626.4 %all-gather.25.cloned.1.call-start = ((), (), s32[]{:S(2)}) async-start(), calls=%async_computation.19 | async-start | bytes 2228224 | tf_op jit(solution)/shard_map/all_gather | solution.py:189
  17.3 736.1 %reduce-scatter.19.cloned.1.call-start = ((), (), s32[]{:S(2)}) async-start(), calls=%async_computation.20 | async-start | bytes 12582912 | tf_op jit(solution)/shard_map/reduce_scatter | solution.py:236
  55.7 569.0 %copy-start.146 = (f32[1,2,4,128]{3,1,2,0:T(2,128)}, f32[1,2,4,128]{3,1,2,0:T(2,128)S(1)}, u32[]{:S(2)}) copy-start(f32[1,2,4,128]{3,1,2,0:T(2,128)S(1)} %copy.585) | copy-start | bytes 12292
  653.9 146.4 %all-gather.29.cloned.1.call-start = ((), (), s32[]{:S(2)}) async-start(), calls=%async_computation.22 | async-start | bytes 3063808 | tf_op jit(solution)/shard_map/all_gather | solution.py:243
  654.7 203.0 %all-gather.27.cloned.1.call-start = ((), (), s32[]{:S(2)}) async-start(), calls=%async_computation.21 | async-start | bytes 6291456 | tf_op jit(solution)/shard_map/all_gather | solution.py:241
  760.0 144.4 %all-gather.31.cloned.1.call-start = ((), (), s32[]{:S(2)}) async-start(), calls=%async_computation.23 | async-start | bytes 3063808 | tf_op jit(solution)/shard_map/all_gather | solution.py:244
  760.6 189.1 %all-gather.33.cloned.1.call-start = ((), (), s32[]{:S(2)}) async-start(), calls=%async_computation.24 | async-start | bytes 3063808 | tf_op jit(solution)/shard_map/all_gather | solution.py:245
  761.3 253.9 %reduce-scatter.21.cloned.1.call-start = ((), (), s32[]{:S(2)}) async-start(), calls=%async_computation.25 | async-start | bytes 6291456 | tf_op jit(solution)/shard_map/reduce_scatter | solution.py:249
  961.1 117.4 %all-gather.35.cloned.1.call-start = ((), (), s32[]{:S(2)}) async-start(), calls=%async_computation.26 | async-start | bytes 6291456 | tf_op jit(solution)/shard_map/all_gather | solution.py:264
  1021.7 148.2 %reduce-scatter.23.cloned.1.call-start = ((), (), s32[]{:S(2)}) async-start(), calls=%async_computation.27 | async-start | bytes 6291456 | tf_op jit(solution)/shard_map/reduce_scatter | solution.py:275
  1115.4 124.0 %all-gather.37.cloned.1.call-start = ((), (), s32[]{:S(2)}) async-start(), calls=%async_computation.28 | async-start | bytes 6291456 | tf_op jit(solution)/shard_map/all_gather | solution.py:280
  1182.3 1572.8 %reduce-scatter.41.cloned.1.call-start = ((), (), s32[]{:S(2)}) async-start(), calls=%async_computation.37 | async-start | bytes 3063808 | tf_op jit(solution)/shard_map/reduce_scatter | solution.py:303
  1194.2 1562.6 %reduce-scatter.37.cloned.1.call-start = ((), (), s32[]{:S(2)}) async-start(), calls=%async_computation.35 | async-start | bytes 3063808 | tf_op jit(solution)/shard_map/reduce_scatter | solution.py:297
  1205.9 1552.6 %reduce-scatter.39.cloned.1.call-start = ((), (), s32[]{:S(2)}) async-start(), calls=%async_computation.36 | async-start | bytes 3063808 | tf_op jit(solution)/shard_map/reduce_scatter | solution.py:300
  1239.4 1523.7 %reduce-scatter.43.cloned.1.call-start = ((), (), s32[]{:S(2)}) async-start(), calls=%async_computation.38 | async-start | bytes 278528
  2574.8 189.7 %reduce-scatter.45.cloned.1.call-start = ((), (), s32[]{:S(2)}) async-start(), calls=%async_computation.39 | async-start | bytes 278528
  2578.6 187.3 %reduce-scatter.29.cloned.1.call-start = ((), (), s32[]{:S(2)}) async-start(), calls=%async_computation.31 | async-start | bytes 1114112 | tf_op jit(solution)/shard_map/reduce_scatter | solution.py:309
  2592.0 217.3 %reduce-scatter.27.cloned.1.call-start = ((), (), s32[]{:S(2)}) async-start(), calls=%async_computation.30 | async-start | bytes 1114112 | tf_op jit(solution)/shard_map/reduce_scatter | solution.py:306
  2629.7 244.0 %reduce-scatter.35.cloned.1.call-start = ((), (), s32[]{:S(2)}) async-start(), calls=%async_computation.34 | async-start | bytes 2228224 | tf_op jit(solution)/shard_map/reduce_scatter | solution.py:324
  2660.8 277.6 %reduce-scatter.31.cloned.1.call-start = ((), (), s32[]{:S(2)}) async-start(), calls=%async_computation.32 | async-start | bytes 2228224 | tf_op jit(solution)/shard_map/reduce_scatter | solution.py:312
  2699.4 303.3 %reduce-scatter.33.cloned.1.call-start = ((), (), s32[]{:S(2)}) async-start(), calls=%async_computation.33 | async-start | bytes 2228224 | tf_op jit(solution)/shard_map/reduce_scatter | solution.py:315
  2711.7 347.2 %reduce-scatter.25.cloned.1.call-start = ((), (), s32[]{:S(2)}) async-start(), calls=%async_computation.29 | async-start | bytes 6291456 | tf_op jit(solution)/shard_map/reduce_scatter | solution.py:291
  2754.2 304.8 %copy-start.37 = (bf16[1024,1024]{1,0:T(8,128)(2,1)S(1)}, bf16[1024,1024]{1,0:T(8,128)(2,1)}, u32[]{:S(2)}) copy-start(bf16[1024,1024]{1,0:T(8,128)(2,1)} %param.26) | copy-start | bytes 6291460
  2754.2 304.8 %copy-start.95 = (f32[1024]{0:T(1024)S(1)}, f32[1024]{0:T(1024)}, u32[]{:S(2)}) copy-start(f32[1024]{0:T(1024)} %copy-done.94) | copy-start | bytes 12292
  2754.2 304.7 %copy-start.96 = (f32[1024]{0:T(1024)S(1)}, f32[1024]{0:T(1024)}, u32[]{:S(2)}) copy-start(f32[1024]{0:T(1024)} %param.30) | copy-start | bytes 12292
  2758.5 303.7 %copy-start.106 = (f32[1024]{0:T(1024)S(1)}, f32[1024]{0:T(1024)}, u32[]{:S(2)}) copy-start(f32[1024]{0:T(1024)} %copy-done.105) | copy-start | bytes 12292
  2760.2 302.1 %copy-start.143 = (f32[256]{0:T(256)S(1)}, f32[256]{0:T(256)}, u32[]{:S(2)}) copy-start(f32[256]{0:T(256)} %get-tuple-element.792) | copy-start | bytes 3076
  (700 other events, 7476.3 us)
Sparse Core Ops, SparseCore 0:
  10.2 38.1 all-gather.20
  50.5 56.6 all-gather.14
  109.4 36.9 all-gather.16
  148.4 40.3 all-gather.18
  190.8 40.1 all-gather.22
  233.0 40.1 all-gather.24
  654.0 99.2 reduce-scatter.18
  755.9 44.3 all-gather.28
  802.5 55.1 all-gather.26
  860.0 44.3 all-gather.30
  906.9 42.6 all-gather.32
  961.2 53.9 reduce-scatter.20
  1021.8 56.6 all-gather.34
  1115.5 54.2 reduce-scatter.22
  1182.4 56.7 all-gather.36
  1243.3 64.7 reduce-scatter.40
  1311.7 63.9 reduce-scatter.36
  1379.8 64.0 reduce-scatter.38
  2574.9 55.5 reduce-scatter.42
  2634.4 54.2 reduce-scatter.44
  2692.4 56.3 reduce-scatter.28
  2752.9 56.4 reduce-scatter.26
  2813.1 60.5 reduce-scatter.34
  2877.8 60.5 reduce-scatter.30
  2942.1 60.5 reduce-scatter.32
  3005.5 53.4 reduce-scatter.24
where the time goes:
time: 3140 us; the launch traced here: 3120 us
  matrix products  1220 us (39%)
  waiting for transfers between devices  758 us (24%)
  local copies, waits for them, and re-layouts  576 us (18%)
  other arithmetic  386 us (12%)
  blocking collectives  116 us (4%)
  loops' own time  42.1 us (1%)
    dot_general x320, matrix products, lower_inverse(): power = jnp.einsum('hij,hjk->hik', power, power, precision=exact_precision)  163 us
    dot_general x320, matrix products, lower_inverse(): jnp.einsum('hij,hjk->hik', inverse, power, precision=exact_precision)  154 us
    squeeze x128, local copies, waits for them, and re-layouts, mixer_sequence(): lax.scan(jax.checkpoint(block_update), state, carried_in)  152 us
    dot_general x64, matrix products, block_update(): jnp.einsum('ihd,hde->ihe', keys, state, precision=exact_precision)  134 us
    dot_general x64, matrix products, block_update(): jnp.einsum('ihd,hde->ihe', queries, state, precision=exact_precision)  108 us
    reduce_scatter x1, waiting for transfers between devices, on_device(): lax.psum_scatter(contract_cols(mixed_low, full_out), 'tensor', scatter_di...  98.6 us
    dot_general x64, matrix products, block_update(): jnp.einsum('hij,jhe->hie', inverse, target_rows, precision=exact_precision)  91.9 us
    dot_general x10, matrix products, contract_cols(): lax.dot_general(left, right, (((1,), (1,)), ((), ())), preferred_element_...  87.2 us
  transfers between devices with their start and end apart: 26, of which 15 were waited for; matrix products, arithmetic and copies ran while one was open for 65% of the time, Pallas kernels for 0%

commit v1 on v0

--- a/solution.py
+++ b/solution.py
@@ -145,7 +145,7 @@
     return (gate_pre, up_pre)
 
 
-def on_device(
+def on_device_split(
     layer_input,
     target,
     segment,
@@ -378,6 +378,224 @@
     )
 
 
+def gather_all(local):
+    rows = lax.all_gather(local, ("tensor", "dp"), axis=0, tiled=True)
+    shares = lax.axis_size("tensor")
+    return rows.reshape(shares, rows.shape[0] // shares, rows.shape[1])
+
+
+def scatter_all(parts):
+    shares, rows, cols = parts.shape
+    return lax.psum_scatter(
+        parts.reshape(shares * rows, cols), ("tensor", "dp"), scatter_dimension=0, tiled=True
+    ).astype(jnp.float32)
+
+
+def columns(array, sizes):
+    pieces, start = [], 0
+    for size in sizes:
+        pieces.append(array[..., start : start + size])
+        start += size
+    return pieces
+
+
+def on_device_whole(
+    layer_input,
+    target,
+    segment,
+    pad_mask,
+    norm1_gain,
+    w_query,
+    w_key,
+    w_value,
+    w_gate_out,
+    w_decay,
+    w_beta,
+    conv_query,
+    conv_key,
+    conv_value,
+    decay_scale,
+    decay_bias,
+    out_norm_gain,
+    w_out,
+    norm2_gain,
+    w_ffn_gate,
+    w_ffn_up,
+    w_ffn_down,
+):
+    own_rows, width = layer_input.shape
+    shares = lax.axis_size("tensor")
+    sequences = own_rows // LENGTH
+    tensor_index = lax.axis_index("tensor")
+    low = jnp.bfloat16
+    proj_local = (w_query, w_key, w_value, w_gate_out, w_decay, w_beta)
+    proj_sizes = [item.shape[1] for item in proj_local]
+    used = sum(proj_sizes)
+    padded = -(-used // 128) * 128
+    proj_all = gather_all(
+        jnp.concatenate(proj_local + (jnp.zeros((w_query.shape[0], padded - used), low),), axis=1)
+    )
+    rest_local = (w_out, w_ffn_gate, w_ffn_up, w_ffn_down)
+    rest_sizes = [item.shape[1] for item in rest_local]
+    rest_all = gather_all(jnp.concatenate(rest_local, axis=1))
+    out_all, gate_all, up_all, down_all = columns(rest_all, rest_sizes)
+    live = pad_mask.astype(jnp.float32)
+    count = lax.psum(jnp.sum(live), ("dp", "tensor"))
+    input_float = layer_input.astype(jnp.float32)
+    normed_float, norm1_pull = jax.vjp(rms_scale, input_float, norm1_gain)
+    normed = normed_float.astype(low)
+    seg_rows = lax.dynamic_slice_in_dim(segment, tensor_index * own_rows, own_rows, 0).reshape(
+        sequences, LENGTH
+    )
+    projected = [
+        columns(jnp.dot(normed, proj_all[part], preferred_element_type=jnp.float32), proj_sizes)
+        for part in range(shares)
+    ]
+    pre = [
+        jnp.concatenate([projected[part][item] for part in range(shares)], axis=1)
+        for item in range(6)
+    ]
+
+    def mixer_local(
+        q_pre, k_pre, v_pre, g_pre, a_pre, b_pre, conv_q, conv_k, conv_v, rate, bias, out_gain
+    ):
+        shaped = [
+            item.reshape(sequences, LENGTH, item.shape[1])
+            for item in (q_pre, k_pre, v_pre, g_pre, a_pre, b_pre)
+        ]
+        mixed_rows = jax.vmap(
+            mixer_sequence, in_axes=(0, 0, 0, 0, 0, 0, 0, None, None, None, None, None, None)
+        )(*shaped, seg_rows, conv_q, conv_k, conv_v, rate, bias, out_gain)
+        return mixed_rows.reshape(own_rows, mixed_rows.shape[2])
+
+    mixed, mixer_pull = jax.vjp(
+        mixer_local,
+        *pre,
+        conv_query,
+        conv_key,
+        conv_value,
+        decay_scale,
+        decay_bias,
+        out_norm_gain
+    )
+    mixed_low = mixed.astype(low)
+    value_cols = w_value.shape[1]
+    residual = input_float
+    for part in range(shares):
+        residual = residual + contract_cols(
+            mixed_low[:, part * value_cols : (part + 1) * value_cols], out_all[part]
+        )
+    normed2_float, norm2_pull = jax.vjp(rms_scale, residual, norm2_gain)
+    normed2 = normed2_float.astype(low)
+    output = residual
+    kept = []
+    for part in range(shares):
+        gate_pre, up_pre = feed_inputs(normed2, gate_all[part], up_all[part])
+        hidden = (jax.nn.silu(gate_pre) * up_pre).astype(low)
+        output = output + contract_cols(hidden, down_all[part])
+        kept.append((gate_pre, up_pre, hidden))
+    error = output - target.astype(jnp.float32)
+    loss_sum = jnp.sum(live[:, None] * error * error)
+    all_tokens = own_rows * lax.axis_size("dp") * lax.axis_size("tensor")
+    grad_output = error * live[:, None] * (all_tokens / count)
+    grad_ffn = grad_output.astype(low)
+    grad_normed2 = jnp.zeros_like(residual)
+    ffn_grads = []
+    for part in range(shares):
+        gate_pre, up_pre, hidden = kept[part]
+        grad_hidden = jnp.dot(grad_ffn, down_all[part], preferred_element_type=jnp.float32)
+        sigmoid_gate = jax.nn.sigmoid(gate_pre)
+        grad_gate = (
+            grad_hidden * up_pre * sigmoid_gate * (1.0 + gate_pre * (1.0 - sigmoid_gate))
+        ).astype(low)
+        grad_up = (grad_hidden * gate_pre * sigmoid_gate).astype(low)
+        grad_normed2 = (
+            grad_normed2
+            + contract_cols(grad_gate, gate_all[part])
+            + contract_cols(grad_up, up_all[part])
+        )
+        ffn_grads.append(
+            (
+                contract_rows(normed2, grad_gate),
+                contract_rows(normed2, grad_up),
+                contract_rows(grad_ffn, hidden),
+            )
+        )
+    grad_residual_norm, grad_gain_two = norm2_pull(grad_normed2)
+    grad_residual = grad_output + grad_residual_norm
+    grad_attention = grad_residual.astype(low)
+    grad_mixed = jnp.concatenate(
+        [
+            jnp.dot(grad_attention, out_all[part], preferred_element_type=jnp.float32)
+            for part in range(shares)
+        ],
+        axis=1,
+    )
+    rest_grads = jnp.stack(
+        [
+            jnp.concatenate(
+                [
+                    item.astype(low)
+                    for item in (
+                        contract_rows(
+                            grad_attention,
+                            mixed_low[:, part * value_cols : (part + 1) * value_cols],
+                        ),
+                    )
+                    + ffn_grads[part]
+                ],
+                axis=1,
+            )
+            for part in range(shares)
+        ]
+    )
+    own_out, own_gate, own_up, own_down = columns(scatter_all(rest_grads), rest_sizes)
+    mixer_grads = mixer_pull(grad_mixed)
+    grad_normed = jnp.zeros_like(residual)
+    proj_grads = []
+    for part in range(shares):
+        grad_part = jnp.concatenate(
+            [
+                item[:, part * size : (part + 1) * size].astype(low)
+                for item, size in zip(mixer_grads[:6], proj_sizes)
+            ]
+            + [jnp.zeros((own_rows, padded - used), low)],
+            axis=1,
+        )
+        grad_normed = grad_normed + contract_cols(grad_part, proj_all[part])
+        proj_grads.append(contract_rows(normed, grad_part).astype(low))
+    own_proj = columns(scatter_all(jnp.stack(proj_grads)), proj_sizes)
+    grad_input_norm, grad_gain_one = norm1_pull(grad_normed)
+    grad_input = grad_residual + grad_input_norm
+    summed = lax.psum(
+        (grad_gain_one, grad_gain_two) + tuple(mixer_grads[6:12]) + (loss_sum,), ("dp", "tensor")
+    )
+    loss = summed[8] / (count * width)
+    return (
+        output,
+        loss,
+        grad_input,
+        summed[0],
+        *own_proj,
+        summed[2],
+        summed[3],
+        summed[4],
+        summed[5],
+        summed[6],
+        summed[7],
+        own_out,
+        summed[1],
+        own_gate,
+        own_up,
+        own_down,
+    )
+
+
+def on_device(layer_input, *others):
+    whole = layer_input.shape[0] % LENGTH == 0
+    return (on_device_whole if whole else on_device_split)(layer_input, *others)
+
+
 def solution(mesh):
     return jax.shard_map(
         on_device,

time: 3140 us -> 2680 us (0.85)
  waiting for transfers between devices: 758 us -> 281 us
    all_gather x12 -> x2, waiting for transfers between devices: 302 us -> 41.1 us  [gather_all(): rows = lax.all_gather(local, ('tensor', 'dp'), axis=0, tiled=True)]
    reduce_scatter x12 -> x1, waiting for transfers between devices: 451 us -> 234 us  [scatter_all(): lax.psum_scatter(parts.reshape(shares * rows, cols), ('tensor', 'dp'), sc...]
    reshape x15 -> x0, local copies, waits for them, and re-layouts: 75.8 us -> none  [the longest x1 10.9 us: mixer_sequence(): jax.nn.silu(short_conv(v_pre, conv_v, masks))]
    dot_general x320, matrix products: 154 us -> 223 us  [lower_inverse(): jnp.einsum('hij,hjk->hik', inverse, power, precision=exact_precision)]
    dynamic_update_slice x16 -> x80, local copies, waits for them, and re-layouts: 10.1 us -> 77.7 us  [mixer_sequence(): lax.scan(jax.checkpoint(block_update), state, carried_in)]
    another operation x0 -> x11, other arithmetic: none -> 66.2 us
    reduce_sum x64 -> x2, local copies, waits for them, and re-layouts: 47.1 us -> 0.32 us  [unit_rows(): values * lax.rsqrt(jnp.sum(values * values, axis=-1, keepdims=True) + 1e-06)]
    dynamic_slice x1 -> x65, local copies, waits for them, and re-layouts: 0.07 us -> 45.8 us  [the longest x64 45.1 us: mixer_sequence(): lax.scan(jax.checkpoint(block_update), state, carried_in)]
  transfers between devices with their start and end apart: 26 -> 4, of which waited for: 15 -> 3; matrix products, arithmetic and copies ran while one was open for 65% -> 25% of each run, Pallas kernels for 0% -> 0%
where the time goes in v1:
time: 2680 us; the launch traced here: 2650 us
  matrix products  1210 us (45%)
  local copies, waits for them, and re-layouts  605 us (23%)
  other arithmetic  388 us (14%)
  waiting for transfers between devices  281 us (10%)
  blocking collectives  87.5 us (3%)
  loops' own time  54 us (2%)
    reduce_scatter x1, waiting for transfers between devices, scatter_all(): lax.psum_scatter(parts.reshape(shares * rows, cols), ('tensor', 'dp'), sc...  234 us
    dot_general x320, matrix products, lower_inverse(): jnp.einsum('hij,hjk->hik', inverse, power, precision=exact_precision)  223 us
    dot_general x320, matrix products, lower_inverse(): power = jnp.einsum('hij,hjk->hik', power, power, precision=exact_precision)  143 us
    dot_general x64, matrix products, block_update(): jnp.einsum('ihd,hde->ihe', keys, state, precision=exact_precision)  129 us
    dot_general x64, matrix products, block_update(): jnp.einsum('ihd,hde->ihe', queries, state, precision=exact_precision)  124 us
    squeeze x96, local copies, waits for them, and re-layouts, mixer_sequence(): lax.scan(jax.checkpoint(block_update), state, carried_in)  108 us
    dot_general x64, matrix products, block_update(): key_gram = jnp.einsum('ihd,jhd->ijh', keys, keys, precision=exact_precision)  107 us
    unnamed x323, local copies, waits for them, and re-layouts  89.7 us
  transfers between devices with their start and end apart: 4, of which 3 were waited for; matrix products, arithmetic and copies ran while one was open for 25% of the time, Pallas kernels for 0%

profile of v1, /device:TPU:8, one launch (start us, length us, event | category | flops | bytes accessed | tf_op | source)
XLA Modules:
  0.0 2648.0 jit_solution(18042416344715169501)
XLA Ops:
  20.9 41.9 %psum.71 = f32[]{:T(128)} all-reduce(f32[]{:T(128)} %convert_reduce_fusion), channel_id=1, replica_groups=mesh['dp'=16,'tensor'=2] {'dp','tensor'}, use_global_device_ids=true, to_apply=%region_11.12 | all-reduce | flops 1 | bytes 8 | tf_op jit(solution)/shard_map/psum | solution.py:443
  69.7 41.1 %all-gather.3.cloned.1.call-done = bf16[2048,3200]{1,0:T(8,128)(2,1)} async-done(((bf16[64,3200]{1,0:T(8,128)(2,1)}), bf16[2048,3200]{1,0:T(8,128)(2,1)}) %all-gather.3.cloned.1.call-update) | async-done | bytes 13107216 | tf_op jit(solution)/shard_map/all_gather | solution.py:382
  110.7 10.3 fusion.233
  124.6 17.3 fusion.229
  147.5 14.0 fusion.329
  196.4 16.0 fusion.224
  249.5 367.0 %while.42 = (s32[]{:T(128)}, f32[1,8,128,256]{3,2,1,0:T(8,128)S(1)}, f32[16,1,64,8,256]{4,2,3,1,0:T(8,128)}, f32[16,1,8,128,256]{4,3,2,1,0:T(8,128)}, s32[16,1,6...) while((s32[]{:T(128)}, ...), condition=%wide.region_5.6_spmd.clone, body=%wide.region_3.0_spmd.clone.sunk | while | flops 1160663296 | bytes 16642413 | solution.py:124
  616.8 13.4 copy.782
  655.6 12.1 multiply_convert_fusion
  688.7 9.9 multiply_convert_fusion.6
  720.3 10.9 multiply_convert_fusion.3
  745.6 9.1 multiply_convert_fusion.1
  754.7 8.9 fusion.277
  763.6 8.5 multiply_reduce_fusion.11
  789.6 17.4 fusion.217
  807.0 10.9 copy.974
  825.6 13.4 multiply_reduce_fusion.4
  854.4 1156.3 %while.43 = (s32[]{:T(128)}, f32[1,8,128,256]{2,3,1,0:T(8,128)}, f32[16,1,64,8,128]{4,3,2,0,1:T(8,128)}, f32[16,1,64,8,128]{4,3,2,0,1:T(8,128)}, f32[16,1,64,8,2...) while((s32[]{:T(128)}, f32[1,8,128,256]{2,3,1,0:T(8,128)}, ...), condition=%wide.region_24.25_spmd.clone, body=%wide.region_14.24_spmd.clone.sunk | while | flops 3179406080 | bytes 84860888 | solution.py:124
  2020.3 9.3 transpose.429
  2029.6 23.1 multiply_reduce_fusion.8
  2099.7 28.4 %multiply_reduce_fusion.19 = (f32[1024]{0:T(1024)}, f32[1024]{0:T(1024)}, f32[1024]{0:T(1024)}, f32[1024]{0:T(1024)}, f32[1024]{0:T(1024)}, /*index=5*/f32[1024]...) fusion(f32[1,1021,1024]{2,1,0:T(8,128)} %bitcast.1398, ...), kind=kLoop, calls=%fused_computation.439 | loop fusion | flops 54517760 | bytes 75493376 | tf_op jit(solution)/shard_map/transpose(jvp(vmap()))/reduce_sum | solution.py:31
  2150.6 12.8 fusion.249
  2168.3 8.2 fusion.284
  2195.0 11.2 concatenate.199
  2206.1 12.3 fusion.225
  2218.6 11.1 concatenate.200
  2229.7 10.8 fusion.226
  2291.6 9.0 pad_maximum_fusion
  2302.1 11.7 fusion.227
  2313.8 13.4 fusion.238
  2327.2 45.6 %all-reduce.36 = (f32[]{:T(128)}, f32[1024]{0:T(1024)}, f32[4,1024]{1,0:T(4,128)}, f32[4,1024]{1,0:T(4,128)}, f32[4,2048]{1,0:T(4,128)}, /*index=5*/f32[8]{0:T(128)}, f32[8]{0:T(128)}, f32[256]{0:T(256)}, f32[1024]{0:T(1024)}) all-reduce(f32[]{:T(128)} %get-tuple-element.1110, ...), channel_id=1, replica_groups=mesh['dp'=16,'tensor'=2] {'dp','tensor'}, use_global_device_ids=true, to_apply=%region_9.10 | all-reduce | flops 18705 | bytes 149640 | tf_op jit(solution)/shard_map/psum | solution.py:570
  2402.1 234.1 %reduce-scatter.5.cloned.1.call-done = bf16[64,5248]{1,0:T(8,128)(2,1)} async-done(((bf16[2048,5248]{1,0:T(8,128)(2,1)}), bf16[64,5248]{1,0:T(8,128)(2,1)}) %reduce-scatter.5.cloned.1.call-update) | async-done | bytes 671760 | tf_op jit(solution)/shard_map/reduce_scatter | solution.py:389
  (3376 shorter events, 1878.7 us)
Async XLA Ops:
  7.2 103.5 %all-gather.3.cloned.1.call-start = ((), (), s32[]{:S(2)}) async-start(), calls=%async_computation.2 | async-start | bytes 13516800 | tf_op jit(solution)/shard_map/all_gather | solution.py:382
  10.8 656.9 %all-gather.5.cloned.1.call-start = ((), (), s32[]{:S(2)}) async-start(), calls=%async_computation.3 | async-start | bytes 22167552 | tf_op jit(solution)/shard_map/all_gather | solution.py:382
  12.9 2383.7 %reduce-scatter.7.cloned.1.call-start = ((), (), s32[]{:S(2)}) async-start(), calls=%async_computation.5 | async-start | bytes 13516800
  19.3 653.2 %copy-start.43 = (bf16[1024,1024]{0,1:T(8,128)(2,1)}, bf16[1024,1024]{0,1:T(8,128)(2,1)S(1)}, u32[]{:S(2)}) copy-start(bf16[1024,1024]{0,1:T(8,128)(2,1)S(1)} %copy.765) | copy-start | bytes 6291460
  19.3 48.9 %copy-start.142 = (s32[2048]{0:T(1024)S(1)}, s32[2048]{0:T(1024)}, u32[]{:S(2)}) copy-start(s32[2048]{0:T(1024)} %param.28) | copy-start | bytes 24580
  19.3 91.4 %copy-start.149 = (f32[1024]{0:T(1024)S(1)}, f32[1024]{0:T(1024)}, u32[]{:S(2)}) copy-start(f32[1024]{0:T(1024)} %param.30) | copy-start | bytes 12292
  19.8 101.3 %copy-start.102 = (f32[1024]{0:T(1024)}, f32[1024]{0:T(1024)S(1)}, u32[]{:S(2)}) copy-start(f32[1024]{0:T(1024)S(1)} %fusion.246) | copy-start | bytes 12292
  19.8 104.8 %copy-start.138 = (f32[1024]{0:T(1024)}, f32[1024]{0:T(1024)S(1)}, u32[]{:S(2)}) copy-start(f32[1024]{0:T(1024)S(1)} %fusion.313) | copy-start | bytes 12292
  19.9 149.7 %copy-start.104 = (f32[1,1024]{1,0:T(1,128)}, f32[1,1024]{1,0:T(1,128)S(1)}, u32[]{:S(2)}) copy-start(f32[1,1024]{1,0:T(1,128)S(1)} %get-tuple-element.1138) | copy-start | bytes 12292
  19.9 149.7 %copy-start.108 = (f32[1,1024]{1,0:T(1,128)}, f32[1,1024]{1,0:T(1,128)S(1)}, u32[]{:S(2)}) copy-start(f32[1,1024]{1,0:T(1,128)S(1)} %get-tuple-element.1139) | copy-start | bytes 12292
  19.9 149.7 %copy-start.110 = (f32[1,1024]{1,0:T(1,128)}, f32[1,1024]{1,0:T(1,128)S(1)}, u32[]{:S(2)}) copy-start(f32[1,1024]{1,0:T(1,128)S(1)} %get-tuple-element.1141) | copy-start | bytes 12292
  19.9 149.7 %copy-start.114 = (f32[1,1024]{1,0:T(1,128)}, f32[1,1024]{1,0:T(1,128)S(1)}, u32[]{:S(2)}) copy-start(f32[1,1024]{1,0:T(1,128)S(1)} %get-tuple-element.1140) | copy-start | bytes 12292
  19.9 176.4 %copy-start.89 = (f32[1,2048]{1,0:T(1,128)}, f32[1,2048]{1,0:T(1,128)S(1)}, u32[]{:S(2)}) copy-start(f32[1,2048]{1,0:T(1,128)S(1)} %get-tuple-element.1132) | copy-start | bytes 24580
  19.9 176.4 %copy-start.91 = (f32[1,2048]{1,0:T(1,128)}, f32[1,2048]{1,0:T(1,128)S(1)}, u32[]{:S(2)}) copy-start(f32[1,2048]{1,0:T(1,128)S(1)} %get-tuple-element.1133) | copy-start | bytes 24580
  20.0 176.4 %copy-start.93 = (f32[1,2048]{1,0:T(1,128)}, f32[1,2048]{1,0:T(1,128)S(1)}, u32[]{:S(2)}) copy-start(f32[1,2048]{1,0:T(1,128)S(1)} %get-tuple-element.1134) | copy-start | bytes 24580
  20.0 176.4 %copy-start.95 = (f32[1,2048]{1,0:T(1,128)}, f32[1,2048]{1,0:T(1,128)S(1)}, u32[]{:S(2)}) copy-start(f32[1,2048]{1,0:T(1,128)S(1)} %get-tuple-element.1135) | copy-start | bytes 24580
  20.0 205.9 %copy-start.106 = (f32[1,1024]{1,0:T(1,128)}, f32[1,1024]{1,0:T(1,128)S(1)}, u32[]{:S(2)}) copy-start(f32[1,1024]{1,0:T(1,128)S(1)} %get-tuple-element.1142) | copy-start | bytes 12292
  20.0 205.9 %copy-start.112 = (f32[1,1024]{1,0:T(1,128)}, f32[1,1024]{1,0:T(1,128)S(1)}, u32[]{:S(2)}) copy-start(f32[1,1024]{1,0:T(1,128)S(1)} %get-tuple-element.1143) | copy-start | bytes 12292
  20.0 205.9 %copy-start.116 = (f32[1,1024]{1,0:T(1,128)}, f32[1,1024]{1,0:T(1,128)S(1)}, u32[]{:S(2)}) copy-start(f32[1,1024]{1,0:T(1,128)S(1)} %get-tuple-element.1145) | copy-start | bytes 12292
  20.0 205.8 %copy-start.118 = (f32[1,1024]{1,0:T(1,128)}, f32[1,1024]{1,0:T(1,128)S(1)}, u32[]{:S(2)}) copy-start(f32[1,1024]{1,0:T(1,128)S(1)} %get-tuple-element.1144) | copy-start | bytes 12292
  20.1 220.1 %copy-start.145 = (f32[8]{0:T(128)}, f32[8]{0:T(128)S(1)}, u32[]{:S(2)}) copy-start(f32[8]{0:T(128)S(1)} %neg.151) | copy-start | bytes 100
  66.8 159.1 %copy-start.79 = (f32[1,1024]{1,0:T(1,128)}, f32[1,1024]{1,0:T(1,128)S(1)}, u32[]{:S(2)}) copy-start(f32[1,1024]{1,0:T(1,128)S(1)} %get-tuple-element.1152) | copy-start | bytes 12292
  66.8 159.1 %copy-start.81 = (f32[1,1024]{1,0:T(1,128)}, f32[1,1024]{1,0:T(1,128)S(1)}, u32[]{:S(2)}) copy-start(f32[1,1024]{1,0:T(1,128)S(1)} %get-tuple-element.1153) | copy-start | bytes 12292
  68.2 157.7 %copy-start.83 = (f32[1024]{0:T(1024)}, f32[1024]{0:T(1024)S(1)}, u32[]{:S(2)}) copy-start(f32[1024]{0:T(1024)S(1)} %fusion.312) | copy-start | bytes 12292
  124.6 40.2 %copy-start.45 = (f32[1024,512]{1,0:T(8,128)}, f32[1024,512]{1,0:T(8,128)S(1)}, u32[]{:S(2)}) copy-start(f32[1024,512]{1,0:T(8,128)S(1)} %get-tuple-element.1093) | copy-start | bytes 6291460
  124.6 40.2 %copy-start.46 = (f32[1024,512]{1,0:T(8,128)}, f32[1024,512]{1,0:T(8,128)S(1)}, u32[]{:S(2)}) copy-start(f32[1024,512]{1,0:T(8,128)S(1)} %get-tuple-element.1094) | copy-start | bytes 6291460
  677.1 28.4 %copy-start.63 = (bf16[1024,1024]{0,1:T(8,128)(2,1)}, bf16[1024,1024]{0,1:T(8,128)(2,1)S(1)}, u32[]{:S(2)}) copy-start(bf16[1024,1024]{0,1:T(8,128)(2,1)S(1)} %multiply_convert_fusion.7) | copy-start | bytes 6291460
  720.3 51.8 %copy-start.51 = (f32[1024,1024]{0,1:T(8,128)}, f32[1024,1024]{0,1:T(8,128)S(1)}, u32[]{:S(2)}) copy-start(f32[1024,1024]{0,1:T(8,128)S(1)} %get-tuple-element.1161) | copy-start | bytes 12582916
  2029.6 23.2 copy-start.96
  2099.7 30.4 %copy-start.115 = (f32[1,1024]{1,0:T(1,128)S(1)}, f32[1,1024]{1,0:T(1,128)}, u32[]{:S(2)}) copy-start(f32[1,1024]{1,0:T(1,128)} %copy-done.114) | copy-start | bytes 12292
  2099.7 30.4 %copy-start.119 = (f32[1,1024]{1,0:T(1,128)S(1)}, f32[1,1024]{1,0:T(1,128)}, u32[]{:S(2)}) copy-start(f32[1,1024]{1,0:T(1,128)} %copy-done.118) | copy-start | bytes 12292
  2247.9 388.3 %reduce-scatter.5.cloned.1.call-start = ((), (), s32[]{:S(2)}) async-start(), calls=%async_computation.4 | async-start | bytes 22167552 | tf_op jit(solution)/shard_map/reduce_scatter | solution.py:389
  (617 other events, 3051.2 us)
Sparse Core Ops, SparseCore 0:
  11.4 99.2 all-gather.2
  113.6 134.5 all-gather.4
  2248.0 148.5 reduce-scatter.6
  2398.9 237.2 reduce-scatter.4

commit v2 on v1

--- a/solution.py
+++ b/solution.py
@@ -1,6 +1,10 @@
+import functools
+
 import jax
 import jax.numpy as jnp
 from jax import lax
+from jax.experimental import pallas as pl
+from jax.experimental.pallas import tpu as pltpu
 from jax.sharding import PartitionSpec as P
 
 CH = 64
@@ -378,6 +382,464 @@
     )
 
 
+TILE = 128
+
+
+def mm(left, right, dims=((1,), (0,))):
+    return lax.dot_general(
+        left.astype(jnp.bfloat16),
+        right.astype(jnp.bfloat16),
+        (dims, ((), ())),
+        preferred_element_type=jnp.float32,
+    )
+
+
+def mm_nt(left, right):
+    return mm(left, right, ((1,), (1,)))
+
+
+def mm_tn(left, right):
+    return mm(left, right, ((0,), (0,)))
+
+
+def mm_fine(left, right):
+    left_high, right_high = left.astype(jnp.bfloat16), right.astype(jnp.bfloat16)
+    left_rest = left - left_high.astype(jnp.float32)
+    right_rest = right - right_high.astype(jnp.float32)
+    return mm(left_high, right_high) + (mm(left_high, right_rest) + mm(left_rest, right_high))
+
+
+def ones_mm(ones, right):
+    high = right.astype(jnp.bfloat16)
+    rest = right - high.astype(jnp.float32)
+    middle = rest.astype(jnp.bfloat16)
+    return mm(ones, high) + (mm(ones, middle) + mm(ones, rest - middle.astype(jnp.float32)))
+
+
+def unit_lower_inverse(part, row, col):
+    size = part.shape[0]
+    eye = (row == col).astype(jnp.float32)
+    block = 16
+    power = jnp.where((row // block) == (col // block), -part, 0.0)
+    inverse = eye + power
+    covered = 2
+    while covered < block:
+        power = mm_fine(power, power)
+        inverse = inverse + mm_fine(inverse, power)
+        covered *= 2
+    while block < size:
+        pair = (row // (2 * block)) == (col // (2 * block))
+        cross = jnp.where(pair & ((row // block) != (col // block)), part, 0.0)
+        inverse = inverse - mm(mm(inverse, cross), inverse)
+        block *= 2
+    return inverse
+
+
+def stable_softplus(values):
+    return jnp.maximum(values, 0.0) + jnp.log1p(jnp.exp(-jnp.abs(values)))
+
+
+def decay_tiles(raw, rate, bias):
+    shifted = raw + bias
+    soft = stable_softplus(shifted)
+    return shifted, soft, -rate * soft
+
+
+def grids():
+    row = lax.broadcasted_iota(jnp.int32, (TILE, TILE), 0)
+    col = lax.broadcasted_iota(jnp.int32, (TILE, TILE), 1)
+    return row, col
+
+
+def forward_body(
+    heads,
+    proj_ref,
+    info_ref,
+    conv_ref,
+    rates_ref,
+    gain_ref,
+    mixed_ref,
+    conv_out_ref,
+    rows_out_ref,
+    state_out_ref,
+    inverse_out_ref,
+    pseudo_out_ref,
+    earlier_ref,
+    state_ref,
+):
+    first = pl.program_id(2) == 0
+    blocks = 4 * heads
+
+    @pl.when(first)
+    def _():
+        earlier_ref[:, 0:8, :] = jnp.zeros((blocks, 8, TILE), jnp.float32)
+        state_ref[...] = jnp.zeros(state_ref.shape, jnp.float32)
+
+    row, col = grids()
+    info = info_ref[...]
+    info_rows = info.T
+    masks = [jnp.broadcast_to(info[:, j : j + 1], (TILE, TILE)) for j in range(3)]
+    visible = (row >= col) & (info[:, 4:5] == info_rows[4:5, :])
+    raw = proj_ref[0, :, 6 * heads * TILE : 6 * heads * TILE + TILE]
+    _, _, log_decay = decay_tiles(raw, rates_ref[0, 0:1, :], rates_ref[0, 1:2, :])
+    total = ones_mm((row >= col).astype(jnp.float32), log_decay)
+    total_rows = total.T
+    carry = jnp.exp(total) * info[:, 3:4]
+    beta_tile = jax.nn.sigmoid(raw)
+    for block in range(blocks):
+        earlier_ref[block, 8 : 8 + TILE, :] = proj_ref[0, :, block * TILE : (block + 1) * TILE]
+
+    def conv_block(block):
+        lanes = slice(block * TILE, (block + 1) * TILE)
+        result = earlier_ref[block, 8 : 8 + TILE, :] * conv_ref[0, 0:1, lanes]
+        for j in range(1, 4):
+            result = result + masks[j - 1] * (
+                earlier_ref[block, 8 - j : 8 - j + TILE, :] * conv_ref[0, j : j + 1, lanes]
+            )
+        conv_out_ref[0, :, lanes] = result
+        return result * jax.nn.sigmoid(result)
+
+    for head in range(heads):
+        query, key = conv_block(head), conv_block(heads + head)
+        query = query * (
+            lax.rsqrt(jnp.sum(query * query, axis=1, keepdims=True) + 1e-06) * TILE ** (-0.5)
+        )
+        key = key * lax.rsqrt(jnp.sum(key * key, axis=1, keepdims=True) + 1e-06)
+        value = jnp.concatenate(
+            [conv_block(2 * heads + 2 * head), conv_block(2 * heads + 2 * head + 1)], axis=1
+        )
+        spread = total[:, head : head + 1] - total_rows[head : head + 1, :]
+        weights = jnp.exp(jnp.where(visible, spread, -1e30))
+        beta = beta_tile[:, heads + head : heads + head + 1]
+        carried = carry[:, head : head + 1]
+        key_low, query_low = key.astype(jnp.bfloat16), query.astype(jnp.bfloat16)
+        both = jnp.concatenate([key_low, query_low], axis=0)
+        grams = mm_nt(both, key_low)
+        part = jnp.where(row > col, beta * weights * grams[:TILE], 0.0)
+        inverse = unit_lower_inverse(part, row, col).astype(jnp.bfloat16)
+        state = state_ref[head]
+        state_low = state.astype(jnp.bfloat16)
+        from_state = mm(both, state_low)
+        pseudo = mm(inverse, beta * (value - carried * from_state[:TILE])).astype(jnp.bfloat16)
+        rows = carried * from_state[TILE:] + mm(grams[TILE:] * weights, pseudo)
+        weighted = key.T * weights[TILE - 1 : TILE, :]
+        state_ref[head] = carried[TILE - 1 : TILE, :] * state + mm(weighted, pseudo)
+        lanes = slice(2 * head * TILE, 2 * (head + 1) * TILE)
+        state_out_ref[0, 0, head] = state_low
+        inverse_out_ref[0, 0, head] = inverse
+        pseudo_out_ref[0, :, lanes] = pseudo
+        rows_out_ref[0, :, lanes] = rows
+        gate = proj_ref[
+            0, :, (4 * heads + 2 * head) * TILE : (4 * heads + 2 * (head + 1)) * TILE
+        ]
+        scale = lax.rsqrt(jnp.mean(rows * rows, axis=1, keepdims=True) + 1e-06)
+        mixed_ref[:, lanes] = (
+            rows * scale * gain_ref[...] * (gate * jax.nn.sigmoid(gate))
+        ).astype(jnp.bfloat16)
+    for block in range(blocks):
+        earlier_ref[block, 0:8, :] = earlier_ref[block, TILE : TILE + 8, :]
+
+
+def backward_body(
+    heads,
+    proj_ref,
+    info_ref,
+    conv_ref,
+    rates_ref,
+    gain_ref,
+    conv_out_ref,
+    rows_ref,
+    state_in_ref,
+    inverse_ref,
+    pseudo_ref,
+    grad_ref,
+    grad_proj_ref,
+    grad_conv_ref,
+    grad_rates_ref,
+    grad_gain_ref,
+    later_ref,
+    grad_state_ref,
+):
+    step = pl.program_id(2)
+    blocks = 4 * heads
+
+    @pl.when(step == 0)
+    def _():
+        later_ref[:, TILE : TILE + 8, :] = jnp.zeros((blocks, 8, TILE), jnp.float32)
+        grad_state_ref[...] = jnp.zeros(grad_state_ref.shape, jnp.float32)
+
+    @pl.when((step == 0) & (pl.program_id(1) == 0))
+    def _():
+        grad_conv_ref[...] = jnp.zeros(grad_conv_ref.shape, jnp.float32)
+        grad_rates_ref[...] = jnp.zeros(grad_rates_ref.shape, jnp.float32)
+        grad_gain_ref[...] = jnp.zeros(grad_gain_ref.shape, jnp.float32)
+
+    row, col = grids()
+    info = info_ref[...]
+    info_rows = info.T
+    masks = [jnp.broadcast_to(info[:, 4 + j : 5 + j], (TILE, TILE)) for j in range(1, 4)]
+    visible = (row >= col) & (info[:, 4:5] == info_rows[4:5, :])
+    raw = proj_ref[0, :, 6 * heads * TILE : 6 * heads * TILE + TILE]
+    rate = rates_ref[0, 0:1, :]
+    shifted, soft, log_decay = decay_tiles(raw, rate, rates_ref[0, 1:2, :])
+    total = ones_mm((row >= col).astype(jnp.float32), log_decay)
+    total_rows = total.T
+    carry = jnp.exp(total) * info[:, 3:4]
+    beta_tile = jax.nn.sigmoid(raw)
+    grad_total = jnp.zeros((TILE, TILE), jnp.float32)
+    grad_beta = jnp.zeros((TILE, TILE), jnp.float32)
+    gain = gain_ref[...]
+    gain_sum = jnp.zeros((1, 2 * TILE), jnp.float32)
+
+    def activation(block):
+        value = conv_out_ref[0, :, block * TILE : (block + 1) * TILE]
+        gate = jax.nn.sigmoid(value)
+        return value * gate, gate * (1.0 + value * (1.0 - gate))
+
+    def close_block(block, grad):
+        later_ref[block, 0:TILE, :] = grad
+        lanes = slice(block * TILE, (block + 1) * TILE)
+        own = proj_ref[0, :, lanes]
+        result = grad * conv_ref[0, 0:1, lanes]
+        sums = [jnp.sum(grad * own, axis=0, keepdims=True)]
+        for j in range(1, 4):
+            moved = masks[j - 1] * later_ref[block, j : j + TILE, :]
+            result = result + moved * conv_ref[0, j : j + 1, lanes]
+            sums.append(jnp.sum(moved * own, axis=0, keepdims=True))
+        grad_proj_ref[0, :, lanes] = result.astype(jnp.bfloat16)
+        for j in range(4):
+            grad_conv_ref[0, j : j + 1, lanes] += sums[j]
+
+    for head in range(heads):
+        lanes = slice(2 * head * TILE, 2 * (head + 1) * TILE)
+        gate_lanes = slice((4 * heads + 2 * head) * TILE, (4 * heads + 2 * (head + 1)) * TILE)
+        rows = rows_ref[0, :, lanes]
+        gate = proj_ref[0, :, gate_lanes]
+        grad = grad_ref[:, lanes]
+        scale = lax.rsqrt(jnp.mean(rows * rows, axis=1, keepdims=True) + 1e-06)
+        level = rows * scale
+        sigmoid = jax.nn.sigmoid(gate)
+        through = grad * (gate * sigmoid)
+        gain_sum = gain_sum + jnp.sum(through * level, axis=0, keepdims=True)
+        grad_proj_ref[0, :, gate_lanes] = (
+            grad * level * gain * (sigmoid * (1.0 + gate * (1.0 - sigmoid)))
+        ).astype(jnp.bfloat16)
+        through = through * gain
+        grad_rows = scale * (
+            through - level * jnp.mean(through * level, axis=1, keepdims=True)
+        )
+
+        query_act, query_slope = activation(head)
+        query_scale = lax.rsqrt(jnp.sum(query_act * query_act, axis=1, keepdims=True) + 1e-06)
+        query_unit = query_act * query_scale
+        query = query_unit * TILE ** (-0.5)
+        key_act, key_slope = activation(heads + head)
+        key_scale = lax.rsqrt(jnp.sum(key_act * key_act, axis=1, keepdims=True) + 1e-06)
+        key = key_act * key_scale
+        value_parts = [activation(2 * heads + 2 * head), activation(2 * heads + 2 * head + 1)]
+        value = jnp.concatenate([value_parts[0][0], value_parts[1][0]], axis=1)
+
+        spread = total[:, head : head + 1] - total_rows[head : head + 1, :]
+        weights = jnp.exp(jnp.where(visible, spread, -1e30))
+        beta = beta_tile[:, heads + head : heads + head + 1]
+        carried = carry[:, head : head + 1]
+        key_low, query_low = key.astype(jnp.bfloat16), query.astype(jnp.bfloat16)
+        both = jnp.concatenate([key_low, query_low], axis=0)
+        grams = mm_nt(both, key_low)
+        state_low = state_in_ref[0, 0, head]
+        inverse = inverse_ref[0, 0, head]
+        pseudo = pseudo_ref[0, :, lanes]
+        grad_state = grad_state_ref[head]
+        grad_state_low = grad_state.astype(jnp.bfloat16)
+        last_row = weights[TILE - 1 : TILE, :]
+        last_col = jnp.sum(jnp.where(row == col, last_row, 0.0), axis=1, keepdims=True)
+        grad_rows_low = grad_rows.astype(jnp.bfloat16)
+        grad_pseudo = mm_tn(grams[TILE:] * weights, grad_rows_low) + mm(
+            last_col * key, grad_state_low
+        )
+        solved = mm_tn(inverse, grad_pseudo)
+        crossed = mm_nt(
+            jnp.concatenate([grad_rows_low, solved.astype(jnp.bfloat16)], axis=0), pseudo
+        )
+        grad_scores = crossed[:TILE] * weights
+        below = jnp.where(row > col, crossed[TILE:] * weights, 0.0)
+        grad_gram = (-beta) * below
+        grad_value = beta * solved
+        from_state = mm(key_low, state_low)
+        grad_beta_col = jnp.sum(
+            solved * (value - carried * from_state), axis=1, keepdims=True
+        ) - jnp.sum(below * grams[:TILE], axis=1, keepdims=True)
+        out_part = (carried * grad_rows).astype(jnp.bfloat16)
+        key_part = ((-carried) * grad_value).astype(jnp.bfloat16)
+        stacked = jnp.concatenate([out_part, key_part], axis=0)
+        to_inputs = mm_nt(stacked, state_low)
+        scores_low, gram_low = grad_scores.astype(jnp.bfloat16), grad_gram.astype(jnp.bfloat16)
+        grad_query = mm(scores_low, key_low) + to_inputs[:TILE]
+        key_own = mm(gram_low, key_low) + to_inputs[TILE:]
+        key_rest = mm_tn(
+            jnp.concatenate([gram_low, scores_low], axis=0), both
+        )
+        key_state = last_col * mm_nt(pseudo, grad_state_low)
+        grad_key = key_own + key_rest + key_state
+        grad_state_ref[head] = carried[TILE - 1 : TILE, :] * grad_state + mm_tn(
+            jnp.concatenate([query_low, key_low], axis=0), stacked
+        )
+        key_exact, query_exact = key_low.astype(jnp.float32), query_low.astype(jnp.float32)
+        state_dot = jnp.sum(key_state * key_exact, axis=1, keepdims=True)
+        tail = jnp.sum(state_dot, axis=0, keepdims=True) + carried[TILE - 1 : TILE, :] * jnp.sum(
+            jnp.sum(grad_state * state_low.astype(jnp.float32), axis=1, keepdims=True),
+            axis=0,
+            keepdims=True,
+        )
+        grad_total_col = (
+            jnp.sum(
+                grad_query * query_exact + (key_own - key_rest) * key_exact, axis=1, keepdims=True
+            )
+            - state_dot
+            + jnp.where(row[:, 0:1] == TILE - 1, tail, 0.0)
+        )
+        grad_total = jnp.where(col == head, grad_total_col, grad_total)
+        grad_beta = jnp.where(col == heads + head, grad_beta_col, grad_beta)
+
+        grad_query = grad_query * TILE ** (-0.5)
+        close_block(
+            head,
+            query_scale
+            * (
+                grad_query
+                - query_unit * jnp.sum(grad_query * query_unit, axis=1, keepdims=True)
+            )
+            * query_slope,
+        )
+        close_block(
+            heads + head,
+            key_scale
+            * (grad_key - key * jnp.sum(grad_key * key, axis=1, keepdims=True))
+            * key_slope,
+        )
+        close_block(2 * heads + 2 * head, grad_value[:, :TILE] * value_parts[0][1])
+        close_block(2 * heads + 2 * head + 1, grad_value[:, TILE:] * value_parts[1][1])
+
+    grad_log = ones_mm((row <= col).astype(jnp.float32), grad_total)
+    grad_raw = -rate * grad_log * jax.nn.sigmoid(shifted)
+    grad_rates_ref[0, 0:1, :] += -jnp.sum(grad_log * soft, axis=0, keepdims=True)
+    grad_rates_ref[0, 1:2, :] += jnp.sum(grad_raw, axis=0, keepdims=True)
+    grad_gain_ref[0, 0:1, :] += gain_sum
+    grad_proj_ref[0, :, 6 * heads * TILE : 6 * heads * TILE + TILE] = jnp.where(
+        col < heads, grad_raw, grad_beta * beta_tile * (1.0 - beta_tile)
+    ).astype(jnp.bfloat16)
+    for block in range(blocks):
+        later_ref[block, TILE : TILE + 8, :] = later_ref[block, 0:8, :]
+
+
+def mixer_specs(parts, rows, wide, heads, blocks, backward):
+    conv_cols, value_cols = 4 * heads * TILE, 2 * heads * TILE
+
+    def place(s, c):
+        return s * blocks + ((blocks - 1 - c) if backward else c)
+
+    return dict(
+        proj=pl.BlockSpec((1, TILE, wide), lambda p, s, c: (p, place(s, c), 0)),
+        info=pl.BlockSpec((TILE, TILE), lambda p, s, c: (place(s, c), 0)),
+        conv=pl.BlockSpec((1, 8, conv_cols), lambda p, s, c: (p, 0, 0)),
+        rates=pl.BlockSpec((1, 8, TILE), lambda p, s, c: (p, 0, 0)),
+        gain=pl.BlockSpec((1, 2 * TILE), lambda p, s, c: (0, 0)),
+        flat=pl.BlockSpec((TILE, value_cols), lambda p, s, c: (place(s, c), p)),
+        conv_out=pl.BlockSpec((1, TILE, conv_cols), lambda p, s, c: (p, place(s, c), 0)),
+        value=pl.BlockSpec((1, TILE, value_cols), lambda p, s, c: (p, place(s, c), 0)),
+        state=pl.BlockSpec(
+            (1, 1, heads, TILE, 2 * TILE), lambda p, s, c: (p, place(s, c), 0, 0, 0)
+        ),
+        inverse=pl.BlockSpec(
+            (1, 1, heads, TILE, TILE), lambda p, s, c: (p, place(s, c), 0, 0, 0)
+        ),
+        gain_sum=pl.BlockSpec((1, 8, 2 * TILE), lambda p, s, c: (p, 0, 0)),
+    )
+
+
+def mixer_forward(proj, info, conv, rates, gain, heads):
+    parts, rows, wide = proj.shape
+    blocks = LENGTH // TILE
+    spec = mixer_specs(parts, rows, wide, heads, blocks, False)
+    conv_cols, value_cols = 4 * heads * TILE, 2 * heads * TILE
+    low, full = jnp.bfloat16, jnp.float32
+    return pl.pallas_call(
+        functools.partial(forward_body, heads),
+        grid=(parts, rows // LENGTH, blocks),
+        in_specs=[spec[n] for n in ("proj", "info", "conv", "rates", "gain")],
+        out_specs=[
+            spec[n] for n in ("flat", "conv_out", "value", "state", "inverse", "value")
+        ],
+        out_shape=[
+            jax.ShapeDtypeStruct((rows, parts * value_cols), low),
+            jax.ShapeDtypeStruct((parts, rows, conv_cols), full),
+            jax.ShapeDtypeStruct((parts, rows, value_cols), full),
+            jax.ShapeDtypeStruct((parts, rows // TILE, heads, TILE, 2 * TILE), low),
+            jax.ShapeDtypeStruct((parts, rows // TILE, heads, TILE, TILE), low),
+            jax.ShapeDtypeStruct((parts, rows, value_cols), low),
+        ],
+        scratch_shapes=[
+            pltpu.VMEM((4 * heads, TILE + 8, TILE), full),
+            pltpu.VMEM((heads, TILE, 2 * TILE), full),
+        ],
+        compiler_params=pltpu.CompilerParams(
+            dimension_semantics=("arbitrary", "arbitrary", "arbitrary"),
+            vmem_limit_bytes=48 * 1024 * 1024,
+        ),
+        name="mixer_forward",
+    )(proj, info, conv, rates, gain)
+
+
+def mixer_backward(proj, info, conv, rates, gain, saved, grad, heads):
+    parts, rows, wide = proj.shape
+    blocks = LENGTH // TILE
+    spec = mixer_specs(parts, rows, wide, heads, blocks, True)
+    conv_cols = 4 * heads * TILE
+    low, full = jnp.bfloat16, jnp.float32
+    return pl.pallas_call(
+        functools.partial(backward_body, heads),
+        grid=(parts, rows // LENGTH, blocks),
+        in_specs=[
+            spec[n]
+            for n in (
+                "proj", "info", "conv", "rates", "gain",
+                "conv_out", "value", "state", "inverse", "value", "flat",
+            )
+        ],
+        out_specs=[spec[n] for n in ("proj", "conv", "rates", "gain_sum")],
+        out_shape=[
+            jax.ShapeDtypeStruct((parts, rows, wide), low),
+            jax.ShapeDtypeStruct((parts, 8, conv_cols), full),
+            jax.ShapeDtypeStruct((parts, 8, TILE), full),
+            jax.ShapeDtypeStruct((parts, 8, 2 * TILE), full),
+        ],
+        scratch_shapes=[
+            pltpu.VMEM((4 * heads, TILE + 8, TILE), full),
+            pltpu.VMEM((heads, TILE, 2 * TILE), full),
+        ],
+        compiler_params=pltpu.CompilerParams(
+            dimension_semantics=("arbitrary", "arbitrary", "arbitrary"),
+            vmem_limit_bytes=48 * 1024 * 1024,
+        ),
+        name="mixer_backward",
+    )(proj, info, conv, rates, gain, *saved, grad)
+
+
+def token_info(seg):
+    sequences, length = seg.shape
+    lanes = []
+    for j in range(1, 4):
+        lanes.append(jnp.pad(seg[:, j:] == seg[:, :-j], ((0, 0), (j, 0))))
+    ends = seg.reshape(sequences, length // TILE, TILE)
+    before = jnp.pad(ends[:, :-1, -1], ((0, 0), (1, 0)), constant_values=-1)
+    lanes.append((ends == before[:, :, None]).reshape(sequences, length))
+    lanes.append(seg)
+    for j in range(1, 4):
+        lanes.append(jnp.pad(seg[:, j:] == seg[:, :-j], ((0, 0), (0, j))))
+    table = jnp.stack([item.astype(jnp.float32).reshape(-1) for item in lanes], axis=1)
+    return jnp.pad(table, ((0, 0), (0, TILE - table.shape[1])))
+
+
 def gather_all(local):
     rows = lax.all_gather(local, ("tensor", "dp"), axis=0, tiled=True)
     shares = lax.axis_size("tensor")
@@ -447,38 +909,27 @@
     seg_rows = lax.dynamic_slice_in_dim(segment, tensor_index * own_rows, own_rows, 0).reshape(
         sequences, LENGTH
     )
-    projected = [
-        columns(jnp.dot(normed, proj_all[part], preferred_element_type=jnp.float32), proj_sizes)
-        for part in range(shares)
-    ]
-    pre = [
-        jnp.concatenate([projected[part][item] for part in range(shares)], axis=1)
-        for item in range(6)
-    ]
-
-    def mixer_local(
-        q_pre, k_pre, v_pre, g_pre, a_pre, b_pre, conv_q, conv_k, conv_v, rate, bias, out_gain
-    ):
-        shaped = [
-            item.reshape(sequences, LENGTH, item.shape[1])
-            for item in (q_pre, k_pre, v_pre, g_pre, a_pre, b_pre)
+    proj = jnp.stack(
+        [
+            jnp.dot(normed, proj_all[part], preferred_element_type=jnp.float32)
+            for part in range(shares)
         ]
-        mixed_rows = jax.vmap(
-            mixer_sequence, in_axes=(0, 0, 0, 0, 0, 0, 0, None, None, None, None, None, None)
-        )(*shaped, seg_rows, conv_q, conv_k, conv_v, rate, bias, out_gain)
-        return mixed_rows.reshape(own_rows, mixed_rows.shape[2])
-
-    mixed, mixer_pull = jax.vjp(
-        mixer_local,
-        *pre,
-        conv_query,
-        conv_key,
-        conv_value,
-        decay_scale,
-        decay_bias,
-        out_norm_gain
-    )
-    mixed_low = mixed.astype(low)
+    )
+    heads = w_decay.shape[1]
+    info = token_info(seg_rows)
+
+    def by_part(item):
+        return item.reshape(item.shape[0], shares, item.shape[1] // shares).transpose(1, 0, 2)
+
+    conv = jnp.pad(
+        jnp.concatenate([by_part(c) for c in (conv_query, conv_key, conv_value)], axis=2),
+        ((0, 0), (0, 4), (0, 0)),
+    )
+    rates = jnp.pad(
+        by_part(jnp.stack([decay_scale, decay_bias])), ((0, 0), (0, 6), (0, TILE - heads))
+    )
+    gain = out_norm_gain.reshape(1, -1)
+    mixed_low, *saved = mixer_forward(proj, info, conv, rates, gain, heads)
     value_cols = w_value.shape[1]
     residual = input_float
     for part in range(shares):
@@ -550,25 +1001,32 @@
         ]
     )
     own_out, own_gate, own_up, own_down = columns(scatter_all(rest_grads), rest_sizes)
-    mixer_grads = mixer_pull(grad_mixed)
+    grad_proj, grad_conv, grad_rates, grad_gain = mixer_backward(
+        proj, info, conv, rates, gain, saved, grad_mixed, heads
+    )
     grad_normed = jnp.zeros_like(residual)
     proj_grads = []
     for part in range(shares):
-        grad_part = jnp.concatenate(
-            [
-                item[:, part * size : (part + 1) * size].astype(low)
-                for item, size in zip(mixer_grads[:6], proj_sizes)
-            ]
-            + [jnp.zeros((own_rows, padded - used), low)],
-            axis=1,
-        )
-        grad_normed = grad_normed + contract_cols(grad_part, proj_all[part])
-        proj_grads.append(contract_rows(normed, grad_part).astype(low))
+        grad_normed = grad_normed + contract_cols(grad_proj[part], proj_all[part])
+        proj_grads.append(contract_rows(normed, grad_proj[part]).astype(low))
+
+    def from_part(item):
+        return item.transpose(1, 0, 2).reshape(item.shape[1], -1)
+
+    query_cols = w_query.shape[1]
+    mixer_grads = [
+        from_part(item)
+        for item in columns(grad_conv[:, :4], (query_cols, query_cols, value_cols))
+    ] + [
+        grad_rates[:, 0, :heads].reshape(-1),
+        grad_rates[:, 1, :heads].reshape(-1),
+        jnp.sum(grad_gain[:, 0], axis=0),
+    ]
     own_proj = columns(scatter_all(jnp.stack(proj_grads)), proj_sizes)
     grad_input_norm, grad_gain_one = norm1_pull(grad_normed)
     grad_input = grad_residual + grad_input_norm
     summed = lax.psum(
-        (grad_gain_one, grad_gain_two) + tuple(mixer_grads[6:12]) + (loss_sum,), ("dp", "tensor")
+        (grad_gain_one, grad_gain_two) + tuple(mixer_grads) + (loss_sum,), ("dp", "tensor")
     )
     loss = summed[8] / (count * width)
     return (

time: 2680 us -> 910 us (0.34)
  matrix products: 1210 us -> 217 us
  local copies, waits for them, and re-layouts: 605 us -> 40 us
  other arithmetic: 388 us -> 59.6 us
  Pallas kernels: 0 us -> 195 us
  loops' own time: 54 us -> 0 us
    dot_general x1056 -> x0, matrix products: 988 us -> none  [the longest x320 223 us: lower_inverse(): jnp.einsum('hij,hjk->hik', inverse, power, precision=exact_precision)]
    pallas_call x0 -> x2, Pallas kernels: none -> 195 us  [the longest x1 124 us: mixer_forward(): pl.pallas_call(functools.partial(forward_body, heads), grid=(parts, rows...]
    squeeze x96 -> x0, local copies, waits for them, and re-layouts: 108 us -> none  [mixer_sequence(): lax.scan(jax.checkpoint(block_update), state, carried_in)]
    mul x126 -> x0, other arithmetic: 98.1 us -> none  [the longest x7 31.1 us: short_conv(): result = result + shifted * masks[offset][:, None] * kernel[offset]]
    reduce_sum x40 -> x1, other arithmetic: 80.4 us -> 0.02 us  [on_device_whole(): jnp.sum(grad_gain[:, 0], axis=0)]
    dynamic_update_slice x80 -> x0, local copies, waits for them, and re-layouts: 77.7 us -> none  [mixer_sequence(): lax.scan(jax.checkpoint(block_update), state, carried_in)]
    while x994 -> x0, local copies, waits for them, and re-layouts: 66.7 us -> none
    unnamed x323 -> x85, local copies, waits for them, and re-layouts: 89.7 us -> 28.6 us
  transfers between devices with their start and end apart: 4 -> 4, of which waited for: 3 -> 3; matrix products, arithmetic and copies ran while one was open for 25% -> 17% of each run, Pallas kernels for 0% -> 14%
where the time goes in v2:
time: 910 us; the launch traced here: 897 us
  waiting for transfers between devices  282 us (31%)
  matrix products  217 us (24%)
  Pallas kernels  195 us (21%)
  blocking collectives  85.8 us (9%)
  other arithmetic  59.6 us (7%)
  local copies, waits for them, and re-layouts  40 us (4%)
  between operations  17.8 us (2%)
    reduce_scatter x1, waiting for transfers between devices, scatter_all(): lax.psum_scatter(parts.reshape(shares * rows, cols), ('tensor', 'dp'), sc...  234 us
    pallas_call x1, Pallas kernels, mixer_forward(): pl.pallas_call(functools.partial(forward_body, heads), grid=(parts, rows...  124 us
    dot_general x10, matrix products, contract_cols(): lax.dot_general(left, right, (((1,), (1,)), ((), ())), preferred_element_...  75.2 us
    pallas_call x1, Pallas kernels, mixer_backward(): pl.pallas_call(functools.partial(backward_body, heads), grid=(parts, rows...  71.8 us
    dot_general x10, matrix products, contract_rows(): lax.dot_general(left, right, (((0,), (0,)), ((), ())), preferred_element_...  54.4 us
    psum x1, blocking collectives, on_device_whole(): lax.psum((grad_gain_one, grad_gain_two) + tuple(mixer_grads) + (loss_sum,...  44 us
    psum x1, blocking collectives, on_device_whole(): count = lax.psum(jnp.sum(live), ('dp', 'tensor'))  41.8 us
    all_gather x2, waiting for transfers between devices, gather_all(): rows = lax.all_gather(local, ('tensor', 'dp'), axis=0, tiled=True)  41.7 us
  transfers between devices with their start and end apart: 4, of which 3 were waited for; matrix products, arithmetic and copies ran while one was open for 17% of the time, Pallas kernels for 14%

profile of v2, /device:TPU:8, one launch (start us, length us, event | category | flops | bytes accessed | tf_op | source)
XLA Modules:
  0.0 897.1 jit_solution(7886056393130922382)
XLA Ops:
  14.2 41.8 %psum.71 = f32[]{:T(128)} all-reduce(f32[]{:T(128)} %convert_reduce_fusion), channel_id=1, replica_groups=mesh['dp'=16,'tensor'=2] {'dp','tensor'}, use_global_device_ids=true, to_apply=%region_5.6 | all-reduce | flops 1 | bytes 8 | tf_op jit(solution)/shard_map/psum | solution.py:905
  69.5 41.6 %all-gather.3.cloned.1.call-done = bf16[2048,3200]{1,0:T(8,128)(2,1)} async-done(((bf16[64,3200]{1,0:T(8,128)(2,1)}), bf16[2048,3200]{1,0:T(8,128)(2,1)}) %all-gather.3.cloned.1.call-update) | async-done | bytes 13107216 | tf_op jit(solution)/shard_map/all_gather | solution.py:844
  111.1 10.4 %convolution_bitcast_fusion = f32[1,1024,3200]{2,1,0:T(8,128)S(1)} fusion(bf16[2048,3200]{1,0:T(8,128)(2,1)} %all-gather.3.cloned.1.call-done, bf16[1024,1024]{0,1:T(8,128)(2,1)S(1)} %copy.134, f32[1024]{0:T(1024)S(1)} %copy-done.21, f32[1024]{0:T(1024)S(1)} %fusion.61), kind=kOutput, calls=%fused_computation.5 | convolution fusion | flops 6715080704 | bytes 21766144 | tf_op jit(solution)/shard_map/dot_general | solution.py:914
  121.5 13.8 %convolution_bitcast_fusion.1 = f32[1,1024,3200]{2,1,0:T(8,128)} fusion(bf16[2048,3200]{1,0:T(8,128)(2,1)} %all-gather.3.cloned.1.call-done, bf16[1024,1024]{0,1:T(8,128)(2,1)S(1)} %copy.134, f32[1024]{0:T(1024)S(1)} %copy-done.21, f32[1024]{0:T(1024)S(1)} %fusion.61), kind=kOutput, calls=%fused_computation.6 | convolution fusion | flops 6715080704 | bytes 21766144 | tf_op jit(solution)/shard_map/dot_general | solution.py:914
  135.3 14.5 %pad_maximum_fusion.proj_ref = f32[2,1024,3200]{2,1,0:T(8,128)} fusion(f32[1,1024,3200]{2,1,0:T(8,128)S(1)} %convolution_bitcast_fusion, f32[1,1024,3200]{2,1,0:T(8,128)} %convolution_bitcast_fusion.1), kind=kLoop, calls=%fused_computation | loop fusion | flops 6553600 | bytes 52428800 | tf_op jit(solution)/shard_map/stack | solution.py:912
  149.8 123.5 %mixer_forward.1 = (bf16[1024,2048]{1,0:T(8,128)(2,1)}, f32[2,1024,2048]{2,1,0:T(8,128)}, f32[2,1024,1024]{2,1,0:T(8,128)}, bf16[2,8,4,128,256]{4,3,2,1,0:T(8,12...) custom-call(f32[2,1024,3200]{2,1,0:T(8,128)} %pad_maximum_fusion.proj_ref, ...), custom_call_target="tpu_custom_call" | custom-call | tf_op jit(solution)/shard_map/mixer_forward/pallas_call | solution.py:766
  282.8 6.1 fusion.38
  288.9 7.5 fusion.32
  296.4 8.3 multiply_convert_fusion.5
  311.6 8.6 multiply_convert_fusion.4
  320.2 6.5 fusion.30
  326.8 12.5 %multiply_convert_fusion = (bf16[1024,1408]{1,0:T(8,128)(2,1)}, bf16[1024,1408]{1,0:T(8,128)(2,1)S(1)}) fusion(f32[1024,1408]{1,0:T(8,128)} %copy-done.25, f32[1024,1408]{1,0:T(8,128)} %get-tuple-element.171, bf16[1024,1024]{0,1:T(8,128)(2,1)S(1)} %get-tuple-element.172, bf16[2,1024,5248]{2,1,0:T(8,128)(2,1)} %bitcast.183), kind=kOutput, calls=%fused_computation.35 | convolution fusion | flops 2971533312 | bytes 22282240 | tf_op jit(solution)/shard_map/dot_general | solution.py:957
  339.2 11.0 %multiply_convert_fusion.2 = (bf16[1024,1408]{1,0:T(8,128)(2,1)}, bf16[1024,1408]{1,0:T(8,128)(2,1)}) fusion(f32[1024,1408]{1,0:T(8,128)S(1)} %fusion.32, f32[1024,1408]{1,0:T(8,128)} %get-tuple-element.169, bf16[1024,1024]{0,1:T(8,128)(2,1)S(1)} %get-tuple-element.172, bf16[2,1024,5248]{2,1,0:T(8,128)(2,1)} %bitcast.184), kind=kOutput, calls=%fused_computation.37 | convolution fusion | flops 2971533312 | bytes 22282240 | tf_op jit(solution)/shard_map/dot_general | solution.py:957
  350.3 5.4 fusion.37
  355.7 7.0 fusion.31
  362.8 6.9 fusion.33
  369.6 10.1 %multiply_reduce_fusion = (f32[1024]{0:T(1024)}, f32[1024]{0:T(1024)S(1)}, f32[1024,1024]{0,1:T(8,128)S(1)}) fusion(f32[1024,1024]{0,1:T(8,128)S(1)} %get-tuple-element.167, f32[1024]{0:T(1024)S(1)} %fusion.62, f32[1024]{0:T(1024)S(1)} %copy-done.15, bf16[1024,1408]{1,0:T(8,128)(2,1)} %get-tuple-element.144, bf16[2,1024,5248]{2,1,0:T(8,128)(2,1)} %bitcast.188, ...), kind=kOutput, calls=%fused_computation.53 | convolution fusion | flops 2962225152 | bytes 26755072 | tf_op jit(solution)/shard_map/dot_general | solution.py:141
  397.5 71.8 %mixer_backward.1 = (bf16[2,1024,3200]{2,1,0:T(8,128)(2,1)}, f32[2,8,2048]{2,1,0:T(8,128)S(1)}, f32[2,8,128]{2,1,0:T(8,128)S(1)}, f32[2,8,256]{2,1,0:T(8,128)S(1)}) custom-call(f32[2,1024,3200]{2,1,0:T(8,128)} %pad_maximum_fusion.proj_ref, f32[1024,128]{1,0:T(8,128)S(1)} %pad.50.info_ref, f32[2,8,2048]{2,1,0:T(8,128)S(1)} %select_maximum_fusion.conv_ref, ...), custom_call_target="tpu_custom_call" | custom-call | tf_op jit(solution)/shard_map/mixer_backward/pallas_call | solution.py:799
  469.4 10.5 %fusion.6 = bf16[1,1024,3200]{2,1,0:T(8,128)(2,1)S(1)} fusion(bf16[2,1024,3200]{2,1,0:T(8,128)(2,1)} %get-tuple-element.37, bf16[1024,1024]{0,1:T(8,128)(2,1)S(1)} %copy-done.4, f32[1024]{0:T(1024)S(1)} %copy-done.22, f32[1024]{0:T(1024)S(1)} %copy-done.19), kind=kOutput, calls=%fused_computation.21 | convolution fusion | flops 6718357504 | bytes 15212544 | tf_op jit(solution)/shard_map/dot_general | solution.py:135
  479.9 10.7 %fusion.9 = bf16[1,1024,3200]{2,1,0:T(8,128)(2,1)S(1)} fusion(bf16[2,1024,3200]{2,1,0:T(8,128)(2,1)} %get-tuple-element.37, bf16[1024,1024]{0,1:T(8,128)(2,1)S(1)} %copy-done.4, f32[1024]{0:T(1024)S(1)} %copy-done.22, f32[1024]{0:T(1024)S(1)} %copy-done.19), kind=kOutput, calls=%fused_computation.22 | convolution fusion | flops 6718357504 | bytes 15212544 | tf_op jit(solution)/shard_map/dot_general | solution.py:135
  490.6 7.3 pad_maximum_fusion.2
  499.5 5.3 convolution_convert_fusion.9
  507.7 6.1 convolution_convert_fusion.8
  543.0 9.0 %pad_maximum_fusion.1 = bf16[2,1024,5248]{2,1,0:T(8,128)(2,1)} fusion(bf16[1,1024,5248]{2,1,0:T(8,128)(2,1)S(1)} %maximum_bitcast_fusion.1, bf16[1,1024,5248]{2,1,0:T(8,128)(2,1)S(1)} %maximum_bitcast_fusion), kind=kLoop, calls=%fused_computation.1 | loop fusion | flops 10747904 | bytes 42991616 | tf_op jit(solution)/shard_map/stack | solution.py:985
  553.0 11.7 %fusion.1 = f32[1024,1024]{0,1:T(8,128)S(1)} fusion(bf16[2048,3200]{1,0:T(8,128)(2,1)} %all-gather.3.cloned.1.call-done, bf16[2,1024,3200]{2,1,0:T(8,128)(2,1)} %get-tuple-element.37), kind=kOutput, calls=%fused_computation.16 | convolution fusion | flops 6710886400 | bytes 17301504 | tf_op jit(solution)/shard_map/dot_general | solution.py:141
  564.7 13.4 %fusion.23 = (f32[1024]{0:T(1024)S(1)}, f32[1024]{0:T(1024)S(1)}, f32[1024,1024]{0,1:T(8,128)}) fusion(bf16[1024,1024]{0,1:T(8,128)(2,1)S(1)} %copy-done.5, f32[1024]{0:T(1024)S(1)} %copy-done.19, f32[1024]{0:T(1024)S(1)} %copy-done.22, f32[1024,1024]{0,1:T(8,128)S(1)} %fusion.1, bf16[2048,3200]{1,0:T(8,128)(2,1)} %all-gather.3.cloned.1.call-done, ...), kind=kOutput, calls=%fused_computation.46 | convolution fusion | flops 6719272960 | bytes 23609344 | tf_op jit(solution)/shard_map/dot_general | solution.py:141
  578.1 44.0 %all-reduce.12 = (f32[]{:T(128)}, f32[1024]{0:T(1024)}, f32[4,1024]{1,0:T(4,128)}, f32[4,1024]{1,0:T(4,128)}, f32[4,2048]{1,0:T(4,128)}, /*index=5*/f32[8]{0:T(128)}, f32[8]{0:T(128)}, f32[256]{0:T(256)}, f32[1024]{0:T(1024)}) all-reduce(f32[]{:T(128)} %get-tuple-element.148, ...), channel_id=1, replica_groups=mesh['dp'=16,'tensor'=2] {'dp','tensor'}, use_global_device_ids=true, to_apply=%region_3.4 | all-reduce | flops 18705 | bytes 149640 | tf_op jit(solution)/shard_map/psum | solution.py:1028
  622.1 5.4 copy.154
  627.5 6.6 fusion.26
  634.1 5.4 copy.155
  640.1 5.6 reduce-scatter.7.cloned.1.call-done
  651.1 234.3 %reduce-scatter.5.cloned.1.call-done = bf16[64,5248]{1,0:T(8,128)(2,1)} async-done(((bf16[2048,5248]{1,0:T(8,128)(2,1)}), bf16[64,5248]{1,0:T(8,128)(2,1)}) %reduce-scatter.5.cloned.1.call-update) | async-done | bytes 671760 | tf_op jit(solution)/shard_map/reduce_scatter | solution.py:851
  (148 shorter events, 96.5 us)
Async XLA Ops:
  7.2 103.9 %all-gather.3.cloned.1.call-start = ((), (), s32[]{:S(2)}) async-start(), calls=%async_computation.2 | async-start | bytes 13516800 | tf_op jit(solution)/shard_map/all_gather | solution.py:844
  10.7 262.6 %all-gather.5.cloned.1.call-start = ((), (), s32[]{:S(2)}) async-start(), calls=%async_computation.3 | async-start | bytes 22167552 | tf_op jit(solution)/shard_map/all_gather | solution.py:844
  12.9 632.8 %reduce-scatter.7.cloned.1.call-start = ((), (), s32[]{:S(2)}) async-start(), calls=%async_computation.5 | async-start | bytes 13516800
  62.9 58.6 %copy-start.2 = (bf16[1024,1024]{0,1:T(8,128)(2,1)}, bf16[1024,1024]{0,1:T(8,128)(2,1)S(1)}, u32[]{:S(2)}) copy-start(bf16[1024,1024]{0,1:T(8,128)(2,1)S(1)} %copy.134) | copy-start | bytes 6291460
  62.9 6.5 copy-start.14
  62.9 6.5 copy-start.16
  62.9 6.5 copy-start.17
  62.9 48.2 %copy-start.21 = (f32[1024]{0:T(1024)S(1)}, f32[1024]{0:T(1024)}, u32[]{:S(2)}) copy-start(f32[1024]{0:T(1024)} %param.26) | copy-start | bytes 12292
  68.9 52.6 %copy-start.18 = (f32[1024]{0:T(1024)}, f32[1024]{0:T(1024)S(1)}, u32[]{:S(2)}) copy-start(f32[1024]{0:T(1024)S(1)} %fusion.61) | copy-start | bytes 12292
  135.3 14.5 %copy-start = (f32[256]{0:T(256)S(1)}, f32[256]{0:T(256)}, u32[]{:S(2)}) copy-start(f32[256]{0:T(256)} %param.38) | copy-start | bytes 3076
  273.4 4.8 copy-start.3
  273.4 4.8 copy-start.23
  278.1 4.2 copy-start.15
  282.8 28.8 %copy-start.10 = (bf16[1024,1024]{0,1:T(8,128)(2,1)}, bf16[1024,1024]{0,1:T(8,128)(2,1)S(1)}, u32[]{:S(2)}) copy-start(bf16[1024,1024]{0,1:T(8,128)(2,1)S(1)} %multiply_convert_fusion.6) | copy-start | bytes 6291460
  288.9 22.7 %copy-start.25 = (f32[1024,1408]{1,0:T(8,128)}, f32[1024,1408]{1,0:T(8,128)S(1)}, u32[]{:S(2)}) copy-start(f32[1024,1408]{1,0:T(8,128)S(1)} %fusion.38) | copy-start | bytes 17301508
  311.6 8.6 copy-start.7
  326.8 12.5 %copy-start.27 = (bf16[1024,1024]{0,1:T(8,128)(2,1)}, bf16[1024,1024]{0,1:T(8,128)(2,1)S(1)}, u32[]{:S(2)}) copy-start(bf16[1024,1024]{0,1:T(8,128)(2,1)S(1)} %get-tuple-element.172) | copy-start | bytes 6291460
  326.8 53.0 %copy-start.6 = (f32[1024,1024]{0,1:T(8,128)}, f32[1024,1024]{0,1:T(8,128)S(1)}, u32[]{:S(2)}) copy-start(f32[1024,1024]{0,1:T(8,128)S(1)} %get-tuple-element.173) | copy-start | bytes 12582916
  339.2 11.1 %copy-start.31 = (bf16[1024,1408]{1,0:T(8,128)(2,1)}, bf16[1024,1408]{1,0:T(8,128)(2,1)S(1)}, u32[]{:S(2)}) copy-start(bf16[1024,1408]{1,0:T(8,128)(2,1)S(1)} %get-tuple-element.145) | copy-start | bytes 8650756
  350.3 5.4 copy-start.33
  355.7 7.0 copy-start.35
  384.7 4.8 copy-start.8
  393.6 3.9 copy-start.1
  397.5 71.9 %copy-start.4 = (bf16[1024,1024]{0,1:T(8,128)(2,1)S(1)}, bf16[1024,1024]{0,1:T(8,128)(2,1)}, u32[]{:S(2)}) copy-start(bf16[1024,1024]{0,1:T(8,128)(2,1)} %copy-done.2) | copy-start | bytes 6291460
  397.5 71.9 %copy-start.19 = (f32[1024]{0:T(1024)S(1)}, f32[1024]{0:T(1024)}, u32[]{:S(2)}) copy-start(f32[1024]{0:T(1024)} %copy-done.18) | copy-start | bytes 12292
  397.5 71.9 %copy-start.22 = (f32[1024]{0:T(1024)S(1)}, f32[1024]{0:T(1024)}, u32[]{:S(2)}) copy-start(f32[1024]{0:T(1024)} %param.26) | copy-start | bytes 12292
  497.9 387.5 %reduce-scatter.5.cloned.1.call-start = ((), (), s32[]{:S(2)}) async-start(), calls=%async_computation.4 | async-start | bytes 22167552 | tf_op jit(solution)/shard_map/reduce_scatter | solution.py:851
  507.7 6.1 copy-start.26
  507.7 6.1 copy-start.28
  553.0 11.7 %copy-start.5 = (bf16[1024,1024]{0,1:T(8,128)(2,1)S(1)}, bf16[1024,1024]{0,1:T(8,128)(2,1)}, u32[]{:S(2)}) copy-start(bf16[1024,1024]{0,1:T(8,128)(2,1)} %copy-done.2) | copy-start | bytes 6291460
  564.7 13.4 %copy-start.20 = (f32[1024]{0:T(1024)S(1)}, f32[1024]{0:T(1024)}, u32[]{:S(2)}) copy-start(f32[1024]{0:T(1024)} %get-tuple-element.125) | copy-start | bytes 12292
  622.1 5.4 copy-start.13
  (9 other events, 25.8 us)
Sparse Core Ops, SparseCore 0:
  11.4 99.6 all-gather.2
  114.0 134.3 all-gather.4
  498.1 147.5 reduce-scatter.6
  648.0 237.4 reduce-scatter.4

commit v3 on v2

--- a/solution.py
+++ b/solution.py
@@ -1,4 +1,5 @@
 import functools
+from types import SimpleNamespace
 
 import jax
 import jax.numpy as jnp
@@ -11,6 +12,7 @@
 LENGTH = 1024
 
 
+DP, TP = "dp", "tensor"
 exact_precision = lax.Precision.HIGHEST
 
 
@@ -176,21 +178,21 @@
     own_rows, width = layer_input.shape
     group_rows = segment.shape[0]
     sequences = group_rows // LENGTH
-    tensor_index = lax.axis_index("tensor")
+    tensor_index = lax.axis_index(TP)
     heads_local = w_decay.shape[1]
     query_cols = w_query.shape[1]
     value_cols = w_value.shape[1]
     input_float = layer_input.astype(jnp.float32)
     normed_own, norm1_pull = jax.vjp(rms_scale, input_float, norm1_gain)
-    normed = lax.all_gather(normed_own.astype(jnp.bfloat16), "tensor", axis=0, tiled=True)
+    normed = lax.all_gather(normed_own.astype(jnp.bfloat16), TP, axis=0, tiled=True)
     full_query, full_key, full_value, full_gate, full_decay, full_beta, full_out = (
-        lax.all_gather(w_query, "dp", axis=0, tiled=True),
-        lax.all_gather(w_key, "dp", axis=0, tiled=True),
-        lax.all_gather(w_value, "dp", axis=0, tiled=True),
-        lax.all_gather(w_gate_out, "dp", axis=0, tiled=True),
-        lax.all_gather(w_decay, "dp", axis=0, tiled=True),
-        lax.all_gather(w_beta, "dp", axis=0, tiled=True),
-        lax.all_gather(w_out, "dp", axis=0, tiled=True),
+        lax.all_gather(w_query, DP, axis=0, tiled=True),
+        lax.all_gather(w_key, DP, axis=0, tiled=True),
+        lax.all_gather(w_value, DP, axis=0, tiled=True),
+        lax.all_gather(w_gate_out, DP, axis=0, tiled=True),
+        lax.all_gather(w_decay, DP, axis=0, tiled=True),
+        lax.all_gather(w_beta, DP, axis=0, tiled=True),
+        lax.all_gather(w_out, DP, axis=0, tiled=True),
     )
     proj_weights = (full_query, full_key, full_value, full_gate, full_decay, full_beta)
     projected = [
@@ -238,21 +240,21 @@
     )
     mixed_low = mixed.astype(jnp.bfloat16)
     attention = lax.psum_scatter(
-        contract_cols(mixed_low, full_out), "tensor", scatter_dimension=0, tiled=True
+        contract_cols(mixed_low, full_out), TP, scatter_dimension=0, tiled=True
     )
     residual = input_float + attention
     normed2_own, norm2_pull = jax.vjp(rms_scale, residual, norm2_gain)
-    normed2 = lax.all_gather(normed2_own.astype(jnp.bfloat16), "tensor", axis=0, tiled=True)
+    normed2 = lax.all_gather(normed2_own.astype(jnp.bfloat16), TP, axis=0, tiled=True)
     ffn_gate_w, ffn_up_w, ffn_down_w = (
-        lax.all_gather(w_ffn_gate, "dp", axis=0, tiled=True),
-        lax.all_gather(w_ffn_up, "dp", axis=0, tiled=True),
-        lax.all_gather(w_ffn_down, "dp", axis=0, tiled=True),
+        lax.all_gather(w_ffn_gate, DP, axis=0, tiled=True),
+        lax.all_gather(w_ffn_up, DP, axis=0, tiled=True),
+        lax.all_gather(w_ffn_down, DP, axis=0, tiled=True),
     )
     gate_pre, up_pre = feed_inputs(normed2, ffn_gate_w, ffn_up_w)
     hidden = (jax.nn.silu(gate_pre) * up_pre).astype(jnp.bfloat16)
     ffn_out = lax.psum_scatter(
         contract_cols(hidden, ffn_down_w).astype(jnp.bfloat16),
-        "tensor",
+        TP,
         scatter_dimension=0,
         tiled=True,
     ).astype(jnp.float32)
@@ -260,12 +262,12 @@
     live = pad_mask.astype(jnp.float32)
     error = output - target.astype(jnp.float32)
     loss_sum, count = lax.psum(
-        (jnp.sum(live[:, None] * error * error), jnp.sum(live)), ("dp", "tensor")
+        (jnp.sum(live[:, None] * error * error), jnp.sum(live)), (DP, TP)
     )
     loss = loss_sum / (count * width)
-    all_tokens = own_rows * lax.axis_size("dp") * lax.axis_size("tensor")
+    all_tokens = own_rows * lax.axis_size(DP) * lax.axis_size(TP)
     grad_output = error * live[:, None] * (all_tokens / count)
-    grad_ffn = lax.all_gather(grad_output.astype(jnp.bfloat16), "tensor", axis=0, tiled=True)
+    grad_ffn = lax.all_gather(grad_output.astype(jnp.bfloat16), TP, axis=0, tiled=True)
     grad_hidden = jnp.dot(grad_ffn, ffn_down_w, preferred_element_type=jnp.float32)
     sigmoid_gate = jax.nn.sigmoid(gate_pre)
     grad_gate = (
@@ -277,12 +279,12 @@
     grad_up_local = contract_rows(normed2, grad_up)
     normed2_part = contract_cols(grad_gate, ffn_gate_w) + contract_cols(grad_up, ffn_up_w)
     grad_normed2 = lax.psum_scatter(
-        normed2_part.astype(jnp.bfloat16), "tensor", scatter_dimension=0, tiled=True
+        normed2_part.astype(jnp.bfloat16), TP, scatter_dimension=0, tiled=True
     ).astype(jnp.float32)
     grad_residual_norm, grad_gain_two = norm2_pull(grad_normed2)
     grad_residual = grad_output + grad_residual_norm
     grad_attention = lax.all_gather(
-        grad_residual.astype(jnp.bfloat16), "tensor", axis=0, tiled=True
+        grad_residual.astype(jnp.bfloat16), TP, axis=0, tiled=True
     )
     grad_mixed = jnp.dot(grad_attention, full_out, preferred_element_type=jnp.float32)
     grad_out_local = contract_rows(grad_attention, mixed_low)
@@ -293,40 +295,40 @@
         normed_part = normed_part + contract_cols(grad_item, weight)
     weight_locals = [contract_rows(normed, grad_item) for grad_item in pre_grads]
     grad_normed = lax.psum_scatter(
-        normed_part.astype(jnp.bfloat16), "tensor", scatter_dimension=0, tiled=True
+        normed_part.astype(jnp.bfloat16), TP, scatter_dimension=0, tiled=True
     ).astype(jnp.float32)
     grad_input_norm, grad_gain_one = norm1_pull(grad_normed)
     grad_input = grad_residual + grad_input_norm
     owned = (
         lax.psum_scatter(
-            grad_gate_local.astype(jnp.bfloat16), "dp", scatter_dimension=0, tiled=True
+            grad_gate_local.astype(jnp.bfloat16), DP, scatter_dimension=0, tiled=True
         ).astype(jnp.float32),
         lax.psum_scatter(
-            grad_up_local.astype(jnp.bfloat16), "dp", scatter_dimension=0, tiled=True
+            grad_up_local.astype(jnp.bfloat16), DP, scatter_dimension=0, tiled=True
         ).astype(jnp.float32),
         lax.psum_scatter(
-            grad_down_local.astype(jnp.bfloat16), "dp", scatter_dimension=0, tiled=True
+            grad_down_local.astype(jnp.bfloat16), DP, scatter_dimension=0, tiled=True
         ).astype(jnp.float32),
         lax.psum_scatter(
-            weight_locals[0].astype(jnp.bfloat16), "dp", scatter_dimension=0, tiled=True
+            weight_locals[0].astype(jnp.bfloat16), DP, scatter_dimension=0, tiled=True
         ).astype(jnp.float32),
         lax.psum_scatter(
-            weight_locals[1].astype(jnp.bfloat16), "dp", scatter_dimension=0, tiled=True
+            weight_locals[1].astype(jnp.bfloat16), DP, scatter_dimension=0, tiled=True
         ).astype(jnp.float32),
         lax.psum_scatter(
-            weight_locals[2].astype(jnp.bfloat16), "dp", scatter_dimension=0, tiled=True
+            weight_locals[2].astype(jnp.bfloat16), DP, scatter_dimension=0, tiled=True
         ).astype(jnp.float32),
         lax.psum_scatter(
-            weight_locals[3].astype(jnp.bfloat16), "dp", scatter_dimension=0, tiled=True
+            weight_locals[3].astype(jnp.bfloat16), DP, scatter_dimension=0, tiled=True
         ).astype(jnp.float32),
         lax.psum_scatter(
-            weight_locals[4].astype(jnp.bfloat16), "dp", scatter_dimension=0, tiled=True
+            weight_locals[4].astype(jnp.bfloat16), DP, scatter_dimension=0, tiled=True
         ).astype(jnp.float32),
         lax.psum_scatter(
-            weight_locals[5].astype(jnp.bfloat16), "dp", scatter_dimension=0, tiled=True
+            weight_locals[5].astype(jnp.bfloat16), DP, scatter_dimension=0, tiled=True
         ).astype(jnp.float32),
         lax.psum_scatter(
-            grad_out_local.astype(jnp.bfloat16), "dp", scatter_dimension=0, tiled=True
+            grad_out_local.astype(jnp.bfloat16), DP, scatter_dimension=0, tiled=True
         ).astype(jnp.float32),
     )
     conv_q_full = lax.dynamic_update_slice_in_dim(
@@ -355,7 +357,7 @@
             bias_full,
             mixer_grads[11],
         ),
-        ("dp", "tensor"),
+        (DP, TP),
     )
     return (
         output,
@@ -382,7 +384,11 @@
     )
 
 
+CORE, SIDE, TENSOR, PLACE = 1, 2, 3, 0
+TENSOR_FIRST = (CORE, TENSOR, SIDE, PLACE)
+SIDE_FIRST = (CORE, SIDE, TENSOR, PLACE)
 TILE = 128
+COST = 4 * 10**10
 
 
 def mm(left, right, dims=((1,), (0,))):
@@ -416,23 +422,29 @@
     return mm(ones, high) + (mm(ones, middle) + mm(ones, rest - middle.astype(jnp.float32)))
 
 
-def unit_lower_inverse(part, row, col):
-    size = part.shape[0]
+def unit_lower_inverses(parts, row, col):
+    size = parts[0].shape[0]
     eye = (row == col).astype(jnp.float32)
     block = 16
-    power = jnp.where((row // block) == (col // block), -part, 0.0)
-    inverse = eye + power
+    inside = (row // block) == (col // block)
+    powers = [jnp.where(inside, -part, 0.0) for part in parts]
+    inverses = [eye + power for power in powers]
     covered = 2
     while covered < block:
-        power = mm_fine(power, power)
-        inverse = inverse + mm_fine(inverse, power)
+        powers = [mm_fine(power, power) for power in powers]
+        moves = [mm_fine(inverse, power) for inverse, power in zip(inverses, powers)]
+        inverses = [inverse + move for inverse, move in zip(inverses, moves)]
         covered *= 2
     while block < size:
-        pair = (row // (2 * block)) == (col // (2 * block))
-        cross = jnp.where(pair & ((row // block) != (col // block)), part, 0.0)
-        inverse = inverse - mm(mm(inverse, cross), inverse)
+        cross = ((row // (2 * block)) == (col // (2 * block))) & (
+            (row // block) != (col // block)
+        )
+        lows = [inverse.astype(jnp.bfloat16) for inverse in inverses]
+        moves = [mm(low, jnp.where(cross, part, 0.0)) for low, part in zip(lows, parts)]
+        moves = [mm(move, low) for move, low in zip(moves, lows)]
+        inverses = [inverse - move for inverse, move in zip(inverses, moves)]
         block *= 2
-    return inverse
+    return inverses
 
 
 def stable_softplus(values):
@@ -499,34 +511,51 @@
         conv_out_ref[0, :, lanes] = result
         return result * jax.nn.sigmoid(result)
 
-    for head in range(heads):
+    every = range(heads)
+    queries, keys, values, parts, scores = [], [], [], [], []
+    for head in every:
         query, key = conv_block(head), conv_block(heads + head)
         query = query * (
             lax.rsqrt(jnp.sum(query * query, axis=1, keepdims=True) + 1e-06) * TILE ** (-0.5)
         )
         key = key * lax.rsqrt(jnp.sum(key * key, axis=1, keepdims=True) + 1e-06)
-        value = jnp.concatenate(
-            [conv_block(2 * heads + 2 * head), conv_block(2 * heads + 2 * head + 1)], axis=1
-        )
         spread = total[:, head : head + 1] - total_rows[head : head + 1, :]
         weights = jnp.exp(jnp.where(visible, spread, -1e30))
+        key_low, query_low = key.astype(jnp.bfloat16), query.astype(jnp.bfloat16)
+        grams = mm_nt(jnp.concatenate([key_low, query_low], axis=0), key_low)
         beta = beta_tile[:, heads + head : heads + head + 1]
-        carried = carry[:, head : head + 1]
-        key_low, query_low = key.astype(jnp.bfloat16), query.astype(jnp.bfloat16)
-        both = jnp.concatenate([key_low, query_low], axis=0)
-        grams = mm_nt(both, key_low)
-        part = jnp.where(row > col, beta * weights * grams[:TILE], 0.0)
-        inverse = unit_lower_inverse(part, row, col).astype(jnp.bfloat16)
-        state = state_ref[head]
-        state_low = state.astype(jnp.bfloat16)
-        from_state = mm(both, state_low)
-        pseudo = mm(inverse, beta * (value - carried * from_state[:TILE])).astype(jnp.bfloat16)
-        rows = carried * from_state[TILE:] + mm(grams[TILE:] * weights, pseudo)
-        weighted = key.T * weights[TILE - 1 : TILE, :]
-        state_ref[head] = carried[TILE - 1 : TILE, :] * state + mm(weighted, pseudo)
+        parts.append(jnp.where(row > col, beta * weights * grams[:TILE], 0.0))
+        scores.append((grams[TILE:] * weights).astype(jnp.bfloat16))
+        queries.append(query_low)
+        keys.append((key_low, (key.T * weights[TILE - 1 : TILE, :]).astype(jnp.bfloat16)))
+    for head in every:
+        values.append(
+            jnp.concatenate(
+                [conv_block(2 * heads + 2 * head), conv_block(2 * heads + 2 * head + 1)], axis=1
+            )
+        )
+    inverses = [item.astype(jnp.bfloat16) for item in unit_lower_inverses(parts, row, col)]
+    states = [state_ref[head] for head in every]
+    lows = [state.astype(jnp.bfloat16) for state in states]
+    from_states = [
+        mm(jnp.concatenate([keys[head][0], queries[head]], axis=0), lows[head]) for head in every
+    ]
+    carries = [carry[:, head : head + 1] for head in every]
+    pseudos = [
+        mm(
+            inverses[head],
+            beta_tile[:, heads + head : heads + head + 1]
+            * (values[head] - carries[head] * from_states[head][:TILE]),
+        ).astype(jnp.bfloat16)
+        for head in every
+    ]
+    for head in every:
         lanes = slice(2 * head * TILE, 2 * (head + 1) * TILE)
-        state_out_ref[0, 0, head] = state_low
-        inverse_out_ref[0, 0, head] = inverse
+        carried, pseudo = carries[head], pseudos[head]
+        state_ref[head] = carried[TILE - 1 : TILE, :] * states[head] + mm(keys[head][1], pseudo)
+        rows = carried * from_states[head][TILE:] + mm(scores[head], pseudo)
+        state_out_ref[0, 0, head] = lows[head]
+        inverse_out_ref[0, 0, head] = inverses[head]
         pseudo_out_ref[0, :, lanes] = pseudo
         rows_out_ref[0, :, lanes] = rows
         gate = proj_ref[
@@ -738,7 +767,7 @@
     def place(s, c):
         return s * blocks + ((blocks - 1 - c) if backward else c)
 
-    return dict(
+    return SimpleNamespace(
         proj=pl.BlockSpec((1, TILE, wide), lambda p, s, c: (p, place(s, c), 0)),
         info=pl.BlockSpec((TILE, TILE), lambda p, s, c: (place(s, c), 0)),
         conv=pl.BlockSpec((1, 8, conv_cols), lambda p, s, c: (p, 0, 0)),
@@ -766,9 +795,9 @@
     return pl.pallas_call(
         functools.partial(forward_body, heads),
         grid=(parts, rows // LENGTH, blocks),
-        in_specs=[spec[n] for n in ("proj", "info", "conv", "rates", "gain")],
+        in_specs=[spec.proj, spec.info, spec.conv, spec.rates, spec.gain],
         out_specs=[
-            spec[n] for n in ("flat", "conv_out", "value", "state", "inverse", "value")
+            spec.flat, spec.conv_out, spec.value, spec.state, spec.inverse, spec.value
         ],
         out_shape=[
             jax.ShapeDtypeStruct((rows, parts * value_cols), low),
@@ -783,9 +812,9 @@
             pltpu.VMEM((heads, TILE, 2 * TILE), full),
         ],
         compiler_params=pltpu.CompilerParams(
-            dimension_semantics=("arbitrary", "arbitrary", "arbitrary"),
             vmem_limit_bytes=48 * 1024 * 1024,
         ),
+        cost_estimate=pl.CostEstimate(flops=COST, transcendentals=0, bytes_accessed=10**8),
         name="mixer_forward",
     )(proj, info, conv, rates, gain)
 
@@ -800,13 +829,10 @@
         functools.partial(backward_body, heads),
         grid=(parts, rows // LENGTH, blocks),
         in_specs=[
-            spec[n]
-            for n in (
-                "proj", "info", "conv", "rates", "gain",
-                "conv_out", "value", "state", "inverse", "value", "flat",
-            )
+            spec.proj, spec.info, spec.conv, spec.rates, spec.gain,
+            spec.conv_out, spec.value, spec.state, spec.inverse, spec.value, spec.flat,
         ],
-        out_specs=[spec[n] for n in ("proj", "conv", "rates", "gain_sum")],
+        out_specs=[spec.proj, spec.conv, spec.rates, spec.gain_sum],
         out_shape=[
             jax.ShapeDtypeStruct((parts, rows, wide), low),
             jax.ShapeDtypeStruct((parts, 8, conv_cols), full),
@@ -818,11 +844,283 @@
             pltpu.VMEM((heads, TILE, 2 * TILE), full),
         ],
         compiler_params=pltpu.CompilerParams(
-            dimension_semantics=("arbitrary", "arbitrary", "arbitrary"),
             vmem_limit_bytes=48 * 1024 * 1024,
         ),
+        cost_estimate=pl.CostEstimate(flops=COST, transcendentals=0, bytes_accessed=10**8),
         name="mixer_backward",
     )(proj, info, conv, rates, gain, *saved, grad)
+
+
+BLOCK = 256
+
+
+def rms_backward(values, gain, grad):
+    scale = lax.rsqrt(jnp.mean(values * values, axis=1, keepdims=True) + 1e-06)
+    level = values * scale
+    through = grad * gain
+    back = scale * (through - level * jnp.mean(through * level, axis=1, keepdims=True))
+    return back, jnp.sum(grad * level, axis=0, keepdims=True)
+
+
+def dense_forward_body(
+    normed_ref,
+    gate_w_ref,
+    up_w_ref,
+    down_w_ref,
+    residual_ref,
+    target_ref,
+    live_ref,
+    level_ref,
+    gate_ref,
+    up_ref,
+    hidden_ref,
+    output_ref,
+    grad_ref,
+    grad_turned_ref,
+    loss_ref,
+    total_ref,
+):
+    part, step = pl.program_id(0), pl.program_id(1)
+    normed = normed_ref[...]
+    gate = mm(normed, gate_w_ref[0])
+    up = mm(normed, up_w_ref[0])
+    hidden = (gate * jax.nn.sigmoid(gate) * up).astype(jnp.bfloat16)
+    gate_ref[0] = gate.astype(jnp.bfloat16)
+    up_ref[0] = up.astype(jnp.bfloat16)
+    hidden_ref[0] = hidden
+    share = mm_nt(hidden, down_w_ref[0])
+    rows = pl.ds(pl.multiple_of(step * BLOCK, BLOCK), BLOCK)
+
+    @pl.when(part == 0)
+    def _():
+        total_ref[rows, :] = share
+
+    @pl.when(part == pl.num_programs(0) - 1)
+    def _():
+        output = residual_ref[...] + (total_ref[rows, :] + share)
+        output_ref[...] = output
+        error = output - target_ref[...].astype(jnp.float32)
+        live = live_ref[:, 0:1]
+        grad = error * live * level_ref[0:1, 0:1]
+        grad_ref[...] = grad.astype(jnp.bfloat16)
+        grad_turned_ref[...] = grad.T.astype(jnp.bfloat16)
+        squares = jnp.sum(live * error * error, axis=0, keepdims=True)
+
+        @pl.when(step == 0)
+        def _():
+            loss_ref[...] = jnp.zeros(loss_ref.shape, jnp.float32)
+
+        loss_ref[0:1, :] += squares
+
+
+def dense_backward_body(
+    grad_ref,
+    gate_w_ref,
+    up_w_ref,
+    down_w_ref,
+    gate_ref,
+    up_ref,
+    residual_ref,
+    output_ref,
+    target_ref,
+    live_ref,
+    level_ref,
+    gain_ref,
+    grad_gate_ref,
+    grad_up_ref,
+    back_ref,
+    back_low_ref,
+    back_turned_ref,
+    gain_sum_ref,
+    total_ref,
+):
+    part, step = pl.program_id(0), pl.program_id(1)
+    grad_hidden = mm(grad_ref[...], down_w_ref[0])
+    gate = gate_ref[0].astype(jnp.float32)
+    up = up_ref[0].astype(jnp.float32)
+    sigmoid = jax.nn.sigmoid(gate)
+    grad_gate = (grad_hidden * up * sigmoid * (1.0 + gate * (1.0 - sigmoid))).astype(jnp.bfloat16)
+    grad_up = (grad_hidden * gate * sigmoid).astype(jnp.bfloat16)
+    grad_gate_ref[0] = grad_gate
+    grad_up_ref[0] = grad_up
+    share = mm_nt(grad_gate, gate_w_ref[0]) + mm_nt(grad_up, up_w_ref[0])
+    rows = pl.ds(pl.multiple_of(step * BLOCK, BLOCK), BLOCK)
+
+    @pl.when(part == 0)
+    def _():
+        total_ref[rows, :] = share
+
+    @pl.when(part == pl.num_programs(0) - 1)
+    def _():
+        error = output_ref[...] - target_ref[...].astype(jnp.float32)
+        back, gain_sum = rms_backward(
+            residual_ref[...], gain_ref[...], total_ref[rows, :] + share
+        )
+        back = error * live_ref[:, 0:1] * level_ref[0:1, 0:1] + back
+        back_ref[...] = back
+        back_low_ref[...] = back.astype(jnp.bfloat16)
+        back_turned_ref[...] = back.T.astype(jnp.bfloat16)
+
+        @pl.when(step == 0)
+        def _():
+            gain_sum_ref[...] = jnp.zeros(gain_sum_ref.shape, jnp.float32)
+
+        gain_sum_ref[0:1, :] += gain_sum
+
+
+def input_backward_body(
+    first_ref, second_ref, weight_ref, input_ref, residual_ref, gain_ref, back_ref, gain_sum_ref, total_ref
+):
+    part, step = pl.program_id(0), pl.program_id(1)
+    grad = jnp.where(part == 0, first_ref[0], second_ref[0])
+    share = mm_nt(grad, weight_ref[0])
+    rows = pl.ds(pl.multiple_of(step * BLOCK, BLOCK), BLOCK)
+
+    @pl.when(part == 0)
+    def _():
+        total_ref[rows, :] = share
+
+    @pl.when(part == pl.num_programs(0) - 1)
+    def _():
+        back, gain_sum = rms_backward(
+            input_ref[...].astype(jnp.float32), gain_ref[...], total_ref[rows, :] + share
+        )
+        back_ref[...] = residual_ref[...] + back
+
+        @pl.when(step == 0)
+        def _():
+            gain_sum_ref[...] = jnp.zeros(gain_sum_ref.shape, jnp.float32)
+
+        gain_sum_ref[0:1, :] += gain_sum
+
+
+def dense_call(body, flags, arrays, choose, width, units):
+    rows = arrays[0].shape[-2]
+    full, low = jnp.float32, jnp.bfloat16
+
+    def cut(block, place, shape=None, kind=full):
+        return (pl.BlockSpec(block, place), jax.ShapeDtypeStruct(shape or block, kind))
+
+    late = (lambda p, i, flags: (i * p, 0), (rows, width))
+    spec = SimpleNamespace(
+        row=cut((BLOCK, width), lambda p, i, flags: (i, 0)),
+        late=cut((BLOCK, width), *late),
+        late_low=cut((BLOCK, width), *late, low),
+        turned=cut((width, BLOCK), lambda p, i, flags: (0, i * p), (width, rows), low),
+        unit=cut((1, BLOCK, units), lambda p, i, flags: (p, i, 0), (2, rows, units), low),
+        first=cut((1, BLOCK, units), lambda p, i, flags: (0, i * (1 - p), 0)),
+        second=cut((1, BLOCK, units), lambda p, i, flags: (0, i * p, 0)),
+        lane=cut((BLOCK, TILE), lambda p, i, flags: (i * p, 0)),
+        level=cut((8, TILE), lambda p, i, flags: (0, 0)),
+        gain=cut((1, width), lambda p, i, flags: (0, 0)),
+        own=cut((1, width, units), lambda p, i, flags: (lax.rem(p + 1 + flags[1], 2), 0, 0)),
+        sums=cut((8, width), lambda p, i, flags: (0, 0)),
+        weights=[
+            cut((1, width, units), lambda p, i, flags, index=index: (p, 0, index)) for index in range(3)
+        ],
+    )
+    taken, given = choose(spec)
+    return pl.pallas_call(
+        lambda flags_ref, *refs: body(*refs),
+        grid_spec=pltpu.PrefetchScalarGridSpec(
+            num_scalar_prefetch=1,
+            grid=(2, rows // BLOCK),
+            in_specs=[item[0] for item in taken],
+            out_specs=[item[0] for item in given],
+            scratch_shapes=[pltpu.VMEM((rows, width), full)],
+        ),
+        out_shape=[item[1] for item in given],
+        compiler_params=pltpu.CompilerParams(vmem_limit_bytes=56 * 1024 * 1024),
+        cost_estimate=pl.CostEstimate(flops=COST, transcendentals=0, bytes_accessed=10**8),
+        name=body.__name__[:-5],
+    )(flags, *arrays)
+
+
+def product_body(own, side_first, flags_ref, left_ref, first_ref, second_ref, *refs):
+    part = pl.program_id(0)
+    shape = left_ref.shape
+    left = left_ref[...].reshape(shape[0] * shape[2], shape[3])
+
+    def finish(right_ref):
+        result = mm(left, right_ref[...].reshape(right_ref.shape[-2:]))
+        if own:
+            result = result + refs[0][0].astype(jnp.float32)
+        result = result.astype(jnp.bfloat16)
+        if not side_first:
+            refs[-1][0] = result
+            return
+        split = result.reshape(shape[0] // 2, 2, shape[2], result.shape[1])
+        count = shape[0] * shape[2] // 2
+        low = split[:, 0].reshape(count, -1)
+        high = split[:, 1].reshape(count, -1)
+        here = flags_ref[2] == 0
+        refs[-2][0] = jnp.where(here, low, high)
+        refs[-1][0] = jnp.where(here, high, low)
+
+    @pl.when(part == 0)
+    def _():
+        finish(first_ref)
+
+    @pl.when(part == 1)
+    def _():
+        finish(second_ref)
+
+
+def product(flags, left, rights, received=None, side_first=False, relative=False):
+    own = received is not None
+    side_first = side_first and own
+    groups, _, rows, tokens = left.shape
+    cols, count = rights[0].shape[-1], len(rights)
+    block = cols if count == 2 else -(-cols // (2 * TILE)) * TILE
+    last = -(-cols // block) - 1
+
+    def slot(p, flags):
+        return 0 if count == 1 else 1 - p if relative else lax.rem(p + flags[1], 2)
+
+    def right_spec(array, index, which):
+        def place(p, j, flags):
+            return j * (1 - p) + last * p if which == 0 else j * p
+
+        if array.ndim == 3:
+            return pl.BlockSpec(
+                (1, tokens, block), lambda p, j, flags: (index, 0, place(p, j, flags))
+            )
+        return pl.BlockSpec((tokens, block), lambda p, j, flags: (0, place(p, j, flags)))
+
+    result_rows = groups * rows // (2 if side_first else 1)
+    result = pl.BlockSpec((1, result_rows, block), lambda p, j, flags: (slot(p, flags), 0, j))
+    kept = jax.ShapeDtypeStruct((count, result_rows, cols), jnp.bfloat16)
+    in_specs = [
+        pl.BlockSpec(
+            (groups, 1, rows, tokens),
+            lambda p, j, flags: (0, flags[0] if own else 1 - flags[0], 0, 0),
+        ),
+        right_spec(rights[0], 0, 0),
+        right_spec(rights[-1], rights[-1].shape[0] - 1, count - 1),
+    ]
+    arrays = [left, rights[0], rights[-1]]
+    if own:
+        in_specs.append(
+            pl.BlockSpec((1, groups * rows, block), lambda p, j, flags: (slot(p, flags), 0, j))
+        )
+        arrays.append(received)
+    many = 2 if side_first else 1
+    results = pl.pallas_call(
+        functools.partial(product_body, own, side_first),
+        grid_spec=pltpu.PrefetchScalarGridSpec(
+            num_scalar_prefetch=1,
+            grid=(count, last + 1),
+            in_specs=in_specs,
+            out_specs=[result] * many,
+        ),
+        out_shape=[kept] * many,
+        compiler_params=pltpu.CompilerParams(vmem_limit_bytes=56 * 1024 * 1024),
+        cost_estimate=pl.CostEstimate(
+            flops=2 * groups * rows * tokens * cols * count, transcendentals=0, bytes_accessed=10**7
+        ),
+        name="product",
+    )(flags, *arrays)
+    return results if side_first else results[0]
 
 
 def token_info(seg):
@@ -841,16 +1139,151 @@
 
 
 def gather_all(local):
-    rows = lax.all_gather(local, ("tensor", "dp"), axis=0, tiled=True)
-    shares = lax.axis_size("tensor")
+    rows = lax.all_gather(local, (TP, DP), axis=0, tiled=True)
+    shares = lax.axis_size(TP)
     return rows.reshape(shares, rows.shape[0] // shares, rows.shape[1])
 
 
 def scatter_all(parts):
     shares, rows, cols = parts.shape
     return lax.psum_scatter(
-        parts.reshape(shares * rows, cols), ("tensor", "dp"), scatter_dimension=0, tiled=True
+        parts.reshape(shares * rows, cols), (TP, DP), scatter_dimension=0, tiled=True
     ).astype(jnp.float32)
+
+
+def exchange(array, axis, bit):
+    size = lax.axis_size(axis)
+    return lax.ppermute(array, axis, [(i, i ^ bit) for i in range(size)])
+
+
+def shift(array, step):
+    size = lax.axis_size(DP)
+    return lax.ppermute(array, DP, [(i, (i + step) % size) for i in range(size)])
+
+
+def pick(array, index, axis):
+    return lax.dynamic_index_in_dim(array, index, axis, keepdims=False)
+
+
+def add_low(left, right):
+    return (left.astype(jnp.float32) + right.astype(jnp.float32)).astype(jnp.bfloat16)
+
+
+def after(value, *earlier):
+    return lax.optimization_barrier((value, earlier))[0]
+
+
+class Scatter:
+    def __init__(self, flags, turned, rights, stages, relative=False):
+        self.relative, self.stages = relative, list(stages)
+        self.size = lax.axis_size(DP)
+        self.flags, self.rights = flags, rights
+        self.left = turned.reshape(self.size // 2, 2, -1, turned.shape[1])
+        self.rows = self.left.shape[2]
+        self.sent = [product(flags, self.left, rights, relative=relative)]
+
+    joined = None
+
+    def routes(self):
+        flat = [item.reshape(-1, item.shape[-1]) for item in self.sent]
+        stage = self.stages[0]
+        return [
+            ((stage, step if stage == PLACE else 0, item.shape[0]), item)
+            for step, item in enumerate(flat)
+        ]
+
+    def take(self, moved):
+        stage = self.stages.pop(0)
+        if stage == PLACE:
+            self.total = self.kept.astype(jnp.float32)
+            for item in moved:
+                self.total = self.total + item.astype(jnp.float32)
+            return
+        if stage == CORE:
+            side_first = self.stages[0] == SIDE
+            held = product(
+                self.flags, self.left, self.rights, moved[0], side_first, self.relative
+            )
+            if side_first:
+                self.kept, self.sent = [list(item) for item in held]
+            else:
+                self.kept, self.sent = [held[0]], [held[1]]
+            return
+        held = [add_low(kept, item) for kept, item in zip(self.kept, moved)]
+        if not self.stages:
+            self.held = held[0]
+            return
+        if self.joined is not None:
+            held = [add_low(held[0], self.joined)]
+        stage = self.stages[0]
+        if stage == TENSOR:
+            self.kept, self.sent = held[:1], held[1:]
+        elif stage == SIDE:
+            held = held[0].reshape(self.size // 4, 2, self.rows, -1)
+            self.kept, self.sent = [
+                [pick(held, index, 1).reshape(-1, held.shape[-1])]
+                for index in (self.flags[2], 1 - self.flags[2])
+            ]
+        else:
+            count = self.size // 4
+            held = held[0].reshape(count, self.rows, -1)
+            self.sent = [
+                pick(held, (self.flags[3] + step) % count, 0) for step in range(1, count)
+            ]
+            self.kept = pick(held, self.flags[3], 0)
+
+
+def send(route, array):
+    stage, step, _ = route
+    if stage == PLACE:
+        return shift(array, 4 * (step + 1))
+    if stage == TENSOR:
+        return exchange(array, TP, 1)
+    return exchange(array, DP, stage)
+
+
+class Transfer:
+    def __init__(self, *items):
+        self.items, self.routes = items, {}
+        for index, item in enumerate(items):
+            for slot, (route, array) in enumerate(item.routes()):
+                key = route + ((index, slot) if route[0] == CORE else ())
+                self.routes.setdefault(key, []).append((index, slot, array))
+        self.packed = [
+            jnp.concatenate([entry[2] for entry in entries], axis=1)
+            for entries in self.routes.values()
+        ]
+
+    def send(self):
+        return [send(key[:3], array) for key, array in zip(self.routes, self.packed)]
+
+    def land(self):
+        self.accept(lax.optimization_barrier(self.send()))
+
+    def accept(self, moved):
+        got = [[None] * len(item.sent) for item in self.items]
+        for entries, array in zip(self.routes.values(), moved):
+            pieces = columns(array, [entry[2].shape[1] for entry in entries])
+            for (index, slot, _), piece in zip(entries, pieces):
+                got[index][slot] = piece
+        for item, mine in zip(self.items, got):
+            item.take([piece.reshape(sent.shape) for piece, sent in zip(mine, item.sent)])
+
+
+class Shared:
+    def __init__(self, flat, stages):
+        self.flat, self.stages = flat.reshape(1, -1), list(stages)
+
+    @property
+    def sent(self):
+        return [self.flat]
+
+    def routes(self):
+        return [((self.stages[0], 0, 1), self.flat)]
+
+    def take(self, moved):
+        self.stages.pop(0)
+        self.flat = self.flat + moved[0]
 
 
 def columns(array, sizes):
@@ -886,9 +1319,9 @@
     w_ffn_down,
 ):
     own_rows, width = layer_input.shape
-    shares = lax.axis_size("tensor")
+    shares = lax.axis_size(TP)
     sequences = own_rows // LENGTH
-    tensor_index = lax.axis_index("tensor")
+    tensor_index = lax.axis_index(TP)
     low = jnp.bfloat16
     proj_local = (w_query, w_key, w_value, w_gate_out, w_decay, w_beta)
     proj_sizes = [item.shape[1] for item in proj_local]
@@ -897,24 +1330,22 @@
     proj_all = gather_all(
         jnp.concatenate(proj_local + (jnp.zeros((w_query.shape[0], padded - used), low),), axis=1)
     )
-    rest_local = (w_out, w_ffn_gate, w_ffn_up, w_ffn_down)
+    rest_local = (w_ffn_gate, w_ffn_up, w_ffn_down, w_out)
     rest_sizes = [item.shape[1] for item in rest_local]
     rest_all = gather_all(jnp.concatenate(rest_local, axis=1))
-    out_all, gate_all, up_all, down_all = columns(rest_all, rest_sizes)
+    out_all = columns(rest_all, rest_sizes)[3]
     live = pad_mask.astype(jnp.float32)
-    count = lax.psum(jnp.sum(live), ("dp", "tensor"))
+    count = lax.psum(jnp.sum(live), (DP, TP))
     input_float = layer_input.astype(jnp.float32)
-    normed_float, norm1_pull = jax.vjp(rms_scale, input_float, norm1_gain)
-    normed = normed_float.astype(low)
+    normed = rms_scale(input_float, norm1_gain).astype(low)
     seg_rows = lax.dynamic_slice_in_dim(segment, tensor_index * own_rows, own_rows, 0).reshape(
         sequences, LENGTH
     )
-    proj = jnp.stack(
-        [
-            jnp.dot(normed, proj_all[part], preferred_element_type=jnp.float32)
-            for part in range(shares)
-        ]
-    )
+    parts = (1 - tensor_index, tensor_index)
+    proj = [
+        jnp.dot(normed, pick(proj_all, part, 0), preferred_element_type=jnp.float32)[None]
+        for part in parts
+    ]
     heads = w_decay.shape[1]
     info = token_info(seg_rows)
 
@@ -929,120 +1360,163 @@
         by_part(jnp.stack([decay_scale, decay_bias])), ((0, 0), (0, 6), (0, TILE - heads))
     )
     gain = out_norm_gain.reshape(1, -1)
-    mixed_low, *saved = mixer_forward(proj, info, conv, rates, gain, heads)
     value_cols = w_value.shape[1]
-    residual = input_float
-    for part in range(shares):
-        residual = residual + contract_cols(
-            mixed_low[:, part * value_cols : (part + 1) * value_cols], out_all[part]
-        )
-    normed2_float, norm2_pull = jax.vjp(rms_scale, residual, norm2_gain)
-    normed2 = normed2_float.astype(low)
-    output = residual
-    kept = []
-    for part in range(shares):
-        gate_pre, up_pre = feed_inputs(normed2, gate_all[part], up_all[part])
-        hidden = (jax.nn.silu(gate_pre) * up_pre).astype(low)
-        output = output + contract_cols(hidden, down_all[part])
-        kept.append((gate_pre, up_pre, hidden))
-    error = output - target.astype(jnp.float32)
-    loss_sum = jnp.sum(live[:, None] * error * error)
-    all_tokens = own_rows * lax.axis_size("dp") * lax.axis_size("tensor")
-    grad_output = error * live[:, None] * (all_tokens / count)
-    grad_ffn = grad_output.astype(low)
-    grad_normed2 = jnp.zeros_like(residual)
-    ffn_grads = []
-    for part in range(shares):
-        gate_pre, up_pre, hidden = kept[part]
-        grad_hidden = jnp.dot(grad_ffn, down_all[part], preferred_element_type=jnp.float32)
-        sigmoid_gate = jax.nn.sigmoid(gate_pre)
-        grad_gate = (
-            grad_hidden * up_pre * sigmoid_gate * (1.0 + gate_pre * (1.0 - sigmoid_gate))
-        ).astype(low)
-        grad_up = (grad_hidden * gate_pre * sigmoid_gate).astype(low)
-        grad_normed2 = (
-            grad_normed2
-            + contract_cols(grad_gate, gate_all[part])
-            + contract_cols(grad_up, up_all[part])
-        )
-        ffn_grads.append(
-            (
-                contract_rows(normed2, grad_gate),
-                contract_rows(normed2, grad_up),
-                contract_rows(grad_ffn, hidden),
-            )
-        )
-    grad_residual_norm, grad_gain_two = norm2_pull(grad_normed2)
-    grad_residual = grad_output + grad_residual_norm
-    grad_attention = grad_residual.astype(low)
-    grad_mixed = jnp.concatenate(
+    mixer_args = [
+        (item, info, pick(conv, part, 0)[None], pick(rates, part, 0)[None], gain)
+        for item, part in zip(proj, parts)
+    ]
+    out_parts = [pick(out_all, part, 0) for part in parts]
+    saved, mixed, residual = [], [], input_float
+    for arguments in mixer_args:
+        mixed_low, *kept = mixer_forward(*arguments, heads)
+        mixed.append(mixed_low)
+        saved.append(kept)
+    for item, weight in zip(mixed, out_parts):
+        residual = residual + contract_cols(item, weight)
+    normed2 = rms_scale(residual, norm2_gain).astype(low)
+    units = w_ffn_gate.shape[1]
+    all_tokens = own_rows * lax.axis_size(DP) * lax.axis_size(TP)
+    level = jnp.full((8, TILE), all_tokens / count, jnp.float32)
+    live_lanes = jnp.broadcast_to(live[:, None], (own_rows, TILE))
+    mine = lax.axis_index(DP)
+    flags = jnp.stack([mine % 2, tensor_index, (mine // 2) % 2, mine // 4]).astype(jnp.int32)
+    weights = [rest_all] * 3
+    gate_pre, up_pre, hidden, output, grad_ffn, grad_ffn_turned, loss_rows = dense_call(
+        dense_forward_body,
+        flags,
+        [normed2, *weights, residual, target, live_lanes, level],
+        lambda s: (
+            [s.row, *s.weights, s.late, s.late, s.lane, s.level],
+            [s.unit, s.unit, s.unit, s.late, s.late_low, s.turned, s.sums],
+        ),
+        width,
+        units,
+    )
+    loss_sum = jnp.sum(loss_rows)
+    down = Scatter(flags, grad_ffn_turned, [hidden, hidden], SIDE_FIRST)
+    cores = Transfer(down)
+    grad_gates, grad_ups, grad_residual, grad_attention, back_turned, gain_two_rows = dense_call(
+        dense_backward_body,
+        flags,
         [
-            jnp.dot(grad_attention, out_all[part], preferred_element_type=jnp.float32)
-            for part in range(shares)
+            after(grad_ffn, cores.packed), *weights, gate_pre, up_pre,
+            residual, output, target, live_lanes, level, norm2_gain.reshape(1, -1),
         ],
-        axis=1,
-    )
-    rest_grads = jnp.stack(
-        [
-            jnp.concatenate(
-                [
-                    item.astype(low)
-                    for item in (
-                        contract_rows(
-                            grad_attention,
-                            mixed_low[:, part * value_cols : (part + 1) * value_cols],
-                        ),
-                    )
-                    + ffn_grads[part]
-                ],
-                axis=1,
-            )
-            for part in range(shares)
-        ]
-    )
-    own_out, own_gate, own_up, own_down = columns(scatter_all(rest_grads), rest_sizes)
-    grad_proj, grad_conv, grad_rates, grad_gain = mixer_backward(
-        proj, info, conv, rates, gain, saved, grad_mixed, heads
-    )
-    grad_normed = jnp.zeros_like(residual)
-    proj_grads = []
-    for part in range(shares):
-        grad_normed = grad_normed + contract_cols(grad_proj[part], proj_all[part])
-        proj_grads.append(contract_rows(normed, grad_proj[part]).astype(low))
+        lambda s: (
+            [s.row, *s.weights, s.unit, s.unit, s.late, s.late, s.late, s.lane, s.level, s.gain],
+            [s.unit, s.unit, s.late, s.late_low, s.turned, s.sums],
+        ),
+        width,
+        units,
+    )
+    grad_gain_two = gain_two_rows[0]
+    turned2 = normed2.T
+    gate = Scatter(flags, turned2, [grad_gates, grad_gates], TENSOR_FIRST)
+    up = Scatter(flags, turned2, [grad_ups, grad_ups], SIDE_FIRST)
+    cores.land()
+    first_down = Transfer(down)
+    gate.sent = after(gate.sent, first_down.packed)
+    cores = Transfer(gate, up)
+    out = Scatter(flags, back_turned, mixed, SIDE_FIRST, True)
+    out_cores = Transfer(out)
+    later = after(grad_attention, out_cores.packed, cores.packed)
+    grad_mixed = [
+        jnp.dot(later, weight, preferred_element_type=jnp.float32) for weight in out_parts
+    ]
+    cores.land()
+    out_cores.land()
+    first_down.land()
+    middle = Transfer(gate, up, out, down)
+    ready = after(grad_mixed[0], middle.packed)
+    per_part = [mixer_backward(*mixer_args[0], saved[0], ready, heads)]
+    turned = normed.T
+    theirs = Scatter(flags, turned, [per_part[0][0]], (CORE, SIDE))
+    theirs_cores = Transfer(theirs)
+    middle.land()
+    middle = Transfer(gate, up, out)
+    theirs.left = after(theirs.left, middle.packed)
+    theirs_cores.land()
+    theirs_side = Transfer(theirs)
+    ready = after(grad_mixed[1], middle.packed, theirs_side.packed)
+    per_part.append(mixer_backward(*mixer_args[1], saved[1], ready, heads))
+    grad_conv, grad_rates, grad_gain = [
+        jnp.roll(
+            jnp.concatenate([item[i] for item in per_part], axis=0), tensor_index + 1, axis=0
+        )
+        for i in (1, 2, 3)
+    ]
 
     def from_part(item):
         return item.transpose(1, 0, 2).reshape(item.shape[1], -1)
 
     query_cols = w_query.shape[1]
-    mixer_grads = [
+    small = [
         from_part(item)
         for item in columns(grad_conv[:, :4], (query_cols, query_cols, value_cols))
     ] + [
         grad_rates[:, 0, :heads].reshape(-1),
         grad_rates[:, 1, :heads].reshape(-1),
         jnp.sum(grad_gain[:, 0], axis=0),
+        grad_gain_two,
+        loss_sum,
     ]
-    own_proj = columns(scatter_all(jnp.stack(proj_grads)), proj_sizes)
-    grad_input_norm, grad_gain_one = norm1_pull(grad_normed)
-    grad_input = grad_residual + grad_input_norm
-    summed = lax.psum(
-        (grad_gain_one, grad_gain_two) + tuple(mixer_grads) + (loss_sum,), ("dp", "tensor")
-    )
-    loss = summed[8] / (count * width)
+    grad_proj = [item[0] for item in per_part]
+    ours = Scatter(flags, turned, [grad_proj[1]], (CORE, SIDE, PLACE))
+    ours_cores = Transfer(ours)
+    theirs.sent = after(theirs.sent, ours_cores.packed)
+    middle.land()
+    theirs_side.land()
+    middle = Transfer(gate, up, out, down)
+    ours.left = after(ours.left, middle.packed, theirs.held)
+    ours_cores.land()
+    ending = Transfer(ours)
+    grad_proj = after(grad_proj, ending.packed)
+    grad_input, gain_one_rows = dense_call(
+        input_backward_body,
+        flags,
+        [*grad_proj, proj_all, layer_input, grad_residual, norm1_gain.reshape(1, -1)],
+        lambda s: ([s.first, s.second, s.own, s.late, s.late, s.gain], [s.late, s.sums]),
+        width,
+        padded,
+    )
+    joined = exchange(theirs.held, TP, 1)
+    joined, gain_one_rows, *moved = lax.optimization_barrier(
+        [joined, gain_one_rows] + middle.send() + ending.send()
+    )
+    ours.joined = joined
+    middle.accept(moved[: len(middle.packed)])
+    ending.accept(moved[len(middle.packed) :])
+    size, places = lax.axis_size(DP), []
+    while 4 << len(places) < size:
+        places.append(4 << len(places))
+    small.append(gain_one_rows[0])
+    flat = jnp.concatenate([item.reshape(-1) for item in small])
+    flat = jnp.pad(flat, (0, -flat.shape[0] % 1024))
+    shared = Shared(flat, places + [CORE, SIDE, TENSOR])
+    for _ in places:
+        Transfer(shared).land()
+    ours.sent = after(ours.sent, shared.flat)
+    ending = Transfer(ours)
+    shared.flat = after(shared.flat, ending.packed)
+    while shared.stages:
+        Transfer(shared).land()
+    ending.land()
+    own_gate, own_up, own_out, own_down = [item.total for item in (gate, up, out, down)]
+    own_proj = columns(ours.total, proj_sizes)
+    summed, start = [], 0
+    for item in small:
+        summed.append(shared.flat[0, start : start + item.size].reshape(item.shape))
+        start += item.size
+    loss = summed[7] / (count * width)
     return (
         output,
         loss,
         grad_input,
-        summed[0],
+        summed[8],
         *own_proj,
-        summed[2],
-        summed[3],
-        summed[4],
-        summed[5],
+        *summed[:6],
+        own_out,
         summed[6],
-        summed[7],
-        own_out,
-        summed[1],
         own_gate,
         own_up,
         own_down,
@@ -1050,7 +1524,9 @@
 
 
 def on_device(layer_input, *others):
-    whole = layer_input.shape[0] % LENGTH == 0
+    size = lax.axis_size(DP)
+    whole = layer_input.shape[0] % LENGTH == 0 and lax.axis_size(TP) == 2
+    whole = whole and size >= 4 and size & (size - 1) == 0
     return (on_device_whole if whole else on_device_split)(layer_input, *others)
 
 
@@ -1059,51 +1535,51 @@
         on_device,
         mesh=mesh,
         in_specs=(
-            P(("dp", "tensor"), None),
-            P(("dp", "tensor"), None),
-            P("dp"),
-            P(("dp", "tensor")),
-            P(),
-            P("dp", "tensor"),
-            P("dp", "tensor"),
-            P("dp", "tensor"),
-            P("dp", "tensor"),
-            P("dp", "tensor"),
-            P("dp", "tensor"),
-            P(),
-            P(),
-            P(),
-            P(),
-            P(),
-            P(),
-            P("dp", "tensor"),
-            P(),
-            P("dp", "tensor"),
-            P("dp", "tensor"),
-            P("dp", "tensor"),
+            P((DP, TP), None),
+            P((DP, TP), None),
+            P(DP),
+            P((DP, TP)),
+            P(),
+            P(DP, TP),
+            P(DP, TP),
+            P(DP, TP),
+            P(DP, TP),
+            P(DP, TP),
+            P(DP, TP),
+            P(),
+            P(),
+            P(),
+            P(),
+            P(),
+            P(),
+            P(DP, TP),
+            P(),
+            P(DP, TP),
+            P(DP, TP),
+            P(DP, TP),
         ),
         out_specs=(
-            P(("dp", "tensor"), None),
-            P(),
-            P(("dp", "tensor"), None),
-            P(),
-            P("dp", "tensor"),
-            P("dp", "tensor"),
-            P("dp", "tensor"),
-            P("dp", "tensor"),
-            P("dp", "tensor"),
-            P("dp", "tensor"),
-            P(),
-            P(),
-            P(),
-            P(),
-            P(),
-            P(),
-            P("dp", "tensor"),
-            P(),
-            P("dp", "tensor"),
-            P("dp", "tensor"),
-            P("dp", "tensor"),
+            P((DP, TP), None),
+            P(),
+            P((DP, TP), None),
+            P(),
+            P(DP, TP),
+            P(DP, TP),
+            P(DP, TP),
+            P(DP, TP),
+            P(DP, TP),
+            P(DP, TP),
+            P(),
+            P(),
+            P(),
+            P(),
+            P(),
+            P(),
+            P(DP, TP),
+            P(),
+            P(DP, TP),
+            P(DP, TP),
+            P(DP, TP),
         ),
         check_vma=False,
     )

time: 910 us -> 715 us (0.79)
  matrix products: 217 us -> 39.2 us
  Pallas kernels: 195 us -> 332 us
  waiting for transfers between devices: 282 us -> 165 us
  blocking collectives: 85.8 us -> 41 us
  starting transfers between devices: 0.16 us -> 28.6 us
  other arithmetic: 59.6 us -> 35.6 us
    reduce_scatter x1 -> x0, waiting for transfers between devices: 234 us -> none  [scatter_all(): lax.psum_scatter(parts.reshape(shares * rows, cols), ('tensor', 'dp'), sc...]
    pallas_call x0 -> x15, Pallas kernels: none -> 203 us  [the longest x12 108 us: product(): pl.pallas_call(functools.partial(product_body, own, side_first), grid_spe...]
    dot_general x20 -> x4, matrix products: 141 us -> 34.2 us  [the longest x2 23.8 us: on_device_whole(): jnp.dot(normed, pick(proj_all, part, 0), preferred_element_type=jnp.float32)]
    dot_general x10 -> x2, matrix products: 75.2 us -> 5.03 us  [contract_cols(): lax.dot_general(left, right, (((1,), (1,)), ((), ())), preferred_element_...]
    pallas_call x1 -> x2, Pallas kernels: 124 us -> 54.8 us  [mixer_forward(): pl.pallas_call(functools.partial(forward_body, heads), grid=(parts, rows...]
    all_gather x2, waiting for transfers between devices: 41.7 us -> 107 us  [gather_all(): rows = lax.all_gather(local, (TP, DP), axis=0, tiled=True)]
    ppermute x0 -> x26, waiting for transfers between devices: none -> 58 us  [the longest x6 44.2 us: shift(): lax.ppermute(array, DP, [(i, (i + step) % size) for i in range(size)])]
    psum x2 -> x1, blocking collectives: 85.8 us -> 41 us  [on_device_whole(): count = lax.psum(jnp.sum(live), (DP, TP))]
  transfers between devices with their start and end apart: 4 -> 28, of which waited for: 3 -> 11; matrix products, arithmetic and copies ran while one was open for 17% -> 13% of each run, Pallas kernels for 14% -> 41%
where the time goes in v3:
time: 715 us; the launch traced here: 707 us
  Pallas kernels  332 us (46%)
  waiting for transfers between devices  165 us (23%)
  local copies, waits for them, and re-layouts  47.3 us (7%)
  blocking collectives  41 us (6%)
  matrix products  39.2 us (5%)
  other arithmetic  35.6 us (5%)
  starting transfers between devices  28.6 us (4%)
  between operations  18.5 us (3%)
    pallas_call x12, Pallas kernels, product(): pl.pallas_call(functools.partial(product_body, own, side_first), grid_spe...  108 us
    all_gather x2, waiting for transfers between devices, gather_all(): rows = lax.all_gather(local, (TP, DP), axis=0, tiled=True)  107 us
    pallas_call x3, Pallas kernels, dense_call(): pl.pallas_call(lambda flags_ref, *refs: body(*refs), grid_spec=pltpu.Pref...  95.1 us
    pallas_call x2, Pallas kernels, mixer_backward(): pl.pallas_call(functools.partial(backward_body, heads), grid=(parts, rows...  74.1 us
    pallas_call x2, Pallas kernels, mixer_forward(): pl.pallas_call(functools.partial(forward_body, heads), grid=(parts, rows...  54.8 us
    ppermute x6, waiting for transfers between devices, shift(): lax.ppermute(array, DP, [(i, (i + step) % size) for i in range(size)])  44.2 us
    psum x1, blocking collectives, on_device_whole(): count = lax.psum(jnp.sum(live), (DP, TP))  41 us
    dot_general x2, matrix products, on_device_whole(): jnp.dot(normed, pick(proj_all, part, 0), preferred_element_type=jnp.float32)  23.8 us
  transfers between devices with their start and end apart: 28, of which 11 were waited for; matrix products, arithmetic and copies ran while one was open for 13% of the time, Pallas kernels for 41%

profile of v3, /device:TPU:8, one launch (start us, length us, event | category | flops | bytes accessed | tf_op | source)
XLA Modules:
  0.0 707.1 jit_solution(2495629696451056522)
XLA Ops:
  13.7 41.0 %psum.7 = f32[]{:T(128)} all-reduce(f32[]{:T(128)} %convert_reduce_fusion), channel_id=1, replica_groups=mesh['dp'=16,'tensor'=2] {'dp','tensor'}, use_global_device_ids=true, to_apply=%region_3.4 | all-reduce | flops 1 | bytes 8 | tf_op jit(solution)/shard_map/psum | solution.py:1338
  57.9 53.4 %all-gather.3.cloned.1.call-done = bf16[2048,3200]{1,0:T(8,128)(2,1)} async-done(((bf16[64,3200]{1,0:T(8,128)(2,1)}), bf16[2048,3200]{1,0:T(8,128)(2,1)}) %all-gather.3.cloned.1.call-update) | async-done | bytes 13107216 | tf_op jit(solution)/shard_map/all_gather | solution.py:1142
  111.3 13.4 %convolution_bitcast_fusion.proj_ref = f32[1,1024,3200]{2,1,0:T(8,128)} fusion(bf16[2,1024,3200]{2,1,0:T(8,128)(2,1)} %bitcast.288, s32[]{:T(128)S(6)} %select_n.141, bf16[1024,1024]{1,0:T(8,128)(2,1)S(1)} %copy-done.16, f32[1024]{0:T(1024)S(1)} %copy-done.47, f32[1024]{0:T(1024)S(1)} %add_rsqrt_fusion.1), kind=kOutput, calls=%fused_computation | convolution fusion | flops 6715080704 | bytes 21766148 | tf_op jit(solution)/shard_map/dot_general | solution.py:1346
  124.7 10.3 %convolution_bitcast_fusion.1.proj_ref = f32[1,1024,3200]{2,1,0:T(8,128)} fusion(bf16[2,1024,3200]{2,1,0:T(8,128)(2,1)S(1)} %bitcast.290, s32[]{:T(128)S(6)} %select_n.139, bf16[1024,1024]{1,0:T(8,128)(2,1)S(1)} %copy-done.16, f32[1024]{0:T(1024)S(1)} %copy-done.47, f32[1024]{0:T(1024)S(1)} %add_rsqrt_fusion.1), kind=kOutput, calls=%fused_computation.1 | convolution fusion | flops 6715080704 | bytes 21766148 | tf_op jit(solution)/shard_map/dot_general | solution.py:1346
  135.1 27.0 %mixer_forward.3 = (bf16[1024,1024]{1,0:T(8,128)(2,1)S(1)}, f32[1,1024,2048]{2,1,0:T(8,128)}, f32[1,1024,1024]{2,1,0:T(8,128)}, bf16[1,8,4,128,256]{4,3,2,1,0:T(...) custom-call(f32[1,1024,3200]{2,1,0:T(8,128)} %convolution_bitcast_fusion.proj_ref, ...), custom_call_target="tpu_custom_call" | custom-call | flops 40000000000 | bytes 100000000 | tf_op jit(solution)/shard_map/mixer_forward/pallas_call | solution.py:795
  164.4 27.7 %mixer_forward.2 = (bf16[1024,1024]{1,0:T(8,128)(2,1)S(1)}, f32[1,1024,2048]{2,1,0:T(8,128)}, f32[1,1024,1024]{2,1,0:T(8,128)}, bf16[1,8,4,128,256]{4,3,2,1,0:T(...) custom-call(f32[1,1024,3200]{2,1,0:T(8,128)} %convolution_bitcast_fusion.1.proj_ref, ...), custom_call_target="tpu_custom_call" | custom-call | flops 40000000000 | bytes 100000000 | tf_op jit(solution)/shard_map/mixer_forward/pallas_call | solution.py:795
  195.8 53.4 %all-gather.5.cloned.1.call-done = bf16[2048,5248]{1,0:T(8,128)(2,1)} async-done(((bf16[64,5248]{1,0:T(8,128)(2,1)}), bf16[2048,5248]{1,0:T(8,128)(2,1)}) %all-gather.5.cloned.1.call-update) | async-done | bytes 21495824 | tf_op jit(solution)/shard_map/all_gather | solution.py:1142
  263.0 33.0 %dense_forward.1 = (bf16[2,1024,1408]{2,1,0:T(8,128)(2,1)}, bf16[2,1024,1408]{2,1,0:T(8,128)(2,1)}, bf16[2,1024,1408]{2,1,0:T(8,128)(2,1)}, f32[1024,1024]{1,0:T...) custom-call(s32[4]{0:T(128)} %pad_add_fusion.flags_ref, ...), custom_call_target="tpu_custom_call" | custom-call | flops 40000000000 | bytes 100000000 | tf_op jit(solution)/shard_map/dense_forward/pallas_call | solution.py:1023
  296.0 8.7 %product.12 = bf16[2,512,1408]{2,1,0:T(8,128)(2,1)} custom-call(s32[4]{0:T(128)} %pad_add_fusion.flags_ref, bf16[8,2,64,1024]{3,2,1,0:T(8,128)(2,1)} %bitcast.232, bf16[2,1024,1408]{2,1,0:T(8,128)(2,1)} %get-tuple-element.105.first_ref.second_ref, bf16[2,1024,1408]{2,1,0:T(8,128)(2,1)} %get-tuple-element.105.first_ref.second_ref), custom_call_target="tpu_custom_call" | custom-call | flops 2952790016 | bytes 10000000 | tf_op jit(solution)/shard_map/product/pallas_call | solution.py:1108
  307.6 36.3 %dense_backward.1 = (bf16[2,1024,1408]{2,1,0:T(8,128)(2,1)}, bf16[2,1024,1408]{2,1,0:T(8,128)(2,1)}, f32[1024,1024]{1,0:T(8,128)}, bf16[1024,1024]{1,0:T(8,128)(...) custom-call(s32[4]{0:T(128)} %pad_add_fusion.flags_ref, bf16[1024,1024]{1,0:T(8,128)(2,1)} %get-tuple-element.106.refs_0_, ...), custom_call_target="tpu_custom_call" | custom-call | flops 40000000000 | bytes 100000000 | tf_op jit(solution)/shard_map/dense_backward/pallas_call | solution.py:1023
  343.9 8.5 %product.16 = bf16[2,512,1408]{2,1,0:T(8,128)(2,1)} custom-call(s32[4]{0:T(128)} %pad_add_fusion.flags_ref, bf16[8,2,64,1024]{3,2,1,0:T(8,128)(2,1)} %bitcast.224, bf16[2,1024,1408]{2,1,0:T(8,128)(2,1)} %get-tuple-element.114.first_ref.second_ref, bf16[2,1024,1408]{2,1,0:T(8,128)(2,1)} %get-tuple-element.114.first_ref.second_ref), custom_call_target="tpu_custom_call" | custom-call | flops 2952790016 | bytes 10000000 | tf_op jit(solution)/shard_map/product/pallas_call | solution.py:1108
  352.7 6.8 product.13
  359.8 8.9 %product.14 = bf16[2,512,1408]{2,1,0:T(8,128)(2,1)} custom-call(s32[4]{0:T(128)} %pad_add_fusion.flags_ref, bf16[8,2,64,1024]{3,2,1,0:T(8,128)(2,1)} %bitcast.225, bf16[2,1024,1408]{2,1,0:T(8,128)(2,1)} %get-tuple-element.111.first_ref.second_ref, bf16[2,1024,1408]{2,1,0:T(8,128)(2,1)} %get-tuple-element.111.first_ref.second_ref), custom_call_target="tpu_custom_call" | custom-call | flops 2952790016 | bytes 10000000 | tf_op jit(solution)/shard_map/product/pallas_call | solution.py:1108
  368.7 9.0 %product.15 = (bf16[2,256,1408]{2,1,0:T(8,128)(2,1)}, bf16[2,256,1408]{2,1,0:T(8,128)(2,1)}) custom-call(s32[4]{0:T(128)} %pad_add_fusion.flags_ref, bf16[8,2,64,1024]{3,2,1,0:T(8,128)(2,1)} %bitcast.233, bf16[2,1024,1408]{2,1,0:T(8,128)(2,1)} %get-tuple-element.105.first_ref.second_ref, bf16[2,1024,1408]{2,1,0:T(8,128)(2,1)} %get-tuple-element.105.first_ref.second_ref, ...), custom_call_target="tpu_custom_call" | custom-call | flops 2952790016 | bytes 10000000 | tf_op jit(solution)/shard_map/product/pallas_call | solution.py:1108
  384.0 4.0 copy.121
  389.9 7.7 %product.19 = (bf16[2,256,1024]{2,1,0:T(8,128)(2,1)}, bf16[2,256,1024]{2,1,0:T(8,128)(2,1)}) custom-call(s32[4]{0:T(128)} %pad_add_fusion.flags_ref, bf16[8,2,64,1024]{3,2,1,0:T(8,128)(2,1)} %bitcast.235, bf16[1024,1024]{1,0:T(8,128)(2,1)} %copy-done.1, bf16[1024,1024]{1,0:T(8,128)(2,1)} %copy-done, bf16[2,512,1024]{2,1,0:T(8,128)(2,1)} %bitcast.51.refs_0_), custom_call_target="tpu_custom_call" | custom-call | flops 2147483648 | bytes 10000000 | tf_op jit(solution)/shard_map/product/pallas_call | solution.py:1108
  399.8 4.4 fusion.15.grad_ref
  404.2 10.4 %collective-permute-done.4 = bf16[256,2816]{1,0:T(8,128)(2,1)} collective-permute-done((bf16[256,2816]{1,0:T(8,128)(2,1)}, bf16[256,2816]{1,0:T(8,128)(2,1)}, u32[]{:S(2)}, u32[]{:S(2)}) %collective-permute-start.4) | collective-permute-done | bytes 1441824 | tf_op jit(solution)/shard_map/ppermute | solution.py:1156
  418.2 9.2 %product.18 = (bf16[2,256,1408]{2,1,0:T(8,128)(2,1)}, bf16[2,256,1408]{2,1,0:T(8,128)(2,1)}) custom-call(s32[4]{0:T(128)} %pad_add_fusion.flags_ref, bf16[8,2,64,1024]{3,2,1,0:T(8,128)(2,1)} %bitcast.226, bf16[2,1024,1408]{2,1,0:T(8,128)(2,1)} %get-tuple-element.114.first_ref.second_ref, bf16[2,1024,1408]{2,1,0:T(8,128)(2,1)} %get-tuple-element.114.first_ref.second_ref, ...), custom_call_target="tpu_custom_call" | custom-call | flops 2952790016 | bytes 10000000 | tf_op jit(solution)/shard_map/product/pallas_call | solution.py:1108
  429.9 9.2 %product.17 = bf16[2,512,1408]{2,1,0:T(8,128)(2,1)} custom-call(s32[4]{0:T(128)} %pad_add_fusion.flags_ref, bf16[8,2,64,1024]{3,2,1,0:T(8,128)(2,1)} %bitcast.227, bf16[2,1024,1408]{2,1,0:T(8,128)(2,1)} %get-tuple-element.111.first_ref.second_ref, bf16[2,1024,1408]{2,1,0:T(8,128)(2,1)} %get-tuple-element.111.first_ref.second_ref, ...), custom_call_target="tpu_custom_call" | custom-call | flops 2952790016 | bytes 10000000 | tf_op jit(solution)/shard_map/product/pallas_call | solution.py:1108
  443.2 37.0 %mixer_backward.2 = (bf16[1,1024,3200]{2,1,0:T(8,128)(2,1)}, f32[1,8,2048]{2,1,0:T(8,128)S(1)}, f32[1,8,128]{2,1,0:T(8,128)S(1)}, f32[1,8,256]{2,1,0:T(8,128)S(1)}) custom-call(f32[1,1024,3200]{2,1,0:T(8,128)} %convolution_bitcast_fusion.1.proj_ref, f32[1024,128]{1,0:T(8,128)S(1)} %pad.54.info_ref, f32[1,8,2048]{2,1,0:T(8,128)S(1)} %get-tuple-element.293.conv_ref, ...), custom_call_target="tpu_custom_call" | custom-call | flops 40000000000 | bytes 100000000 | tf_op jit(solution)/shard_map/mixer_backward/pallas_call | solution.py:828
  480.2 10.0 %product.20 = bf16[1,512,3200]{2,1,0:T(8,128)(2,1)} custom-call(s32[4]{0:T(128)} %pad_add_fusion.flags_ref, bf16[8,2,64,1024]{3,2,1,0:T(8,128)(2,1)} %bitcast.228, bf16[1,1024,3200]{2,1,0:T(8,128)(2,1)} %get-tuple-element.150.first_ref.second_ref.refs_0_, bf16[1,1024,3200]{2,1,0:T(8,128)(2,1)} %get-tuple-element.150.first_ref.second_ref.refs_0_), custom_call_target="tpu_custom_call" | custom-call | flops 3355443200 | bytes 10000000 | tf_op jit(solution)/shard_map/product/pallas_call | solution.py:1108
  490.3 6.1 fusion.11.grad_ref
  509.2 10.5 %product.21 = (bf16[1,256,3200]{2,1,0:T(8,128)(2,1)}, bf16[1,256,3200]{2,1,0:T(8,128)(2,1)}) custom-call(s32[4]{0:T(128)} %pad_add_fusion.flags_ref, bf16[8,2,64,1024]{3,2,1,0:T(8,128)(2,1)} %bitcast.229, bf16[1,1024,3200]{2,1,0:T(8,128)(2,1)} %get-tuple-element.150.first_ref.second_ref.refs_0_, ...), custom_call_target="tpu_custom_call" | custom-call | flops 3355443200 | bytes 10000000 | tf_op jit(solution)/shard_map/product/pallas_call | solution.py:1108
  520.5 37.1 %mixer_backward.3 = (bf16[1,1024,3200]{2,1,0:T(8,128)(2,1)}, f32[1,8,2048]{2,1,0:T(8,128)S(1)}, f32[1,8,128]{2,1,0:T(8,128)S(1)}, f32[1,8,256]{2,1,0:T(8,128)S(1)}) custom-call(f32[1,1024,3200]{2,1,0:T(8,128)} %convolution_bitcast_fusion.proj_ref, f32[1024,128]{1,0:T(8,128)S(1)} %pad.54.info_ref, f32[1,8,2048]{2,1,0:T(8,128)S(1)} %get-tuple-element.294.conv_ref, ...), custom_call_target="tpu_custom_call" | custom-call | flops 40000000000 | bytes 100000000 | tf_op jit(solution)/shard_map/mixer_backward/pallas_call | solution.py:828
  557.6 9.3 %product.22 = bf16[1,512,3200]{2,1,0:T(8,128)(2,1)} custom-call(s32[4]{0:T(128)} %pad_add_fusion.flags_ref, bf16[8,2,64,1024]{3,2,1,0:T(8,128)(2,1)} %bitcast.230, bf16[1,1024,3200]{2,1,0:T(8,128)(2,1)} %get-tuple-element.151.first_ref.second_ref.refs_1_, bf16[1,1024,3200]{2,1,0:T(8,128)(2,1)} %get-tuple-element.151.first_ref.second_ref.refs_1_), custom_call_target="tpu_custom_call" | custom-call | flops 3355443200 | bytes 10000000 | tf_op jit(solution)/shard_map/product/pallas_call | solution.py:1108
  581.9 10.2 %product.23 = (bf16[1,256,3200]{2,1,0:T(8,128)(2,1)}, bf16[1,256,3200]{2,1,0:T(8,128)(2,1)}) custom-call(s32[4]{0:T(128)} %pad_add_fusion.flags_ref, bf16[8,2,64,1024]{3,2,1,0:T(8,128)(2,1)} %bitcast.231, bf16[1,1024,3200]{2,1,0:T(8,128)(2,1)} %get-tuple-element.151.first_ref.second_ref.refs_1_, ...), custom_call_target="tpu_custom_call" | custom-call | flops 3355443200 | bytes 10000000 | tf_op jit(solution)/shard_map/product/pallas_call | solution.py:1108
  592.7 25.9 %input_backward.1 = (f32[1024,1024]{1,0:T(8,128)}, f32[8,1024]{1,0:T(8,128)}) custom-call(s32[4]{0:T(128)} %pad_add_fusion.flags_ref, bf16[1,1024,3200]{2,1,0:T(8,128)(2,1)} %get-tuple-element.150.first_ref.second_ref.refs_0_, bf16[1,1024,3200]{2,1,0:T(8,128)(2,1)} %get-tuple-element.151.first_ref.second_ref.refs_1_, bf16[2,1024,3200]{2,1,0:T(8,128)(2,1)} %bitcast.289, ...), custom_call_target="tpu_custom_call" | custom-call | flops 40000000000 | bytes 100000000 | tf_op jit(solution)/shard_map/input_backward/pallas_call | solution.py:1023
  620.2 14.3 %collective-permute-done.14 = bf16[64,5248]{1,0:T(8,128)(2,1)S(1)} collective-permute-done((bf16[64,5248]{1,0:T(8,128)(2,1)S(1)}, bf16[64,5248]{1,0:T(8,128)(2,1)S(1)}, u32[]{:S(2)}, u32[]{:S(2)}) %collective-permute-start.14) | collective-permute-done | bytes 671776 | tf_op jit(solution)/shard_map/ppermute | solution.py:1161
  638.5 3.0 add_convert_fusion
  667.3 19.3 %collective-permute-done.23 = bf16[64,3200]{1,0:T(8,128)(2,1)S(1)} collective-permute-done((bf16[64,3200]{1,0:T(8,128)(2,1)}, bf16[64,3200]{1,0:T(8,128)(2,1)S(1)}, u32[]{:S(2)}, u32[]{:S(2)}) %collective-permute-start.23) | collective-permute-done | bytes 409632 | tf_op jit(solution)/shard_map/ppermute | solution.py:1161
  686.5 6.8 collective-permute-done.24
  (265 shorter events, 116.8 us)
Async XLA Ops:
  7.2 48.7 %copy-start.52 = (f32[8]{0:T(128)S(1)}, f32[8]{0:T(128)}, u32[]{:S(2)}) copy-start(f32[8]{0:T(128)} %param.37) | copy-start | bytes 100
  7.2 104.1 %all-gather.3.cloned.1.call-start = ((), (), s32[]{:S(2)}) async-start(), calls=%async_computation | async-start | bytes 13516800 | tf_op jit(solution)/shard_map/all_gather | solution.py:1142
  10.8 238.4 %all-gather.5.cloned.1.call-start = ((), (), s32[]{:S(2)}) async-start(), calls=%async_computation.1 | async-start | bytes 22167552 | tf_op jit(solution)/shard_map/all_gather | solution.py:1142
  55.6 55.7 %copy-start.47 = (f32[1024]{0:T(1024)S(1)}, f32[1024]{0:T(1024)}, u32[]{:S(2)}) copy-start(f32[1024]{0:T(1024)} %param.26) | copy-start | bytes 12292
  57.8 66.9 %copy-start.45 = (f32[1024]{0:T(1024)}, f32[1024]{0:T(1024)S(1)}, u32[]{:S(2)}) copy-start(f32[1024]{0:T(1024)S(1)} %add_rsqrt_fusion.1) | copy-start | bytes 12292
  164.4 87.4 %copy-start = (bf16[1024,1024]{1,0:T(8,128)(2,1)}, bf16[1024,1024]{1,0:T(8,128)(2,1)S(1)}, u32[]{:S(2)}) copy-start(bf16[1024,1024]{1,0:T(8,128)(2,1)S(1)} %get-tuple-element.96.second_ref) | copy-start | bytes 6291460
  304.7 63.9 %collective-permute-start = (bf16[1024,1408]{1,0:T(8,128)(2,1)}, bf16[1024,1408]{1,0:T(8,128)(2,1)}, u32[]{:S(2)}, u32[]{:S(2)}) collective-permute-start(bf16[1024,1408]{1,0:T(8,128)(2,1)} %bitcast.243), channel_id=1, source_target_pairs={{0,2},{2,0},{4,6},{6,4},{8,10},{10,8},{12,14},{14,12},{16,18},{18,... | collective-permute-start | bytes 8650760 | tf_op jit(solution)/shard_map/ppermute | solution.py:1156
  352.4 65.7 %collective-permute-start.2 = (bf16[1024,1408]{1,0:T(8,128)(2,1)}, bf16[1024,1408]{1,0:T(8,128)(2,1)}, u32[]{:S(2)}, u32[]{:S(2)}) collective-permute-start(bf16[1024,1408]{1,0:T(8,128)(2,1)} %bitcast.242), channel_id=1, source_target_pairs={{0,2},{2,0},{4,6},{6,4},{8,10},{10,8},{12,14},{14,12},{16,18},{18,... | collective-permute-start | bytes 8650760 | tf_op jit(solution)/shard_map/ppermute | solution.py:1156
  359.5 30.4 %collective-permute-start.3 = (bf16[1024,1024]{1,0:T(8,128)(2,1)}, bf16[1024,1024]{1,0:T(8,128)(2,1)}, u32[]{:S(2)}, u32[]{:S(2)}) collective-permute-start(bf16[1024,1024]{1,0:T(8,128)(2,1)} %bitcast.250), channel_id=1, source_target_pairs={{0,2},{2,0},{4,6},{6,4},{8,10},{10,8},{12,14},{14,12},{16,18},{18,... | collective-permute-start | bytes 6291464 | tf_op jit(solution)/shard_map/ppermute | solution.py:1156
  380.3 37.9 %collective-permute-start.1 = (bf16[1024,1408]{1,0:T(8,128)(2,1)}, bf16[1024,1408]{1,0:T(8,128)(2,1)}, u32[]{:S(2)}, u32[]{:S(2)}) collective-permute-start(bf16[1024,1408]{1,0:T(8,128)(2,1)} %bitcast.44), channel_id=1, source_target_pairs={{0,2},{2,0},{4,6},{6,4},{8,10},{10,8},{12,14},{14,12},{16,18},{18,... | collective-permute-start | bytes 8650760 | tf_op jit(solution)/shard_map/ppermute | solution.py:1156
  380.6 34.1 %collective-permute-start.4 = (bf16[256,2816]{1,0:T(8,128)(2,1)}, bf16[256,2816]{1,0:T(8,128)(2,1)}, u32[]{:S(2)}, u32[]{:S(2)}) collective-permute-start(bf16[256,2816]{1,0:T(8,128)(2,1)} %pad_maximum_fusion.1), channel_id=1, source_target_pairs={{0,4},{2,6},{4,0},{6,2},{8,12},{10,14},{12,8},{14,10},{16,20},{18,... | collective-permute-start | bytes 4325384 | tf_op jit(solution)/shard_map/ppermute | solution.py:1156
  416.9 79.5 %collective-permute-start.7 = (bf16[256,1408]{1,0:T(8,128)(2,1)}, bf16[256,1408]{1,0:T(8,128)(2,1)}, u32[]{:S(2)}, u32[]{:S(2)}) collective-permute-start(bf16[256,1408]{1,0:T(8,128)(2,1)} %fusion.29), channel_id=1, source_target_pairs={{0,1},{1,0},{2,3},{3,2},{4,5},{5,4},{6,7},{7,6},{8,9},{9,8},{10,11... | collective-permute-start | bytes 2162696 | tf_op jit(solution)/shard_map/ppermute | solution.py:1156
  429.1 67.3 %collective-permute-start.6 = (bf16[256,4864]{1,0:T(8,128)(2,1)S(1)}, bf16[256,4864]{1,0:T(8,128)(2,1)}, u32[]{:S(2)}, u32[]{:S(2)}) collective-permute-start(bf16[256,4864]{1,0:T(8,128)(2,1)S(1)} %pad_maximum_fusion), channel_id=1, source_target_pairs={{0,4},{2,6},{4,0},{6,2},{8,12},{10,14},{12,8},{14,10},{16,20},{18,... | collective-permute-start | bytes 7471112 | tf_op jit(solution)/shard_map/ppermute | solution.py:1156
  441.8 54.5 %collective-permute-start.5 = (bf16[512,1408]{1,0:T(8,128)(2,1)}, bf16[512,1408]{1,0:T(8,128)(2,1)}, u32[]{:S(2)}, u32[]{:S(2)}) collective-permute-start(bf16[512,1408]{1,0:T(8,128)(2,1)} %slice_bitcast_fusion.1), channel_id=1, source_target_pairs={{0,1},{1,0},{2,3},{3,2},{4,5},{5,4},{6,7},{7,6},{8,9},{9,8},{10,11... | collective-permute-start | bytes 4325384 | tf_op jit(solution)/shard_map/ppermute | solution.py:1156
  490.2 17.3 %collective-permute-start.8 = (bf16[512,3200]{1,0:T(8,128)(2,1)}, bf16[512,3200]{1,0:T(8,128)(2,1)S(1)}, u32[]{:S(2)}, u32[]{:S(2)}) collective-permute-start(bf16[512,3200]{1,0:T(8,128)(2,1)} %bitcast.241), channel_id=1, source_target_pairs={{0,2},{2,0},{4,6},{6,4},{8,10},{10,8},{12,14},{14,12},{16,18},{18,... | collective-permute-start | bytes 9830408 | tf_op jit(solution)/shard_map/ppermute | solution.py:1156
  500.3 67.1 %collective-permute-start.12 = (bf16[256,2432]{1,0:T(8,128)(2,1)}, bf16[256,2432]{1,0:T(8,128)(2,1)}, u32[]{:S(2)}, u32[]{:S(2)}) collective-permute-start(bf16[256,2432]{1,0:T(8,128)(2,1)} %pad_maximum_fusion.2), channel_id=1, source_target_pairs={{0,1},{1,0},{2,3},{3,2},{4,5},{5,4},{6,7},{7,6},{8,9},{9,8},{10,11... | collective-permute-start | bytes 3735560 | tf_op jit(solution)/shard_map/ppermute | solution.py:1156
  503.7 63.7 %collective-permute-start.11 = (bf16[256,1408]{1,0:T(8,128)(2,1)}, bf16[256,1408]{1,0:T(8,128)(2,1)S(1)}, u32[]{:S(2)}, u32[]{:S(2)}) collective-permute-start(bf16[256,1408]{1,0:T(8,128)(2,1)} %bitcast.57), channel_id=1, source_target_pairs={{0,4},{2,6},{4,0},{6,2},{8,12},{10,14},{12,8},{14,10},{16,20},{18,... | collective-permute-start | bytes 2162696 | tf_op jit(solution)/shard_map/ppermute | solution.py:1156
  519.7 58.9 %collective-permute-start.9 = (bf16[256,3200]{1,0:T(8,128)(2,1)}, bf16[256,3200]{1,0:T(8,128)(2,1)}, u32[]{:S(2)}, u32[]{:S(2)}) collective-permute-start(bf16[256,3200]{1,0:T(8,128)(2,1)} %bitcast.291), channel_id=1, source_target_pairs={{0,4},{2,6},{4,0},{6,2},{8,12},{10,14},{12,8},{14,10},{16,20},{18,... | collective-permute-start | bytes 4915208 | tf_op jit(solution)/shard_map/ppermute | solution.py:1156
  567.0 14.9 %collective-permute-start.13 = (bf16[512,3200]{1,0:T(8,128)(2,1)}, bf16[512,3200]{1,0:T(8,128)(2,1)}, u32[]{:S(2)}, u32[]{:S(2)}) collective-permute-start(bf16[512,3200]{1,0:T(8,128)(2,1)} %bitcast.239), channel_id=1, source_target_pairs={{0,2},{2,0},{4,6},{6,4},{8,10},{10,8},{12,14},{14,12},{16,18},{18,... | collective-permute-start | bytes 9830408 | tf_op jit(solution)/shard_map/ppermute | solution.py:1156
  573.1 45.5 %collective-permute-start.16 = (bf16[64,5248]{1,0:T(8,128)(2,1)S(1)}, bf16[64,5248]{1,0:T(8,128)(2,1)S(1)}, u32[]{:S(2)}, u32[]{:S(2)}) collective-permute-start(bf16[64,5248]{1,0:T(8,128)(2,1)S(1)} %pad_maximum_fusion.6), channel_id=1, source_target_pairs={{0,24},{2,26},{4,28},{6,30},{8,0},{10,2},{12,4},{14,6},{16,8},{18,... | collective-permute-start | bytes 2015240 | tf_op jit(solution)/shard_map/ppermute | solution.py:1161
  575.5 44.7 %collective-permute-start.15 = (bf16[64,5248]{1,0:T(8,128)(2,1)S(1)}, bf16[64,5248]{1,0:T(8,128)(2,1)S(1)}, u32[]{:S(2)}, u32[]{:S(2)}) collective-permute-start(bf16[64,5248]{1,0:T(8,128)(2,1)S(1)} %pad_maximum_fusion.5), channel_id=1, source_target_pairs={{0,16},{2,18},{4,20},{6,22},{8,24},{10,26},{12,28},{14,30},{16,0},... | collective-permute-start | bytes 2015240 | tf_op jit(solution)/shard_map/ppermute | solution.py:1161
  577.2 57.4 %collective-permute-start.14 = (bf16[64,5248]{1,0:T(8,128)(2,1)S(1)}, bf16[64,5248]{1,0:T(8,128)(2,1)S(1)}, u32[]{:S(2)}, u32[]{:S(2)}) collective-permute-start(bf16[64,5248]{1,0:T(8,128)(2,1)S(1)} %pad_maximum_fusion.4), channel_id=1, source_target_pairs={{0,8},{2,10},{4,12},{6,14},{8,16},{10,18},{12,20},{14,22},{16,24},... | collective-permute-start | bytes 2015240 | tf_op jit(solution)/shard_map/ppermute | solution.py:1161
  580.4 54.1 %collective-permute-start.10 = (bf16[256,3200]{1,0:T(8,128)(2,1)S(1)}, bf16[256,3200]{1,0:T(8,128)(2,1)}, u32[]{:S(2)}, u32[]{:S(2)}) collective-permute-start(bf16[256,3200]{1,0:T(8,128)(2,1)S(1)} %fusion.9), channel_id=1, source_target_pairs={{0,1},{1,0},{2,3},{3,2},{4,5},{5,4},{6,7},{7,6},{8,9},{9,8},{10,11... | collective-permute-start | bytes 4915208 | tf_op jit(solution)/shard_map/ppermute | solution.py:1156
  592.1 42.5 %collective-permute-start.17 = (bf16[256,3200]{1,0:T(8,128)(2,1)}, bf16[256,3200]{1,0:T(8,128)(2,1)}, u32[]{:S(2)}, u32[]{:S(2)}) collective-permute-start(bf16[256,3200]{1,0:T(8,128)(2,1)} %bitcast.292), channel_id=1, source_target_pairs={{0,4},{2,6},{4,0},{6,2},{8,12},{10,14},{12,8},{14,10},{16,20},{18,... | collective-permute-start | bytes 4915208 | tf_op jit(solution)/shard_map/ppermute | solution.py:1156
  636.9 4.6 collective-permute-start.18
  641.7 5.6 collective-permute-start.19
  647.4 1.3 collective-permute-start.20
  648.8 4.5 collective-permute-start.21
  653.3 8.6 %collective-permute-start.22 = (f32[1,19456]{1,0:T(1,128)S(1)}, f32[1,19456]{1,0:T(1,128)S(1)}, u32[]{:S(2)}, u32[]{:S(2)}) collective-permute-start(f32[1,19456]{1,0:T(1,128)S(1)} %add.309), channel_id=1, source_target_pairs={{0,1},{1,0},{2,3},{3,2},{4,5},{5,4},{6,7},{7,6},{8,9},{9,8},{10,11... | collective-permute-start | bytes 233480 | tf_op jit(solution)/shard_map/ppermute | solution.py:1156
  656.6 29.9 %collective-permute-start.23 = (bf16[64,3200]{1,0:T(8,128)(2,1)}, bf16[64,3200]{1,0:T(8,128)(2,1)S(1)}, u32[]{:S(2)}, u32[]{:S(2)}) collective-permute-start(bf16[64,3200]{1,0:T(8,128)(2,1)} %get-tuple-element.158), channel_id=1, source_target_pairs={{0,8},{2,10},{4,12},{6,14},{8,16},{10,18},{12,20},{14,22},{16,24},... | collective-permute-start | bytes 1228808 | tf_op jit(solution)/shard_map/ppermute | solution.py:1161
  658.7 34.6 %collective-permute-start.24 = (bf16[64,3200]{1,0:T(8,128)(2,1)}, bf16[64,3200]{1,0:T(8,128)(2,1)S(1)}, u32[]{:S(2)}, u32[]{:S(2)}) collective-permute-start(bf16[64,3200]{1,0:T(8,128)(2,1)} %get-tuple-element.159), channel_id=1, source_target_pairs={{0,16},{2,18},{4,20},{6,22},{8,24},{10,26},{12,28},{14,30},{16,0},... | collective-permute-start | bytes 1228808 | tf_op jit(solution)/shard_map/ppermute | solution.py:1161
  660.9 34.6 %collective-permute-start.25 = (bf16[64,3200]{1,0:T(8,128)(2,1)}, bf16[64,3200]{1,0:T(8,128)(2,1)S(1)}, u32[]{:S(2)}, u32[]{:S(2)}) collective-permute-start(bf16[64,3200]{1,0:T(8,128)(2,1)} %get-tuple-element.160), channel_id=1, source_target_pairs={{0,24},{2,26},{4,28},{6,30},{8,0},{10,2},{12,4},{14,6},{16,8},{18,... | collective-permute-start | bytes 1228808 | tf_op jit(solution)/shard_map/ppermute | solution.py:1161
  (50 other events, 546.4 us)
Sparse Core Ops, SparseCore 0:
  11.5 99.7 all-gather.2
  114.8 134.3 all-gather.4

commit v4 on v3

--- a/solution.py
+++ b/solution.py
@@ -388,6 +388,7 @@
 TENSOR_FIRST = (CORE, TENSOR, SIDE, PLACE)
 SIDE_FIRST = (CORE, SIDE, TENSOR, PLACE)
 TILE = 128
+DONE = object()
 COST = 4 * 10**10
 
 
@@ -639,7 +640,7 @@
         for j in range(4):
             grad_conv_ref[0, j : j + 1, lanes] += sums[j]
 
-    for head in range(heads):
+    def head_steps(head):
         lanes = slice(2 * head * TILE, 2 * (head + 1) * TILE)
         gate_lanes = slice((4 * heads + 2 * head) * TILE, (4 * heads + 2 * (head + 1)) * TILE)
         rows = rows_ref[0, :, lanes]
@@ -649,7 +650,7 @@
         level = rows * scale
         sigmoid = jax.nn.sigmoid(gate)
         through = grad * (gate * sigmoid)
-        gain_sum = gain_sum + jnp.sum(through * level, axis=0, keepdims=True)
+        gain_sums.append(jnp.sum(through * level, axis=0, keepdims=True))
         grad_proj_ref[0, :, gate_lanes] = (
             grad * level * gain * (sigmoid * (1.0 + gate * (1.0 - sigmoid)))
         ).astype(jnp.bfloat16)
@@ -658,6 +659,7 @@
             through - level * jnp.mean(through * level, axis=1, keepdims=True)
         )
 
+        yield
         query_act, query_slope = activation(head)
         query_scale = lax.rsqrt(jnp.sum(query_act * query_act, axis=1, keepdims=True) + 1e-06)
         query_unit = query_act * query_scale
@@ -668,6 +670,7 @@
         value_parts = [activation(2 * heads + 2 * head), activation(2 * heads + 2 * head + 1)]
         value = jnp.concatenate([value_parts[0][0], value_parts[1][0]], axis=1)
 
+        yield
         spread = total[:, head : head + 1] - total_rows[head : head + 1, :]
         weights = jnp.exp(jnp.where(visible, spread, -1e30))
         beta = beta_tile[:, heads + head : heads + head + 1]
@@ -675,6 +678,7 @@
         key_low, query_low = key.astype(jnp.bfloat16), query.astype(jnp.bfloat16)
         both = jnp.concatenate([key_low, query_low], axis=0)
         grams = mm_nt(both, key_low)
+        yield
         state_low = state_in_ref[0, 0, head]
         inverse = inverse_ref[0, 0, head]
         pseudo = pseudo_ref[0, :, lanes]
@@ -686,10 +690,13 @@
         grad_pseudo = mm_tn(grams[TILE:] * weights, grad_rows_low) + mm(
             last_col * key, grad_state_low
         )
+        yield
         solved = mm_tn(inverse, grad_pseudo)
+        yield
         crossed = mm_nt(
             jnp.concatenate([grad_rows_low, solved.astype(jnp.bfloat16)], axis=0), pseudo
         )
+        yield
         grad_scores = crossed[:TILE] * weights
         below = jnp.where(row > col, crossed[TILE:] * weights, 0.0)
         grad_gram = (-beta) * below
@@ -698,10 +705,12 @@
         grad_beta_col = jnp.sum(
             solved * (value - carried * from_state), axis=1, keepdims=True
         ) - jnp.sum(below * grams[:TILE], axis=1, keepdims=True)
+        yield
         out_part = (carried * grad_rows).astype(jnp.bfloat16)
         key_part = ((-carried) * grad_value).astype(jnp.bfloat16)
         stacked = jnp.concatenate([out_part, key_part], axis=0)
         to_inputs = mm_nt(stacked, state_low)
+        yield
         scores_low, gram_low = grad_scores.astype(jnp.bfloat16), grad_gram.astype(jnp.bfloat16)
         grad_query = mm(scores_low, key_low) + to_inputs[:TILE]
         key_own = mm(gram_low, key_low) + to_inputs[TILE:]
@@ -713,6 +722,7 @@
         grad_state_ref[head] = carried[TILE - 1 : TILE, :] * grad_state + mm_tn(
             jnp.concatenate([query_low, key_low], axis=0), stacked
         )
+        yield
         key_exact, query_exact = key_low.astype(jnp.float32), query_low.astype(jnp.float32)
         state_dot = jnp.sum(key_state * key_exact, axis=1, keepdims=True)
         tail = jnp.sum(state_dot, axis=0, keepdims=True) + carried[TILE - 1 : TILE, :] * jnp.sum(
@@ -727,8 +737,8 @@
             - state_dot
             + jnp.where(row[:, 0:1] == TILE - 1, tail, 0.0)
         )
-        grad_total = jnp.where(col == head, grad_total_col, grad_total)
-        grad_beta = jnp.where(col == heads + head, grad_beta_col, grad_beta)
+        columns_of[head] = (grad_total_col, grad_beta_col)
+        yield
 
         grad_query = grad_query * TILE ** (-0.5)
         close_block(
@@ -740,14 +750,25 @@
             )
             * query_slope,
         )
+        yield
         close_block(
             heads + head,
             key_scale
             * (grad_key - key * jnp.sum(grad_key * key, axis=1, keepdims=True))
             * key_slope,
         )
+        yield
         close_block(2 * heads + 2 * head, grad_value[:, :TILE] * value_parts[0][1])
         close_block(2 * heads + 2 * head + 1, grad_value[:, TILE:] * value_parts[1][1])
+
+    gain_sums, columns_of = [], {}
+    waiting = [head_steps(head) for head in range(heads)]
+    while waiting:
+        waiting = [steps for steps in waiting if next(steps, DONE) is not DONE]
+    for head in range(heads):
+        grad_total = jnp.where(col == head, columns_of[head][0], grad_total)
+        grad_beta = jnp.where(col == heads + head, columns_of[head][1], grad_beta)
+        gain_sum = gain_sum + gain_sums[head]
 
     grad_log = ones_mm((row <= col).astype(jnp.float32), grad_total)
     grad_raw = -rate * grad_log * jax.nn.sigmoid(shifted)
@@ -1425,15 +1446,15 @@
     ]
     cores.land()
     out_cores.land()
-    first_down.land()
-    middle = Transfer(gate, up, out, down)
+    middle = Transfer(gate, up, out)
     ready = after(grad_mixed[0], middle.packed)
     per_part = [mixer_backward(*mixer_args[0], saved[0], ready, heads)]
     turned = normed.T
     theirs = Scatter(flags, turned, [per_part[0][0]], (CORE, SIDE))
     theirs_cores = Transfer(theirs)
     middle.land()
-    middle = Transfer(gate, up, out)
+    first_down.land()
+    middle = Transfer(gate, up, out, down)
     theirs.left = after(theirs.left, middle.packed)
     theirs_cores.land()
     theirs_side = Transfer(theirs)

time: 715 us -> 700 us (0.979)
  starting transfers between devices: 28.6 us -> 20.9 us
    ppermute x20 -> x19, starting transfers between devices: 17.8 us -> 11.9 us  [exchange(): return lax.ppermute(array, axis, [(i, i ^ bit) for i in range(size)])]
    convert_element_type x10 -> x9, other arithmetic: 18.4 us -> 16.4 us  [add_low(): (left.astype(jnp.float32) + right.astype(jnp.float32)).astype(jnp.bfloat16)]
    unnamed x115 -> x103, local copies, waits for them, and re-layouts: 13.6 us -> 14.5 us
  transfers between devices with their start and end apart: 28 -> 27, of which waited for: 11 -> 11; matrix products, arithmetic and copies ran while one was open for 13% -> 13% of each run, Pallas kernels for 41% -> 42%
where the time goes in v4:
time: 700 us; the launch traced here: 692 us
  Pallas kernels  329 us (47%)
  waiting for transfers between devices  159 us (23%)
  local copies, waits for them, and re-layouts  45.3 us (6%)
  matrix products  41.4 us (6%)
  blocking collectives  41 us (6%)
  other arithmetic  37.1 us (5%)
  starting transfers between devices  20.9 us (3%)
  between operations  18.4 us (3%)
    pallas_call x12, Pallas kernels, product(): pl.pallas_call(functools.partial(product_body, own, side_first), grid_spe...  107 us
    all_gather x2, waiting for transfers between devices, gather_all(): rows = lax.all_gather(local, (TP, DP), axis=0, tiled=True)  107 us
    pallas_call x3, Pallas kernels, dense_call(): pl.pallas_call(lambda flags_ref, *refs: body(*refs), grid_spec=pltpu.Pref...  95.2 us
    pallas_call x2, Pallas kernels, mixer_backward(): pl.pallas_call(functools.partial(backward_body, heads), grid=(parts, rows...  71.5 us
    pallas_call x2, Pallas kernels, mixer_forward(): pl.pallas_call(functools.partial(forward_body, heads), grid=(parts, rows...  54.8 us
    ppermute x6, waiting for transfers between devices, shift(): lax.ppermute(array, DP, [(i, (i + step) % size) for i in range(size)])  44.7 us
    psum x1, blocking collectives, on_device_whole(): count = lax.psum(jnp.sum(live), (DP, TP))  41 us
    dot_general x2, matrix products, on_device_whole(): jnp.dot(normed, pick(proj_all, part, 0), preferred_element_type=jnp.float32)  23.8 us
  transfers between devices with their start and end apart: 27, of which 11 were waited for; matrix products, arithmetic and copies ran while one was open for 13% of the time, Pallas kernels for 42%

profile of v4, /device:TPU:8, one launch (start us, length us, event | category | flops | bytes accessed | tf_op | source)
XLA Modules:
  0.0 691.7 jit_solution(17661595961295730328)
XLA Ops:
  13.7 41.0 %psum.7 = f32[]{:T(128)} all-reduce(f32[]{:T(128)} %convert_reduce_fusion), channel_id=1, replica_groups=mesh['dp'=16,'tensor'=2] {'dp','tensor'}, use_global_device_ids=true, to_apply=%region_3.4 | all-reduce | flops 1 | bytes 8 | tf_op jit(solution)/shard_map/psum | solution.py:1359
  57.9 53.4 %all-gather.3.cloned.1.call-done = bf16[2048,3200]{1,0:T(8,128)(2,1)} async-done(((bf16[64,3200]{1,0:T(8,128)(2,1)}), bf16[2048,3200]{1,0:T(8,128)(2,1)}) %all-gather.3.cloned.1.call-update) | async-done | bytes 13107216 | tf_op jit(solution)/shard_map/all_gather | solution.py:1163
  111.3 13.4 %convolution_bitcast_fusion.proj_ref = f32[1,1024,3200]{2,1,0:T(8,128)} fusion(bf16[2,1024,3200]{2,1,0:T(8,128)(2,1)} %bitcast.288, s32[]{:T(128)S(6)} %select_n.141, bf16[1024,1024]{1,0:T(8,128)(2,1)S(1)} %copy-done.16, f32[1024]{0:T(1024)S(1)} %copy-done.40, f32[1024]{0:T(1024)S(1)} %add_rsqrt_fusion.1), kind=kOutput, calls=%fused_computation | convolution fusion | flops 6715080704 | bytes 21766148 | tf_op jit(solution)/shard_map/dot_general | solution.py:1367
  124.8 10.3 %convolution_bitcast_fusion.1.proj_ref = f32[1,1024,3200]{2,1,0:T(8,128)} fusion(bf16[2,1024,3200]{2,1,0:T(8,128)(2,1)S(1)} %bitcast.290, s32[]{:T(128)S(6)} %select_n.139, bf16[1024,1024]{1,0:T(8,128)(2,1)S(1)} %copy-done.16, f32[1024]{0:T(1024)S(1)} %copy-done.40, f32[1024]{0:T(1024)S(1)} %add_rsqrt_fusion.1), kind=kOutput, calls=%fused_computation.1 | convolution fusion | flops 6715080704 | bytes 21766148 | tf_op jit(solution)/shard_map/dot_general | solution.py:1367
  135.1 27.0 %mixer_forward.3 = (bf16[1024,1024]{1,0:T(8,128)(2,1)S(1)}, f32[1,1024,2048]{2,1,0:T(8,128)}, f32[1,1024,1024]{2,1,0:T(8,128)}, bf16[1,8,4,128,256]{4,3,2,1,0:T(...) custom-call(f32[1,1024,3200]{2,1,0:T(8,128)} %convolution_bitcast_fusion.proj_ref, ...), custom_call_target="tpu_custom_call" | custom-call | flops 40000000000 | bytes 100000000 | tf_op jit(solution)/shard_map/mixer_forward/pallas_call | solution.py:816
  164.4 27.8 %mixer_forward.2 = (bf16[1024,1024]{1,0:T(8,128)(2,1)S(1)}, f32[1,1024,2048]{2,1,0:T(8,128)}, f32[1,1024,1024]{2,1,0:T(8,128)}, bf16[1,8,4,128,256]{4,3,2,1,0:T(...) custom-call(f32[1,1024,3200]{2,1,0:T(8,128)} %convolution_bitcast_fusion.1.proj_ref, ...), custom_call_target="tpu_custom_call" | custom-call | flops 40000000000 | bytes 100000000 | tf_op jit(solution)/shard_map/mixer_forward/pallas_call | solution.py:816
  195.9 53.3 %all-gather.5.cloned.1.call-done = bf16[2048,5248]{1,0:T(8,128)(2,1)} async-done(((bf16[64,5248]{1,0:T(8,128)(2,1)}), bf16[2048,5248]{1,0:T(8,128)(2,1)}) %all-gather.5.cloned.1.call-update) | async-done | bytes 21495824 | tf_op jit(solution)/shard_map/all_gather | solution.py:1163
  262.9 33.0 %dense_forward.1 = (bf16[2,1024,1408]{2,1,0:T(8,128)(2,1)}, bf16[2,1024,1408]{2,1,0:T(8,128)(2,1)}, bf16[2,1024,1408]{2,1,0:T(8,128)(2,1)}, f32[1024,1024]{1,0:T...) custom-call(s32[4]{0:T(128)} %pad_add_fusion.flags_ref, ...), custom_call_target="tpu_custom_call" | custom-call | flops 40000000000 | bytes 100000000 | tf_op jit(solution)/shard_map/dense_forward/pallas_call | solution.py:1044
  295.9 8.7 %product.12 = bf16[2,512,1408]{2,1,0:T(8,128)(2,1)} custom-call(s32[4]{0:T(128)} %pad_add_fusion.flags_ref, bf16[8,2,64,1024]{3,2,1,0:T(8,128)(2,1)} %bitcast.232, bf16[2,1024,1408]{2,1,0:T(8,128)(2,1)} %get-tuple-element.104.first_ref.second_ref, bf16[2,1024,1408]{2,1,0:T(8,128)(2,1)} %get-tuple-element.104.first_ref.second_ref), custom_call_target="tpu_custom_call" | custom-call | flops 2952790016 | bytes 10000000 | tf_op jit(solution)/shard_map/product/pallas_call | solution.py:1129
  307.4 36.4 %dense_backward.1 = (bf16[2,1024,1408]{2,1,0:T(8,128)(2,1)}, bf16[2,1024,1408]{2,1,0:T(8,128)(2,1)}, f32[1024,1024]{1,0:T(8,128)}, bf16[1024,1024]{1,0:T(8,128)(...) custom-call(s32[4]{0:T(128)} %pad_add_fusion.flags_ref, bf16[1024,1024]{1,0:T(8,128)(2,1)} %get-tuple-element.105.refs_0_, ...), custom_call_target="tpu_custom_call" | custom-call | flops 40000000000 | bytes 100000000 | tf_op jit(solution)/shard_map/dense_backward/pallas_call | solution.py:1044
  343.8 8.5 %product.16 = bf16[2,512,1408]{2,1,0:T(8,128)(2,1)} custom-call(s32[4]{0:T(128)} %pad_add_fusion.flags_ref, bf16[8,2,64,1024]{3,2,1,0:T(8,128)(2,1)} %bitcast.224, bf16[2,1024,1408]{2,1,0:T(8,128)(2,1)} %get-tuple-element.113.first_ref.second_ref, bf16[2,1024,1408]{2,1,0:T(8,128)(2,1)} %get-tuple-element.113.first_ref.second_ref), custom_call_target="tpu_custom_call" | custom-call | flops 2952790016 | bytes 10000000 | tf_op jit(solution)/shard_map/product/pallas_call | solution.py:1129
  352.6 6.8 product.13
  359.6 8.9 %product.14 = bf16[2,512,1408]{2,1,0:T(8,128)(2,1)} custom-call(s32[4]{0:T(128)} %pad_add_fusion.flags_ref, bf16[8,2,64,1024]{3,2,1,0:T(8,128)(2,1)} %bitcast.225, bf16[2,1024,1408]{2,1,0:T(8,128)(2,1)} %get-tuple-element.110.first_ref.second_ref, bf16[2,1024,1408]{2,1,0:T(8,128)(2,1)} %get-tuple-element.110.first_ref.second_ref), custom_call_target="tpu_custom_call" | custom-call | flops 2952790016 | bytes 10000000 | tf_op jit(solution)/shard_map/product/pallas_call | solution.py:1129
  368.5 9.0 %product.15 = (bf16[2,256,1408]{2,1,0:T(8,128)(2,1)}, bf16[2,256,1408]{2,1,0:T(8,128)(2,1)}) custom-call(s32[4]{0:T(128)} %pad_add_fusion.flags_ref, bf16[8,2,64,1024]{3,2,1,0:T(8,128)(2,1)} %bitcast.233, bf16[2,1024,1408]{2,1,0:T(8,128)(2,1)} %get-tuple-element.104.first_ref.second_ref, bf16[2,1024,1408]{2,1,0:T(8,128)(2,1)} %get-tuple-element.104.first_ref.second_ref, ...), custom_call_target="tpu_custom_call" | custom-call | flops 2952790016 | bytes 10000000 | tf_op jit(solution)/shard_map/product/pallas_call | solution.py:1129
  384.2 7.7 %product.19 = (bf16[2,256,1024]{2,1,0:T(8,128)(2,1)}, bf16[2,256,1024]{2,1,0:T(8,128)(2,1)}) custom-call(s32[4]{0:T(128)} %pad_add_fusion.flags_ref, bf16[8,2,64,1024]{3,2,1,0:T(8,128)(2,1)} %bitcast.235, bf16[1024,1024]{1,0:T(8,128)(2,1)} %copy-done.1, bf16[1024,1024]{1,0:T(8,128)(2,1)} %copy-done, bf16[2,512,1024]{2,1,0:T(8,128)(2,1)} %bitcast.51.refs_0_), custom_call_target="tpu_custom_call" | custom-call | flops 2147483648 | bytes 10000000 | tf_op jit(solution)/shard_map/product/pallas_call | solution.py:1129
  395.1 6.0 fusion.15.grad_ref
  401.1 9.1 %product.17 = bf16[2,512,1408]{2,1,0:T(8,128)(2,1)} custom-call(s32[4]{0:T(128)} %pad_add_fusion.flags_ref, bf16[8,2,64,1024]{3,2,1,0:T(8,128)(2,1)} %bitcast.226, bf16[2,1024,1408]{2,1,0:T(8,128)(2,1)} %get-tuple-element.110.first_ref.second_ref, bf16[2,1024,1408]{2,1,0:T(8,128)(2,1)} %get-tuple-element.110.first_ref.second_ref, ...), custom_call_target="tpu_custom_call" | custom-call | flops 2952790016 | bytes 10000000 | tf_op jit(solution)/shard_map/product/pallas_call | solution.py:1129
  412.8 9.1 %product.18 = (bf16[2,256,1408]{2,1,0:T(8,128)(2,1)}, bf16[2,256,1408]{2,1,0:T(8,128)(2,1)}) custom-call(s32[4]{0:T(128)} %pad_add_fusion.flags_ref, bf16[8,2,64,1024]{3,2,1,0:T(8,128)(2,1)} %bitcast.227, bf16[2,1024,1408]{2,1,0:T(8,128)(2,1)} %get-tuple-element.113.first_ref.second_ref, bf16[2,1024,1408]{2,1,0:T(8,128)(2,1)} %get-tuple-element.113.first_ref.second_ref, ...), custom_call_target="tpu_custom_call" | custom-call | flops 2952790016 | bytes 10000000 | tf_op jit(solution)/shard_map/product/pallas_call | solution.py:1129
  427.2 35.8 %mixer_backward.2 = (bf16[1,1024,3200]{2,1,0:T(8,128)(2,1)}, f32[1,8,2048]{2,1,0:T(8,128)S(1)}, f32[1,8,128]{2,1,0:T(8,128)S(1)}, f32[1,8,256]{2,1,0:T(8,128)S(1)}) custom-call(f32[1,1024,3200]{2,1,0:T(8,128)} %convolution_bitcast_fusion.1.proj_ref, f32[1024,128]{1,0:T(8,128)S(1)} %pad.54.info_ref, f32[1,8,2048]{2,1,0:T(8,128)S(1)} %get-tuple-element.293.conv_ref, ...), custom_call_target="tpu_custom_call" | custom-call | flops 40000000000 | bytes 100000000 | tf_op jit(solution)/shard_map/mixer_backward/pallas_call | solution.py:849
  462.9 9.8 %product.20 = bf16[1,512,3200]{2,1,0:T(8,128)(2,1)} custom-call(s32[4]{0:T(128)} %pad_add_fusion.flags_ref, bf16[8,2,64,1024]{3,2,1,0:T(8,128)(2,1)} %bitcast.228, bf16[1,1024,3200]{2,1,0:T(8,128)(2,1)} %get-tuple-element.148.first_ref.second_ref.refs_0_, bf16[1,1024,3200]{2,1,0:T(8,128)(2,1)} %get-tuple-element.148.first_ref.second_ref.refs_0_), custom_call_target="tpu_custom_call" | custom-call | flops 3355443200 | bytes 10000000 | tf_op jit(solution)/shard_map/product/pallas_call | solution.py:1129
  474.3 6.7 fusion.11.grad_ref
  491.1 10.5 %product.21 = (bf16[1,256,3200]{2,1,0:T(8,128)(2,1)}, bf16[1,256,3200]{2,1,0:T(8,128)(2,1)}) custom-call(s32[4]{0:T(128)} %pad_add_fusion.flags_ref, bf16[8,2,64,1024]{3,2,1,0:T(8,128)(2,1)} %bitcast.229, bf16[1,1024,3200]{2,1,0:T(8,128)(2,1)} %get-tuple-element.148.first_ref.second_ref.refs_0_, ...), custom_call_target="tpu_custom_call" | custom-call | flops 3355443200 | bytes 10000000 | tf_op jit(solution)/shard_map/product/pallas_call | solution.py:1129
  503.1 35.7 %mixer_backward.3 = (bf16[1,1024,3200]{2,1,0:T(8,128)(2,1)}, f32[1,8,2048]{2,1,0:T(8,128)S(1)}, f32[1,8,128]{2,1,0:T(8,128)S(1)}, f32[1,8,256]{2,1,0:T(8,128)S(1)}) custom-call(f32[1,1024,3200]{2,1,0:T(8,128)} %convolution_bitcast_fusion.proj_ref, f32[1024,128]{1,0:T(8,128)S(1)} %pad.54.info_ref, f32[1,8,2048]{2,1,0:T(8,128)S(1)} %get-tuple-element.294.conv_ref, ...), custom_call_target="tpu_custom_call" | custom-call | flops 40000000000 | bytes 100000000 | tf_op jit(solution)/shard_map/mixer_backward/pallas_call | solution.py:849
  540.8 9.3 %product.22 = bf16[1,512,3200]{2,1,0:T(8,128)(2,1)} custom-call(s32[4]{0:T(128)} %pad_add_fusion.flags_ref, bf16[8,2,64,1024]{3,2,1,0:T(8,128)(2,1)} %bitcast.230, bf16[1,1024,3200]{2,1,0:T(8,128)(2,1)} %get-tuple-element.149.first_ref.second_ref.refs_1_, bf16[1,1024,3200]{2,1,0:T(8,128)(2,1)} %get-tuple-element.149.first_ref.second_ref.refs_1_), custom_call_target="tpu_custom_call" | custom-call | flops 3355443200 | bytes 10000000 | tf_op jit(solution)/shard_map/product/pallas_call | solution.py:1129
  568.7 10.0 %product.23 = (bf16[1,256,3200]{2,1,0:T(8,128)(2,1)}, bf16[1,256,3200]{2,1,0:T(8,128)(2,1)}) custom-call(s32[4]{0:T(128)} %pad_add_fusion.flags_ref, bf16[8,2,64,1024]{3,2,1,0:T(8,128)(2,1)} %bitcast.231, bf16[1,1024,3200]{2,1,0:T(8,128)(2,1)} %get-tuple-element.149.first_ref.second_ref.refs_1_, ...), custom_call_target="tpu_custom_call" | custom-call | flops 3355443200 | bytes 10000000 | tf_op jit(solution)/shard_map/product/pallas_call | solution.py:1129
  580.0 25.9 %input_backward.1 = (f32[1024,1024]{1,0:T(8,128)}, f32[8,1024]{1,0:T(8,128)}) custom-call(s32[4]{0:T(128)} %pad_add_fusion.flags_ref, bf16[1,1024,3200]{2,1,0:T(8,128)(2,1)} %get-tuple-element.148.first_ref.second_ref.refs_0_, bf16[1,1024,3200]{2,1,0:T(8,128)(2,1)} %get-tuple-element.149.first_ref.second_ref.refs_1_, bf16[2,1024,3200]{2,1,0:T(8,128)(2,1)} %bitcast.289, ...), custom_call_target="tpu_custom_call" | custom-call | flops 40000000000 | bytes 100000000 | tf_op jit(solution)/shard_map/input_backward/pallas_call | solution.py:1044
  605.9 13.0 %collective-permute-done.14 = bf16[64,5248]{1,0:T(8,128)(2,1)} collective-permute-done((bf16[64,5248]{1,0:T(8,128)(2,1)}, bf16[64,5248]{1,0:T(8,128)(2,1)}, u32[]{:S(2)}, u32[]{:S(2)}) %collective-permute-start.14) | collective-permute-done | bytes 671776 | tf_op jit(solution)/shard_map/ppermute | solution.py:1182
  629.4 3.8 collective-permute-done.18
  641.9 4.2 collective-permute-start.23
  651.3 3.2 collective-permute-done.22
  654.5 22.3 %collective-permute-done.23 = bf16[64,3200]{1,0:T(8,128)(2,1)S(1)} collective-permute-done((bf16[64,3200]{1,0:T(8,128)(2,1)}, bf16[64,3200]{1,0:T(8,128)(2,1)S(1)}, u32[]{:S(2)}, u32[]{:S(2)}) %collective-permute-start.23) | collective-permute-done | bytes 409632 | tf_op jit(solution)/shard_map/ppermute | solution.py:1182
  676.8 3.4 collective-permute-done.24
  (250 shorter events, 110.2 us)
Async XLA Ops:
  7.2 104.1 %all-gather.3.cloned.1.call-start = ((), (), s32[]{:S(2)}) async-start(), calls=%async_computation | async-start | bytes 13516800 | tf_op jit(solution)/shard_map/all_gather | solution.py:1163
  8.0 47.7 %copy-start.46 = (f32[8]{0:T(128)S(1)}, f32[8]{0:T(128)}, u32[]{:S(2)}) copy-start(f32[8]{0:T(128)} %param.37) | copy-start | bytes 100
  8.0 47.8 %copy-start.47 = (f32[8]{0:T(128)S(1)}, f32[8]{0:T(128)}, u32[]{:S(2)}) copy-start(f32[8]{0:T(128)} %param.36) | copy-start | bytes 100
  10.8 238.4 %all-gather.5.cloned.1.call-start = ((), (), s32[]{:S(2)}) async-start(), calls=%async_computation.1 | async-start | bytes 22167552 | tf_op jit(solution)/shard_map/all_gather | solution.py:1163
  55.6 55.7 %copy-start.40 = (f32[1024]{0:T(1024)S(1)}, f32[1024]{0:T(1024)}, u32[]{:S(2)}) copy-start(f32[1024]{0:T(1024)} %param.26) | copy-start | bytes 12292
  57.8 66.9 %copy-start.37 = (f32[1024]{0:T(1024)}, f32[1024]{0:T(1024)S(1)}, u32[]{:S(2)}) copy-start(f32[1024]{0:T(1024)S(1)} %add_rsqrt_fusion.1) | copy-start | bytes 12292
  164.4 87.4 %copy-start = (bf16[1024,1024]{1,0:T(8,128)(2,1)}, bf16[1024,1024]{1,0:T(8,128)(2,1)S(1)}, u32[]{:S(2)}) copy-start(bf16[1024,1024]{1,0:T(8,128)(2,1)S(1)} %get-tuple-element.95.second_ref) | copy-start | bytes 6291460
  304.6 63.9 %collective-permute-start = (bf16[1024,1408]{1,0:T(8,128)(2,1)}, bf16[1024,1408]{1,0:T(8,128)(2,1)}, u32[]{:S(2)}, u32[]{:S(2)}) collective-permute-start(bf16[1024,1408]{1,0:T(8,128)(2,1)} %bitcast.243), channel_id=1, source_target_pairs={{0,2},{2,0},{4,6},{6,4},{8,10},{10,8},{12,14},{14,12},{16,18},{18,... | collective-permute-start | bytes 8650760 | tf_op jit(solution)/shard_map/ppermute | solution.py:1177
  352.3 48.8 %collective-permute-start.2 = (bf16[1024,1408]{1,0:T(8,128)(2,1)}, bf16[1024,1408]{1,0:T(8,128)(2,1)}, u32[]{:S(2)}, u32[]{:S(2)}) collective-permute-start(bf16[1024,1408]{1,0:T(8,128)(2,1)} %bitcast.242), channel_id=1, source_target_pairs={{0,2},{2,0},{4,6},{6,4},{8,10},{10,8},{12,14},{14,12},{16,18},{18,... | collective-permute-start | bytes 8650760 | tf_op jit(solution)/shard_map/ppermute | solution.py:1177
  359.4 24.8 %collective-permute-start.3 = (bf16[1024,1024]{1,0:T(8,128)(2,1)}, bf16[1024,1024]{1,0:T(8,128)(2,1)}, u32[]{:S(2)}, u32[]{:S(2)}) collective-permute-start(bf16[1024,1024]{1,0:T(8,128)(2,1)} %bitcast.250), channel_id=1, source_target_pairs={{0,2},{2,0},{4,6},{6,4},{8,10},{10,8},{12,14},{14,12},{16,18},{18,... | collective-permute-start | bytes 6291464 | tf_op jit(solution)/shard_map/ppermute | solution.py:1177
  380.2 20.8 %collective-permute-start.1 = (bf16[1024,1408]{1,0:T(8,128)(2,1)}, bf16[1024,1408]{1,0:T(8,128)(2,1)}, u32[]{:S(2)}, u32[]{:S(2)}) collective-permute-start(bf16[1024,1408]{1,0:T(8,128)(2,1)} %bitcast.44), channel_id=1, source_target_pairs={{0,2},{2,0},{4,6},{6,4},{8,10},{10,8},{12,14},{14,12},{16,18},{18,... | collective-permute-start | bytes 8650760 | tf_op jit(solution)/shard_map/ppermute | solution.py:1177
  393.6 87.4 %collective-permute-start.6 = (bf16[256,2816]{1,0:T(8,128)(2,1)S(1)}, bf16[256,2816]{1,0:T(8,128)(2,1)}, u32[]{:S(2)}, u32[]{:S(2)}) collective-permute-start(bf16[256,2816]{1,0:T(8,128)(2,1)S(1)} %copy-done.26), channel_id=1, source_target_pairs={{0,4},{2,6},{4,0},{6,2},{8,12},{10,14},{12,8},{14,10},{16,20},{18,... | collective-permute-start | bytes 4325384 | tf_op jit(solution)/shard_map/ppermute | solution.py:1177
  423.4 58.9 %collective-permute-start.4 = (bf16[512,1408]{1,0:T(8,128)(2,1)}, bf16[512,1408]{1,0:T(8,128)(2,1)}, u32[]{:S(2)}, u32[]{:S(2)}) collective-permute-start(bf16[512,1408]{1,0:T(8,128)(2,1)} %slice_bitcast_fusion.1), channel_id=1, source_target_pairs={{0,1},{1,0},{2,3},{3,2},{4,5},{5,4},{6,7},{7,6},{8,9},{9,8},{10,11... | collective-permute-start | bytes 4325384 | tf_op jit(solution)/shard_map/ppermute | solution.py:1177
  425.6 56.7 %collective-permute-start.5 = (bf16[256,4864]{1,0:T(8,128)(2,1)}, bf16[256,4864]{1,0:T(8,128)(2,1)}, u32[]{:S(2)}, u32[]{:S(2)}) collective-permute-start(bf16[256,4864]{1,0:T(8,128)(2,1)} %pad_maximum_fusion), channel_id=1, source_target_pairs={{0,4},{2,6},{4,0},{6,2},{8,12},{10,14},{12,8},{14,10},{16,20},{18,... | collective-permute-start | bytes 7471112 | tf_op jit(solution)/shard_map/ppermute | solution.py:1177
  472.8 18.3 %collective-permute-start.7 = (bf16[512,3200]{1,0:T(8,128)(2,1)}, bf16[512,3200]{1,0:T(8,128)(2,1)}, u32[]{:S(2)}, u32[]{:S(2)}) collective-permute-start(bf16[512,3200]{1,0:T(8,128)(2,1)} %bitcast.239), channel_id=1, source_target_pairs={{0,2},{2,0},{4,6},{6,4},{8,10},{10,8},{12,14},{14,12},{16,18},{18,... | collective-permute-start | bytes 9830408 | tf_op jit(solution)/shard_map/ppermute | solution.py:1177
  485.1 65.6 %collective-permute-start.10 = (bf16[256,1408]{1,0:T(8,128)(2,1)}, bf16[256,1408]{1,0:T(8,128)(2,1)}, u32[]{:S(2)}, u32[]{:S(2)}) collective-permute-start(bf16[256,1408]{1,0:T(8,128)(2,1)} %bitcast.56), channel_id=1, source_target_pairs={{0,4},{2,6},{4,0},{6,2},{8,12},{10,14},{12,8},{14,10},{16,20},{18,... | collective-permute-start | bytes 2162696 | tf_op jit(solution)/shard_map/ppermute | solution.py:1177
  490.4 60.3 %collective-permute-start.11 = (bf16[256,3840]{1,0:T(8,128)(2,1)}, bf16[256,3840]{1,0:T(8,128)(2,1)}, u32[]{:S(2)}, u32[]{:S(2)}) collective-permute-start(bf16[256,3840]{1,0:T(8,128)(2,1)} %pad_maximum_fusion.1), channel_id=1, source_target_pairs={{0,1},{1,0},{2,3},{3,2},{4,5},{5,4},{6,7},{7,6},{8,9},{9,8},{10,11... | collective-permute-start | bytes 5898248 | tf_op jit(solution)/shard_map/ppermute | solution.py:1177
  501.6 62.9 %collective-permute-start.8 = (bf16[256,3200]{1,0:T(8,128)(2,1)}, bf16[256,3200]{1,0:T(8,128)(2,1)}, u32[]{:S(2)}, u32[]{:S(2)}) collective-permute-start(bf16[256,3200]{1,0:T(8,128)(2,1)} %bitcast.291), channel_id=1, source_target_pairs={{0,4},{2,6},{4,0},{6,2},{8,12},{10,14},{12,8},{14,10},{16,20},{18,... | collective-permute-start | bytes 4915208 | tf_op jit(solution)/shard_map/ppermute | solution.py:1177
  550.1 16.9 %collective-permute-start.12 = (bf16[512,3200]{1,0:T(8,128)(2,1)}, bf16[512,3200]{1,0:T(8,128)(2,1)S(1)}, u32[]{:S(2)}, u32[]{:S(2)}) collective-permute-start(bf16[512,3200]{1,0:T(8,128)(2,1)} %bitcast.241), channel_id=1, source_target_pairs={{0,2},{2,0},{4,6},{6,4},{8,10},{10,8},{12,14},{14,12},{16,18},{18,... | collective-permute-start | bytes 9830408 | tf_op jit(solution)/shard_map/ppermute | solution.py:1177
  558.0 47.9 %collective-permute-start.13 = (bf16[64,5248]{1,0:T(8,128)(2,1)}, bf16[64,5248]{1,0:T(8,128)(2,1)}, u32[]{:S(2)}, u32[]{:S(2)}) collective-permute-start(bf16[64,5248]{1,0:T(8,128)(2,1)} %pad_maximum_fusion.4), channel_id=1, source_target_pairs={{0,8},{2,10},{4,12},{6,14},{8,16},{10,18},{12,20},{14,22},{16,24},... | collective-permute-start | bytes 2015240 | tf_op jit(solution)/shard_map/ppermute | solution.py:1182
  561.3 57.6 %collective-permute-start.14 = (bf16[64,5248]{1,0:T(8,128)(2,1)}, bf16[64,5248]{1,0:T(8,128)(2,1)}, u32[]{:S(2)}, u32[]{:S(2)}) collective-permute-start(bf16[64,5248]{1,0:T(8,128)(2,1)} %pad_maximum_fusion.5), channel_id=1, source_target_pairs={{0,16},{2,18},{4,20},{6,22},{8,24},{10,26},{12,28},{14,30},{16,0},... | collective-permute-start | bytes 2015240 | tf_op jit(solution)/shard_map/ppermute | solution.py:1182
  564.5 57.2 %collective-permute-start.15 = (bf16[64,5248]{1,0:T(8,128)(2,1)}, bf16[64,5248]{1,0:T(8,128)(2,1)}, u32[]{:S(2)}, u32[]{:S(2)}) collective-permute-start(bf16[64,5248]{1,0:T(8,128)(2,1)} %pad_maximum_fusion.6), channel_id=1, source_target_pairs={{0,24},{2,26},{4,28},{6,30},{8,0},{10,2},{12,4},{14,6},{16,8},{18,... | collective-permute-start | bytes 2015240 | tf_op jit(solution)/shard_map/ppermute | solution.py:1182
  566.3 55.4 %collective-permute-start.9 = (bf16[256,3200]{1,0:T(8,128)(2,1)S(1)}, bf16[256,3200]{1,0:T(8,128)(2,1)}, u32[]{:S(2)}, u32[]{:S(2)}) collective-permute-start(bf16[256,3200]{1,0:T(8,128)(2,1)S(1)} %fusion.9), channel_id=1, source_target_pairs={{0,1},{1,0},{2,3},{3,2},{4,5},{5,4},{6,7},{7,6},{8,9},{9,8},{10,11... | collective-permute-start | bytes 4915208 | tf_op jit(solution)/shard_map/ppermute | solution.py:1177
  578.7 43.0 %collective-permute-start.16 = (bf16[256,3200]{1,0:T(8,128)(2,1)}, bf16[256,3200]{1,0:T(8,128)(2,1)}, u32[]{:S(2)}, u32[]{:S(2)}) collective-permute-start(bf16[256,3200]{1,0:T(8,128)(2,1)} %bitcast.292), channel_id=1, source_target_pairs={{0,4},{2,6},{4,0},{6,2},{8,12},{10,14},{12,8},{14,10},{16,20},{18,... | collective-permute-start | bytes 4915208 | tf_op jit(solution)/shard_map/ppermute | solution.py:1177
  623.2 4.5 collective-permute-start.17
  627.8 5.5 collective-permute-start.18
  633.3 1.3 collective-permute-start.19
  634.8 4.5 collective-permute-start.20
  639.3 6.7 collective-permute-start.21
  641.9 12.6 %collective-permute-start.22 = (bf16[64,3200]{1,0:T(8,128)(2,1)}, bf16[64,3200]{1,0:T(8,128)(2,1)S(1)}, u32[]{:S(2)}, u32[]{:S(2)}) collective-permute-start(bf16[64,3200]{1,0:T(8,128)(2,1)} %get-tuple-element.156), channel_id=1, source_target_pairs={{0,8},{2,10},{4,12},{6,14},{8,16},{10,18},{12,20},{14,22},{16,24},... | collective-permute-start | bytes 1228808 | tf_op jit(solution)/shard_map/ppermute | solution.py:1182
  641.9 34.9 %collective-permute-start.23 = (bf16[64,3200]{1,0:T(8,128)(2,1)}, bf16[64,3200]{1,0:T(8,128)(2,1)S(1)}, u32[]{:S(2)}, u32[]{:S(2)}) collective-permute-start(bf16[64,3200]{1,0:T(8,128)(2,1)} %get-tuple-element.157), channel_id=1, source_target_pairs={{0,16},{2,18},{4,20},{6,22},{8,24},{10,26},{12,28},{14,30},{16,0},... | collective-permute-start | bytes 1228808 | tf_op jit(solution)/shard_map/ppermute | solution.py:1182
  646.0 34.2 %collective-permute-start.24 = (bf16[64,3200]{1,0:T(8,128)(2,1)S(1)}, bf16[64,3200]{1,0:T(8,128)(2,1)S(1)}, u32[]{:S(2)}, u32[]{:S(2)}) collective-permute-start(bf16[64,3200]{1,0:T(8,128)(2,1)S(1)} %get-tuple-element.158), channel_id=1, source_target_pairs={{0,24},{2,26},{4,28},{6,30},{8,0},{10,2},{12,4},{14,6},{16,8},{18,... | collective-permute-start | bytes 1228808 | tf_op jit(solution)/shard_map/ppermute | solution.py:1182
  (43 other events, 570.0 us)
Sparse Core Ops, SparseCore 0:
  11.5 99.7 all-gather.2
  114.7 134.3 all-gather.4

commit v5 on v4

--- a/solution.py
+++ b/solution.py
@@ -1057,9 +1057,11 @@
     )(flags, *arrays)
 
 
-def product_body(own, side_first, flags_ref, left_ref, first_ref, second_ref, *refs):
+def product_body(own, side_first, paired, flags_ref, left_ref, first_ref, *refs):
     part = pl.program_id(0)
     shape = left_ref.shape
+    if paired:
+        second_ref, *refs = refs
     left = left_ref[...].reshape(shape[0] * shape[2], shape[3])
 
     def finish(right_ref):
@@ -1078,6 +1080,10 @@
         refs[-2][0] = jnp.where(here, low, high)
         refs[-1][0] = jnp.where(here, high, low)
 
+    if not paired:
+        finish(first_ref)
+        return
+
     @pl.when(part == 0)
     def _():
         finish(first_ref)
@@ -1116,10 +1122,17 @@
             (groups, 1, rows, tokens),
             lambda p, j, flags: (0, flags[0] if own else 1 - flags[0], 0, 0),
         ),
-        right_spec(rights[0], 0, 0),
-        right_spec(rights[-1], rights[-1].shape[0] - 1, count - 1),
     ]
-    arrays = [left, rights[0], rights[-1]]
+    paired = count == 2 and rights[0] is not rights[1]
+    arrays = [left, rights[0]]
+    if paired:
+        arrays.append(rights[1])
+        in_specs += [
+            right_spec(rights[0], 0, 0),
+            right_spec(rights[1], rights[1].shape[0] - 1, 1),
+        ]
+    else:
+        in_specs.append(pl.BlockSpec((1, tokens, block), lambda p, j, flags: (p, 0, j)))
     if own:
         in_specs.append(
             pl.BlockSpec((1, groups * rows, block), lambda p, j, flags: (slot(p, flags), 0, j))
@@ -1127,7 +1140,7 @@
         arrays.append(received)
     many = 2 if side_first else 1
     results = pl.pallas_call(
-        functools.partial(product_body, own, side_first),
+        functools.partial(product_body, own, side_first, paired),
         grid_spec=pltpu.PrefetchScalarGridSpec(
             num_scalar_prefetch=1,
             grid=(count, last + 1),

time: 700 us -> 689 us (0.984)
  Pallas kernels: 329 us -> 318 us
    pallas_call x12, Pallas kernels: 107 us -> 96.8 us  [product(): pl.pallas_call(functools.partial(product_body, own, side_first, paired),...]
    unnamed x103 -> x101, local copies, waits for them, and re-layouts: 14.5 us -> 13 us
  transfers between devices with their start and end apart: 27 -> 27, of which waited for: 11 -> 13; matrix products, arithmetic and copies ran while one was open for 13% -> 13% of each run, Pallas kernels for 42% -> 41%
where the time goes in v5:
time: 689 us; the launch traced here: 680 us
  Pallas kernels  318 us (46%)
  waiting for transfers between devices  162 us (24%)
  local copies, waits for them, and re-layouts  43.3 us (6%)
  matrix products  41.4 us (6%)
  blocking collectives  41 us (6%)
  other arithmetic  33.3 us (5%)
  starting transfers between devices  22.6 us (3%)
  between operations  18.4 us (3%)
    all_gather x2, waiting for transfers between devices, gather_all(): rows = lax.all_gather(local, (TP, DP), axis=0, tiled=True)  107 us
    pallas_call x12, Pallas kernels, product(): pl.pallas_call(functools.partial(product_body, own, side_first, paired),...  96.8 us
    pallas_call x3, Pallas kernels, dense_call(): pl.pallas_call(lambda flags_ref, *refs: body(*refs), grid_spec=pltpu.Pref...  95 us
    pallas_call x2, Pallas kernels, mixer_backward(): pl.pallas_call(functools.partial(backward_body, heads), grid=(parts, rows...  71.5 us
    pallas_call x2, Pallas kernels, mixer_forward(): pl.pallas_call(functools.partial(forward_body, heads), grid=(parts, rows...  54.8 us
    ppermute x6, waiting for transfers between devices, shift(): lax.ppermute(array, DP, [(i, (i + step) % size) for i in range(size)])  47.4 us
    psum x1, blocking collectives, on_device_whole(): count = lax.psum(jnp.sum(live), (DP, TP))  41 us
    dot_general x2, matrix products, on_device_whole(): jnp.dot(normed, pick(proj_all, part, 0), preferred_element_type=jnp.float32)  23.8 us
  transfers between devices with their start and end apart: 27, of which 13 were waited for; matrix products, arithmetic and copies ran while one was open for 13% of the time, Pallas kernels for 41%

profile of v5, /device:TPU:8, one launch (start us, length us, event | category | flops | bytes accessed | tf_op | source)
XLA Modules:
  0.0 680.0 jit_solution(10003658578647264952)
XLA Ops:
  13.7 41.0 %psum.7 = f32[]{:T(128)} all-reduce(f32[]{:T(128)} %convert_reduce_fusion), channel_id=1, replica_groups=mesh['dp'=16,'tensor'=2] {'dp','tensor'}, use_global_device_ids=true, to_apply=%region_3.4 | all-reduce | flops 1 | bytes 8 | tf_op jit(solution)/shard_map/psum | solution.py:1372
  57.9 53.4 %all-gather.3.cloned.1.call-done = bf16[2048,3200]{1,0:T(8,128)(2,1)} async-done(((bf16[64,3200]{1,0:T(8,128)(2,1)}), bf16[2048,3200]{1,0:T(8,128)(2,1)}) %all-gather.3.cloned.1.call-update) | async-done | bytes 13107216 | tf_op jit(solution)/shard_map/all_gather | solution.py:1176
  111.3 13.4 %convolution_bitcast_fusion.proj_ref = f32[1,1024,3200]{2,1,0:T(8,128)} fusion(bf16[2,1024,3200]{2,1,0:T(8,128)(2,1)} %bitcast.281, s32[]{:T(128)S(6)} %select_n.141, bf16[1024,1024]{1,0:T(8,128)(2,1)S(1)} %copy-done.16, f32[1024]{0:T(1024)S(1)} %copy-done.41, f32[1024]{0:T(1024)S(1)} %add_rsqrt_fusion.1), kind=kOutput, calls=%fused_computation | convolution fusion | flops 6715080704 | bytes 21766148 | tf_op jit(solution)/shard_map/dot_general | solution.py:1380
  124.7 10.3 %convolution_bitcast_fusion.1.proj_ref = f32[1,1024,3200]{2,1,0:T(8,128)} fusion(bf16[2,1024,3200]{2,1,0:T(8,128)(2,1)S(1)} %bitcast.283, s32[]{:T(128)S(6)} %select_n.139, bf16[1024,1024]{1,0:T(8,128)(2,1)S(1)} %copy-done.16, f32[1024]{0:T(1024)S(1)} %copy-done.41, f32[1024]{0:T(1024)S(1)} %add_rsqrt_fusion.1), kind=kOutput, calls=%fused_computation.1 | convolution fusion | flops 6715080704 | bytes 21766148 | tf_op jit(solution)/shard_map/dot_general | solution.py:1380
  135.1 27.0 %mixer_forward.3 = (bf16[1024,1024]{1,0:T(8,128)(2,1)S(1)}, f32[1,1024,2048]{2,1,0:T(8,128)}, f32[1,1024,1024]{2,1,0:T(8,128)}, bf16[1,8,4,128,256]{4,3,2,1,0:T(...) custom-call(f32[1,1024,3200]{2,1,0:T(8,128)} %convolution_bitcast_fusion.proj_ref, ...), custom_call_target="tpu_custom_call" | custom-call | flops 40000000000 | bytes 100000000 | tf_op jit(solution)/shard_map/mixer_forward/pallas_call | solution.py:816
  164.4 27.8 %mixer_forward.2 = (bf16[1024,1024]{1,0:T(8,128)(2,1)S(1)}, f32[1,1024,2048]{2,1,0:T(8,128)}, f32[1,1024,1024]{2,1,0:T(8,128)}, bf16[1,8,4,128,256]{4,3,2,1,0:T(...) custom-call(f32[1,1024,3200]{2,1,0:T(8,128)} %convolution_bitcast_fusion.1.proj_ref, ...), custom_call_target="tpu_custom_call" | custom-call | flops 40000000000 | bytes 100000000 | tf_op jit(solution)/shard_map/mixer_forward/pallas_call | solution.py:816
  195.9 53.3 %all-gather.5.cloned.1.call-done = bf16[2048,5248]{1,0:T(8,128)(2,1)} async-done(((bf16[64,5248]{1,0:T(8,128)(2,1)}), bf16[2048,5248]{1,0:T(8,128)(2,1)}) %all-gather.5.cloned.1.call-update) | async-done | bytes 21495824 | tf_op jit(solution)/shard_map/all_gather | solution.py:1176
  262.9 33.0 %dense_forward.1 = (bf16[2,1024,1408]{2,1,0:T(8,128)(2,1)}, bf16[2,1024,1408]{2,1,0:T(8,128)(2,1)}, bf16[2,1024,1408]{2,1,0:T(8,128)(2,1)}, f32[1024,1024]{1,0:T...) custom-call(s32[4]{0:T(128)} %pad_add_fusion.flags_ref, ...), custom_call_target="tpu_custom_call" | custom-call | flops 40000000000 | bytes 100000000 | tf_op jit(solution)/shard_map/dense_forward/pallas_call | solution.py:1044
  295.8 7.5 %product.12 = bf16[2,512,1408]{2,1,0:T(8,128)(2,1)} custom-call(s32[4]{0:T(128)} %pad_add_fusion.flags_ref, bf16[8,2,64,1024]{3,2,1,0:T(8,128)(2,1)} %bitcast.290, bf16[2,1024,1408]{2,1,0:T(8,128)(2,1)} %get-tuple-element.104.first_ref), custom_call_target="tpu_custom_call" | custom-call | flops 2952790016 | bytes 10000000 | tf_op jit(solution)/shard_map/product/pallas_call | solution.py:1142
  303.6 3.0 copy.120
  306.6 36.2 %dense_backward.1 = (bf16[2,1024,1408]{2,1,0:T(8,128)(2,1)}, bf16[2,1024,1408]{2,1,0:T(8,128)(2,1)}, f32[1024,1024]{1,0:T(8,128)}, bf16[1024,1024]{1,0:T(8,128)(...) custom-call(s32[4]{0:T(128)} %pad_add_fusion.flags_ref, bf16[1024,1024]{1,0:T(8,128)(2,1)} %get-tuple-element.105.refs_0_, ...), custom_call_target="tpu_custom_call" | custom-call | flops 40000000000 | bytes 100000000 | tf_op jit(solution)/shard_map/dense_backward/pallas_call | solution.py:1044
  342.8 7.5 %product.16 = bf16[2,512,1408]{2,1,0:T(8,128)(2,1)} custom-call(s32[4]{0:T(128)} %pad_add_fusion.flags_ref, bf16[8,2,64,1024]{3,2,1,0:T(8,128)(2,1)} %bitcast.224, bf16[2,1024,1408]{2,1,0:T(8,128)(2,1)} %get-tuple-element.113.first_ref), custom_call_target="tpu_custom_call" | custom-call | flops 2952790016 | bytes 10000000 | tf_op jit(solution)/shard_map/product/pallas_call | solution.py:1142
  350.6 6.8 %product.13 = bf16[2,512,1024]{2,1,0:T(8,128)(2,1)} custom-call(s32[4]{0:T(128)} %pad_add_fusion.flags_ref, bf16[8,2,64,1024]{3,2,1,0:T(8,128)(2,1)} %bitcast.228, bf16[1024,1024]{1,0:T(8,128)(2,1)} %copy-done.1, bf16[1024,1024]{1,0:T(8,128)(2,1)} %copy-done), custom_call_target="tpu_custom_call" | custom-call | flops 2147483648 | bytes 10000000 | tf_op jit(solution)/shard_map/product/pallas_call | solution.py:1142
  357.7 7.5 %product.14 = bf16[2,512,1408]{2,1,0:T(8,128)(2,1)} custom-call(s32[4]{0:T(128)} %pad_add_fusion.flags_ref, bf16[8,2,64,1024]{3,2,1,0:T(8,128)(2,1)} %bitcast.225, bf16[2,1024,1408]{2,1,0:T(8,128)(2,1)} %get-tuple-element.110.first_ref), custom_call_target="tpu_custom_call" | custom-call | flops 2952790016 | bytes 10000000 | tf_op jit(solution)/shard_map/product/pallas_call | solution.py:1142
  365.2 8.0 %product.15 = (bf16[2,256,1408]{2,1,0:T(8,128)(2,1)}, bf16[2,256,1408]{2,1,0:T(8,128)(2,1)}) custom-call(s32[4]{0:T(128)} %pad_add_fusion.flags_ref, bf16[8,2,64,1024]{3,2,1,0:T(8,128)(2,1)} %bitcast.291, bf16[2,1024,1408]{2,1,0:T(8,128)(2,1)} %get-tuple-element.104.first_ref, bf16[2,512,1408]{2,1,0:T(8,128)(2,1)} %bitcast.41.refs_0_), custom_call_target="tpu_custom_call" | custom-call | flops 2952790016 | bytes 10000000 | tf_op jit(solution)/shard_map/product/pallas_call | solution.py:1142
  379.9 7.8 %product.19 = (bf16[2,256,1024]{2,1,0:T(8,128)(2,1)}, bf16[2,256,1024]{2,1,0:T(8,128)(2,1)}) custom-call(s32[4]{0:T(128)} %pad_add_fusion.flags_ref, bf16[8,2,64,1024]{3,2,1,0:T(8,128)(2,1)} %bitcast.229, bf16[1024,1024]{1,0:T(8,128)(2,1)} %copy-done.1, bf16[1024,1024]{1,0:T(8,128)(2,1)} %copy-done, bf16[2,512,1024]{2,1,0:T(8,128)(2,1)} %bitcast.51.refs_1_), custom_call_target="tpu_custom_call" | custom-call | flops 2147483648 | bytes 10000000 | tf_op jit(solution)/shard_map/product/pallas_call | solution.py:1142
  390.8 6.0 fusion.15.grad_ref
  396.8 8.0 %product.17 = bf16[2,512,1408]{2,1,0:T(8,128)(2,1)} custom-call(s32[4]{0:T(128)} %pad_add_fusion.flags_ref, bf16[8,2,64,1024]{3,2,1,0:T(8,128)(2,1)} %bitcast.226, bf16[2,1024,1408]{2,1,0:T(8,128)(2,1)} %get-tuple-element.110.first_ref, bf16[2,512,1408]{2,1,0:T(8,128)(2,1)} %bitcast.46.refs_0_), custom_call_target="tpu_custom_call" | custom-call | flops 2952790016 | bytes 10000000 | tf_op jit(solution)/shard_map/product/pallas_call | solution.py:1142
  407.4 8.1 %product.18 = (bf16[2,256,1408]{2,1,0:T(8,128)(2,1)}, bf16[2,256,1408]{2,1,0:T(8,128)(2,1)}) custom-call(s32[4]{0:T(128)} %pad_add_fusion.flags_ref, bf16[8,2,64,1024]{3,2,1,0:T(8,128)(2,1)} %bitcast.227, bf16[2,1024,1408]{2,1,0:T(8,128)(2,1)} %get-tuple-element.113.first_ref, bf16[2,512,1408]{2,1,0:T(8,128)(2,1)} %bitcast.48.refs_0_), custom_call_target="tpu_custom_call" | custom-call | flops 2952790016 | bytes 10000000 | tf_op jit(solution)/shard_map/product/pallas_call | solution.py:1142
  420.7 35.8 %mixer_backward.2 = (bf16[1,1024,3200]{2,1,0:T(8,128)(2,1)}, f32[1,8,2048]{2,1,0:T(8,128)S(1)}, f32[1,8,128]{2,1,0:T(8,128)S(1)}, f32[1,8,256]{2,1,0:T(8,128)S(1)}) custom-call(f32[1,1024,3200]{2,1,0:T(8,128)} %convolution_bitcast_fusion.1.proj_ref, f32[1024,128]{1,0:T(8,128)S(1)} %pad.54.info_ref, f32[1,8,2048]{2,1,0:T(8,128)S(1)} %get-tuple-element.293.conv_ref, ...), custom_call_target="tpu_custom_call" | custom-call | flops 40000000000 | bytes 100000000 | tf_op jit(solution)/shard_map/mixer_backward/pallas_call | solution.py:849
  456.5 8.7 %product.20 = bf16[1,512,3200]{2,1,0:T(8,128)(2,1)} custom-call(s32[4]{0:T(128)} %pad_add_fusion.flags_ref, bf16[8,2,64,1024]{3,2,1,0:T(8,128)(2,1)} %bitcast.239, bf16[1,1024,3200]{2,1,0:T(8,128)(2,1)} %get-tuple-element.148.first_ref.refs_0_), custom_call_target="tpu_custom_call" | custom-call | flops 3355443200 | bytes 10000000 | tf_op jit(solution)/shard_map/product/pallas_call | solution.py:1142
  466.6 6.7 fusion.11.grad_ref
  485.3 9.4 %product.21 = (bf16[1,256,3200]{2,1,0:T(8,128)(2,1)}, bf16[1,256,3200]{2,1,0:T(8,128)(2,1)}) custom-call(s32[4]{0:T(128)} %pad_add_fusion.flags_ref, bf16[8,2,64,1024]{3,2,1,0:T(8,128)(2,1)} %bitcast.240, bf16[1,1024,3200]{2,1,0:T(8,128)(2,1)} %get-tuple-element.148.first_ref.refs_0_, bf16[1,512,3200]{2,1,0:T(8,128)(2,1)} %bitcast.63.refs_0_), custom_call_target="tpu_custom_call" | custom-call | flops 3355443200 | bytes 10000000 | tf_op jit(solution)/shard_map/product/pallas_call | solution.py:1142
  496.0 35.7 %mixer_backward.3 = (bf16[1,1024,3200]{2,1,0:T(8,128)(2,1)}, f32[1,8,2048]{2,1,0:T(8,128)S(1)}, f32[1,8,128]{2,1,0:T(8,128)S(1)}, f32[1,8,256]{2,1,0:T(8,128)S(1)}) custom-call(f32[1,1024,3200]{2,1,0:T(8,128)} %convolution_bitcast_fusion.proj_ref, f32[1024,128]{1,0:T(8,128)S(1)} %pad.54.info_ref, f32[1,8,2048]{2,1,0:T(8,128)S(1)} %get-tuple-element.294.conv_ref, ...), custom_call_target="tpu_custom_call" | custom-call | flops 40000000000 | bytes 100000000 | tf_op jit(solution)/shard_map/mixer_backward/pallas_call | solution.py:849
  532.1 8.6 %product.22 = bf16[1,512,3200]{2,1,0:T(8,128)(2,1)} custom-call(s32[4]{0:T(128)} %pad_add_fusion.flags_ref, bf16[8,2,64,1024]{3,2,1,0:T(8,128)(2,1)} %bitcast.241, bf16[1,1024,3200]{2,1,0:T(8,128)(2,1)} %get-tuple-element.149.first_ref.refs_1_), custom_call_target="tpu_custom_call" | custom-call | flops 3355443200 | bytes 10000000 | tf_op jit(solution)/shard_map/product/pallas_call | solution.py:1142
  554.3 8.8 %product.23 = (bf16[1,256,3200]{2,1,0:T(8,128)(2,1)}, bf16[1,256,3200]{2,1,0:T(8,128)(2,1)}) custom-call(s32[4]{0:T(128)} %pad_add_fusion.flags_ref, bf16[8,2,64,1024]{3,2,1,0:T(8,128)(2,1)} %bitcast.242, bf16[1,1024,3200]{2,1,0:T(8,128)(2,1)} %get-tuple-element.149.first_ref.refs_1_, bf16[1,512,3200]{2,1,0:T(8,128)(2,1)} %bitcast.92.refs_0_), custom_call_target="tpu_custom_call" | custom-call | flops 3355443200 | bytes 10000000 | tf_op jit(solution)/shard_map/product/pallas_call | solution.py:1142
  564.7 25.8 %input_backward.1 = (f32[1024,1024]{1,0:T(8,128)}, f32[8,1024]{1,0:T(8,128)}) custom-call(s32[4]{0:T(128)} %pad_add_fusion.flags_ref, bf16[1,1024,3200]{2,1,0:T(8,128)(2,1)} %get-tuple-element.148.first_ref.refs_0_, bf16[1,1024,3200]{2,1,0:T(8,128)(2,1)} %get-tuple-element.149.first_ref.refs_1_, bf16[2,1024,3200]{2,1,0:T(8,128)(2,1)} %bitcast.282, ...), custom_call_target="tpu_custom_call" | custom-call | flops 40000000000 | bytes 100000000 | tf_op jit(solution)/shard_map/input_backward/pallas_call | solution.py:1044
  593.1 14.1 %collective-permute-done.14 = bf16[64,5248]{1,0:T(8,128)(2,1)S(1)} collective-permute-done((bf16[64,5248]{1,0:T(8,128)(2,1)S(1)}, bf16[64,5248]{1,0:T(8,128)(2,1)S(1)}, u32[]{:S(2)}, u32[]{:S(2)}) %collective-permute-start.14) | collective-permute-done | bytes 671776 | tf_op jit(solution)/shard_map/ppermute | solution.py:1195
  611.7 3.0 add_convert_fusion
  618.8 2.8 collective-permute-done.18
  640.0 19.0 %collective-permute-done.22 = bf16[64,3200]{1,0:T(8,128)(2,1)S(1)} collective-permute-done((bf16[64,3200]{1,0:T(8,128)(2,1)}, bf16[64,3200]{1,0:T(8,128)(2,1)S(1)}, u32[]{:S(2)}, u32[]{:S(2)}) %collective-permute-start.22) | collective-permute-done | bytes 409632 | tf_op jit(solution)/shard_map/ppermute | solution.py:1195
  658.9 6.9 %collective-permute-done.23 = bf16[64,3200]{1,0:T(8,128)(2,1)S(1)} collective-permute-done((bf16[64,3200]{1,0:T(8,128)(2,1)}, bf16[64,3200]{1,0:T(8,128)(2,1)S(1)}, u32[]{:S(2)}, u32[]{:S(2)}) %collective-permute-start.23) | collective-permute-done | bytes 409632 | tf_op jit(solution)/shard_map/ppermute | solution.py:1195
  (248 shorter events, 110.7 us)
Async XLA Ops:
  7.2 104.1 %all-gather.3.cloned.1.call-start = ((), (), s32[]{:S(2)}) async-start(), calls=%async_computation | async-start | bytes 13516800 | tf_op jit(solution)/shard_map/all_gather | solution.py:1176
  8.0 47.7 %copy-start.45 = (f32[8]{0:T(128)S(1)}, f32[8]{0:T(128)}, u32[]{:S(2)}) copy-start(f32[8]{0:T(128)} %param.37) | copy-start | bytes 100
  8.0 47.8 %copy-start.46 = (f32[8]{0:T(128)S(1)}, f32[8]{0:T(128)}, u32[]{:S(2)}) copy-start(f32[8]{0:T(128)} %param.36) | copy-start | bytes 100
  10.8 238.4 %all-gather.5.cloned.1.call-start = ((), (), s32[]{:S(2)}) async-start(), calls=%async_computation.1 | async-start | bytes 22167552 | tf_op jit(solution)/shard_map/all_gather | solution.py:1176
  55.6 55.7 %copy-start.41 = (f32[1024]{0:T(1024)S(1)}, f32[1024]{0:T(1024)}, u32[]{:S(2)}) copy-start(f32[1024]{0:T(1024)} %param.26) | copy-start | bytes 12292
  57.8 66.9 %copy-start.39 = (f32[1024]{0:T(1024)}, f32[1024]{0:T(1024)S(1)}, u32[]{:S(2)}) copy-start(f32[1024]{0:T(1024)S(1)} %add_rsqrt_fusion.1) | copy-start | bytes 12292
  164.4 87.4 %copy-start = (bf16[1024,1024]{1,0:T(8,128)(2,1)}, bf16[1024,1024]{1,0:T(8,128)(2,1)S(1)}, u32[]{:S(2)}) copy-start(bf16[1024,1024]{1,0:T(8,128)(2,1)S(1)} %get-tuple-element.95.refs_0_) | copy-start | bytes 6291460
  303.4 61.8 %collective-permute-start = (bf16[1024,1408]{1,0:T(8,128)(2,1)}, bf16[1024,1408]{1,0:T(8,128)(2,1)}, u32[]{:S(2)}, u32[]{:S(2)}) collective-permute-start(bf16[1024,1408]{1,0:T(8,128)(2,1)} %bitcast.287), channel_id=1, source_target_pairs={{0,2},{2,0},{4,6},{6,4},{8,10},{10,8},{12,14},{14,12},{16,18},{18,... | collective-permute-start | bytes 8650760 | tf_op jit(solution)/shard_map/ppermute | solution.py:1190
  350.4 46.4 %collective-permute-start.2 = (bf16[1024,1408]{1,0:T(8,128)(2,1)}, bf16[1024,1408]{1,0:T(8,128)(2,1)}, u32[]{:S(2)}, u32[]{:S(2)}) collective-permute-start(bf16[1024,1408]{1,0:T(8,128)(2,1)} %bitcast.286), channel_id=1, source_target_pairs={{0,2},{2,0},{4,6},{6,4},{8,10},{10,8},{12,14},{14,12},{16,18},{18,... | collective-permute-start | bytes 8650760 | tf_op jit(solution)/shard_map/ppermute | solution.py:1190
  357.4 22.5 %collective-permute-start.3 = (bf16[1024,1024]{1,0:T(8,128)(2,1)}, bf16[1024,1024]{1,0:T(8,128)(2,1)}, u32[]{:S(2)}, u32[]{:S(2)}) collective-permute-start(bf16[1024,1024]{1,0:T(8,128)(2,1)} %bitcast.243), channel_id=1, source_target_pairs={{0,2},{2,0},{4,6},{6,4},{8,10},{10,8},{12,14},{14,12},{16,18},{18,... | collective-permute-start | bytes 6291464 | tf_op jit(solution)/shard_map/ppermute | solution.py:1190
  375.9 20.9 %collective-permute-start.1 = (bf16[1024,1408]{1,0:T(8,128)(2,1)}, bf16[1024,1408]{1,0:T(8,128)(2,1)}, u32[]{:S(2)}, u32[]{:S(2)}) collective-permute-start(bf16[1024,1408]{1,0:T(8,128)(2,1)} %bitcast.44), channel_id=1, source_target_pairs={{0,2},{2,0},{4,6},{6,4},{8,10},{10,8},{12,14},{14,12},{16,18},{18,... | collective-permute-start | bytes 8650760 | tf_op jit(solution)/shard_map/ppermute | solution.py:1190
  389.3 83.9 %collective-permute-start.6 = (bf16[256,2816]{1,0:T(8,128)(2,1)S(1)}, bf16[256,2816]{1,0:T(8,128)(2,1)}, u32[]{:S(2)}, u32[]{:S(2)}) collective-permute-start(bf16[256,2816]{1,0:T(8,128)(2,1)S(1)} %copy-done.25), channel_id=1, source_target_pairs={{0,4},{2,6},{4,0},{6,2},{8,12},{10,14},{12,8},{14,10},{16,20},{18,... | collective-permute-start | bytes 4325384 | tf_op jit(solution)/shard_map/ppermute | solution.py:1190
  417.0 57.6 %collective-permute-start.4 = (bf16[512,1408]{1,0:T(8,128)(2,1)}, bf16[512,1408]{1,0:T(8,128)(2,1)}, u32[]{:S(2)}, u32[]{:S(2)}) collective-permute-start(bf16[512,1408]{1,0:T(8,128)(2,1)} %slice_bitcast_fusion.1), channel_id=1, source_target_pairs={{0,1},{1,0},{2,3},{3,2},{4,5},{5,4},{6,7},{7,6},{8,9},{9,8},{10,11... | collective-permute-start | bytes 4325384 | tf_op jit(solution)/shard_map/ppermute | solution.py:1190
  419.2 57.3 %collective-permute-start.5 = (bf16[256,4864]{1,0:T(8,128)(2,1)}, bf16[256,4864]{1,0:T(8,128)(2,1)}, u32[]{:S(2)}, u32[]{:S(2)}) collective-permute-start(bf16[256,4864]{1,0:T(8,128)(2,1)} %pad_maximum_fusion), channel_id=1, source_target_pairs={{0,4},{2,6},{4,0},{6,2},{8,12},{10,14},{12,8},{14,10},{16,20},{18,... | collective-permute-start | bytes 7471112 | tf_op jit(solution)/shard_map/ppermute | solution.py:1190
  465.2 20.1 %collective-permute-start.7 = (bf16[512,3200]{1,0:T(8,128)(2,1)}, bf16[512,3200]{1,0:T(8,128)(2,1)}, u32[]{:S(2)}, u32[]{:S(2)}) collective-permute-start(bf16[512,3200]{1,0:T(8,128)(2,1)} %bitcast.284), channel_id=1, source_target_pairs={{0,2},{2,0},{4,6},{6,4},{8,10},{10,8},{12,14},{14,12},{16,18},{18,... | collective-permute-start | bytes 9830408 | tf_op jit(solution)/shard_map/ppermute | solution.py:1190
  479.3 61.6 %collective-permute-start.10 = (bf16[256,1408]{1,0:T(8,128)(2,1)}, bf16[256,1408]{1,0:T(8,128)(2,1)}, u32[]{:S(2)}, u32[]{:S(2)}) collective-permute-start(bf16[256,1408]{1,0:T(8,128)(2,1)} %bitcast.56), channel_id=1, source_target_pairs={{0,4},{2,6},{4,0},{6,2},{8,12},{10,14},{12,8},{14,10},{16,20},{18,... | collective-permute-start | bytes 2162696 | tf_op jit(solution)/shard_map/ppermute | solution.py:1190
  484.8 56.1 %collective-permute-start.11 = (bf16[256,3840]{1,0:T(8,128)(2,1)}, bf16[256,3840]{1,0:T(8,128)(2,1)}, u32[]{:S(2)}, u32[]{:S(2)}) collective-permute-start(bf16[256,3840]{1,0:T(8,128)(2,1)} %pad_maximum_fusion.1), channel_id=1, source_target_pairs={{0,1},{1,0},{2,3},{3,2},{4,5},{5,4},{6,7},{7,6},{8,9},{9,8},{10,11... | collective-permute-start | bytes 5898248 | tf_op jit(solution)/shard_map/ppermute | solution.py:1190
  494.7 56.9 %collective-permute-start.8 = (bf16[256,3200]{1,0:T(8,128)(2,1)}, bf16[256,3200]{1,0:T(8,128)(2,1)}, u32[]{:S(2)}, u32[]{:S(2)}) collective-permute-start(bf16[256,3200]{1,0:T(8,128)(2,1)} %bitcast.288), channel_id=1, source_target_pairs={{0,4},{2,6},{4,0},{6,2},{8,12},{10,14},{12,8},{14,10},{16,20},{18,... | collective-permute-start | bytes 4915208 | tf_op jit(solution)/shard_map/ppermute | solution.py:1190
  540.7 13.6 %collective-permute-start.12 = (bf16[512,3200]{1,0:T(8,128)(2,1)}, bf16[512,3200]{1,0:T(8,128)(2,1)}, u32[]{:S(2)}, u32[]{:S(2)}) collective-permute-start(bf16[512,3200]{1,0:T(8,128)(2,1)} %bitcast.285), channel_id=1, source_target_pairs={{0,2},{2,0},{4,6},{6,4},{8,10},{10,8},{12,14},{14,12},{16,18},{18,... | collective-permute-start | bytes 9830408 | tf_op jit(solution)/shard_map/ppermute | solution.py:1190
  546.8 46.2 %collective-permute-start.13 = (bf16[64,5248]{1,0:T(8,128)(2,1)S(1)}, bf16[64,5248]{1,0:T(8,128)(2,1)S(1)}, u32[]{:S(2)}, u32[]{:S(2)}) collective-permute-start(bf16[64,5248]{1,0:T(8,128)(2,1)S(1)} %pad_maximum_fusion.4), channel_id=1, source_target_pairs={{0,8},{2,10},{4,12},{6,14},{8,16},{10,18},{12,20},{14,22},{16,24},... | collective-permute-start | bytes 2015240 | tf_op jit(solution)/shard_map/ppermute | solution.py:1195
  549.1 58.1 %collective-permute-start.14 = (bf16[64,5248]{1,0:T(8,128)(2,1)S(1)}, bf16[64,5248]{1,0:T(8,128)(2,1)S(1)}, u32[]{:S(2)}, u32[]{:S(2)}) collective-permute-start(bf16[64,5248]{1,0:T(8,128)(2,1)S(1)} %pad_maximum_fusion.5), channel_id=1, source_target_pairs={{0,16},{2,18},{4,20},{6,22},{8,24},{10,26},{12,28},{14,30},{16,0},... | collective-permute-start | bytes 2015240 | tf_op jit(solution)/shard_map/ppermute | solution.py:1195
  551.5 57.7 %collective-permute-start.15 = (bf16[64,5248]{1,0:T(8,128)(2,1)S(1)}, bf16[64,5248]{1,0:T(8,128)(2,1)S(1)}, u32[]{:S(2)}, u32[]{:S(2)}) collective-permute-start(bf16[64,5248]{1,0:T(8,128)(2,1)S(1)} %pad_maximum_fusion.6), channel_id=1, source_target_pairs={{0,24},{2,26},{4,28},{6,30},{8,0},{10,2},{12,4},{14,6},{16,8},{18,... | collective-permute-start | bytes 2015240 | tf_op jit(solution)/shard_map/ppermute | solution.py:1195
  553.4 55.8 %collective-permute-start.9 = (bf16[256,3200]{1,0:T(8,128)(2,1)S(1)}, bf16[256,3200]{1,0:T(8,128)(2,1)}, u32[]{:S(2)}, u32[]{:S(2)}) collective-permute-start(bf16[256,3200]{1,0:T(8,128)(2,1)S(1)} %fusion.9), channel_id=1, source_target_pairs={{0,1},{1,0},{2,3},{3,2},{4,5},{5,4},{6,7},{7,6},{8,9},{9,8},{10,11... | collective-permute-start | bytes 4915208 | tf_op jit(solution)/shard_map/ppermute | solution.py:1190
  563.2 46.1 %collective-permute-start.16 = (bf16[256,3200]{1,0:T(8,128)(2,1)}, bf16[256,3200]{1,0:T(8,128)(2,1)}, u32[]{:S(2)}, u32[]{:S(2)}) collective-permute-start(bf16[256,3200]{1,0:T(8,128)(2,1)} %bitcast.289), channel_id=1, source_target_pairs={{0,4},{2,6},{4,0},{6,2},{8,12},{10,14},{12,8},{14,10},{16,20},{18,... | collective-permute-start | bytes 4915208 | tf_op jit(solution)/shard_map/ppermute | solution.py:1190
  611.6 4.5 collective-permute-start.17
  616.2 5.4 collective-permute-start.18
  621.7 1.3 collective-permute-start.19
  623.1 4.5 collective-permute-start.20
  627.7 7.0 %collective-permute-start.21 = (f32[1,19456]{1,0:T(1,128)S(1)}, f32[1,19456]{1,0:T(1,128)S(1)}, u32[]{:S(2)}, u32[]{:S(2)}) collective-permute-start(f32[1,19456]{1,0:T(1,128)S(1)} %add.309), channel_id=1, source_target_pairs={{0,1},{1,0},{2,3},{3,2},{4,5},{5,4},{6,7},{7,6},{8,9},{9,8},{10,11... | collective-permute-start | bytes 233480 | tf_op jit(solution)/shard_map/ppermute | solution.py:1190
  630.4 28.6 %collective-permute-start.22 = (bf16[64,3200]{1,0:T(8,128)(2,1)}, bf16[64,3200]{1,0:T(8,128)(2,1)S(1)}, u32[]{:S(2)}, u32[]{:S(2)}) collective-permute-start(bf16[64,3200]{1,0:T(8,128)(2,1)} %get-tuple-element.156), channel_id=1, source_target_pairs={{0,8},{2,10},{4,12},{6,14},{8,16},{10,18},{12,20},{14,22},{16,24},... | collective-permute-start | bytes 1228808 | tf_op jit(solution)/shard_map/ppermute | solution.py:1195
  631.1 34.7 %collective-permute-start.23 = (bf16[64,3200]{1,0:T(8,128)(2,1)}, bf16[64,3200]{1,0:T(8,128)(2,1)S(1)}, u32[]{:S(2)}, u32[]{:S(2)}) collective-permute-start(bf16[64,3200]{1,0:T(8,128)(2,1)} %get-tuple-element.157), channel_id=1, source_target_pairs={{0,16},{2,18},{4,20},{6,22},{8,24},{10,26},{12,28},{14,30},{16,0},... | collective-permute-start | bytes 1228808 | tf_op jit(solution)/shard_map/ppermute | solution.py:1195
  633.4 35.1 %collective-permute-start.24 = (bf16[64,3200]{1,0:T(8,128)(2,1)}, bf16[64,3200]{1,0:T(8,128)(2,1)S(1)}, u32[]{:S(2)}, u32[]{:S(2)}) collective-permute-start(bf16[64,3200]{1,0:T(8,128)(2,1)} %get-tuple-element.158), channel_id=1, source_target_pairs={{0,24},{2,26},{4,28},{6,30},{8,0},{10,2},{12,4},{14,6},{16,8},{18,... | collective-permute-start | bytes 1228808 | tf_op jit(solution)/shard_map/ppermute | solution.py:1195
  (42 other events, 411.9 us)
Sparse Core Ops, SparseCore 0:
  11.5 99.7 all-gather.2
  114.7 134.3 all-gather.4
